TPU v7x, 32 devices: a whole 2x2x4 slice. The times are simulated.
32 devices in a mesh: job: 2 (over y), tile: 4 (over z), src: 4 (over x, core).
Axes of the slice: x: 2, y: 2, z: 4, core: 2. Of those that a mesh axis runs over, the one named last changes fastest.
Arguments:
- forward_field: float32 [8, 2, 16, 256, 128], P(('job', 'src'), None, 'tile'), parts along dimension 0, may hold values from -6 to 6
- adjoint_guess: float32 [8, 2, 16, 256, 128], P(('job', 'src'), None, 'tile'), parts along dimension 0, may hold values from -6 to 6
- conductivity: float32 [32, 256, 128], P(('job', 'tile')), parts along dimension 0, may hold values from 0.3 to 3
- freq_kappa: float32 [8], P('job'), parts along dimension 0, may hold values from 0.5 to 4
- pair_freq: int32 [8], P(('job', 'src')), parts along dimension 0, may hold values from 0 to 3
- recv_data: float32 [8, 2, 256], P(('job', 'src')), parts along dimension 0, may hold values from -6 to 6
- recv_weights: float32 [512, 64], P('job'), parts along dimension 0, may hold values from 0.05 to 1
- recv_x: int32 [512], P('job'), parts along dimension 0, may hold values from 0 to 12
- recv_y: int32 [512], P('job'), parts along dimension 0, may hold values from 0 to 252
- recv_z: int32 [512], P('job'), parts along dimension 0, may hold values from 0 to 124
Outputs:
- adjoint: float32 [8, 2, 16, 256, 128], P(('job', 'src'), None, 'tile'), parts along dimension 0
- gradient: float32 [32, 256, 128], P(('job', 'tile'), 'src'), parts along dimension 0
There are 2 independent parts, one for each index of `job`. A program takes and returns all parts, laid end to end along the dimension named above; each array names one. Nothing has to cross between parts.
Inputs may be any that keep to these rules, and one draw needn't show every extreme that they name: `recv_x`: each receiver's block of 4 x 4 x 4 cells lies inside the grid along the first dimension. `recv_y`: each receiver's block lies inside the grid along the second dimension. `recv_z`: each receiver's block lies inside the grid along the third dimension. `pair_freq`: an index into freq_kappa.
All inputs are finite; a program needn't handle non-finite values.
Results may differ from a plain program's by a relative error of at most 0.00011.
Values sent between devices are 32-bit elements; how exact they have to be, the bound alone decides.
No kernel may reach another device: no remote copies, remote signals or barrier semaphores. Data moves between devices by JAX's collectives and lax.ppermute only.
A program may use at most 64 MiB of HBM per device.

v0:
```python
import jax
import jax.numpy as jnp
from jax import lax
from jax.sharding import PartitionSpec as P


def with_halo(cells, sides, width):
    for axis, dim in sides:
        count = lax.axis_size(axis)
        ends = count - 1
        head = lax.slice_in_dim(cells, 0, width, axis=dim)
        tail = lax.slice_in_dim(cells, cells.shape[dim] - width, cells.shape[dim], axis=dim)
        cells = jnp.concatenate(
            [
                lax.ppermute(tail, axis, [(i, (i + 1) % count) for i in range(ends)]),
                cells,
                lax.ppermute(head, axis, [((i + 1) % count, i) for i in range(ends)]),
            ],
            axis=dim,
        )
    return cells


def neighbour_update(extended, source, coupling, denominator, update_mask):
    inner = extended[:, :, 1:-1]
    padded = jnp.pad(inner, ((0, 0), (0, 0), (0, 0), (1, 1), (1, 1)))
    beside_all = extended[:, :, 2:] + extended[:, :, :-2]
    beside_all = beside_all + padded[:, :, :, 2:, 1:-1] + padded[:, :, :, :-2, 1:-1]
    beside_all = beside_all + padded[:, :, :, 1:-1, 2:] + padded[:, :, :, 1:-1, :-2]
    sums = source + beside_all
    real_part = (6.0 * sums[:, 0] + coupling * sums[:, 1]) / denominator
    imag_part = (6.0 * sums[:, 1] - coupling * sums[:, 0]) / denominator
    return jnp.where(update_mask[None, None], jnp.stack([real_part, imag_part], axis=1), inner)


def local_source(recv_data, recv_weights, recv_x, recv_y, recv_z, start_x, layers, size_y, size_z):
    recv_count = recv_weights.shape[0]
    pair_count = recv_data.shape[0]
    steps_four = jnp.arange(4, dtype=jnp.int32)
    rows_y = jnp.arange(size_y, dtype=jnp.int32)
    row_match = (
        (rows_y[:, None, None] == recv_y[None, :, None] + steps_four[None, None, :])
        .astype(jnp.float32)
        .reshape(size_y, recv_count * 4)
    )
    cols_z = jnp.arange(size_z, dtype=jnp.int32)
    col_match = (cols_z[None, None, :] == recv_z[:, None, None] + steps_four[None, :, None]).astype(
        jnp.float32
    )
    weight_block = recv_weights.reshape(recv_count, 4, 4, 4)

    def one_layer(layer):
        offset_x = start_x + layer - recv_x
        pick = (offset_x[:, None] == steps_four[None, :]).astype(jnp.float32)
        plane = jnp.sum(pick[:, :, None, None] * weight_block, axis=1)
        spread = jnp.einsum("rbk,rkz->rbz", plane, col_match, precision=lax.Precision.HIGHEST)
        scaled = (recv_data[:, :, :, None, None] * spread[None, None]).reshape(
            pair_count, 2, recv_count * 4, size_z
        )
        return jnp.einsum("ym,pcmz->pcyz", row_match, scaled, precision=lax.Precision.HIGHEST)

    stacked = lax.map(one_layer, jnp.arange(layers, dtype=jnp.int32))
    return jnp.moveaxis(stacked, 0, 2)


def colour_table(start_x, layers, size_y, size_z):
    along_x = start_x + jnp.arange(layers, dtype=jnp.int32)
    return (
        along_x[:, None, None]
        + jnp.arange(size_y, dtype=jnp.int32)[None, :, None]
        + jnp.arange(size_z, dtype=jnp.int32)[None, None, :]
    ) % 2


def body(
    forward_field,
    adjoint_guess,
    conductivity,
    freq_kappa,
    pair_freq,
    recv_data,
    recv_weights,
    recv_x,
    recv_y,
    recv_z,
):
    pair_count, parts, layers_dev, size_y, size_z = adjoint_guess.shape
    first_x = lax.axis_index("tile") * layers_dev
    freq_count = freq_kappa.shape[0]
    kappa = jnp.sum(
        jnp.where(
            pair_freq[:, None] == jnp.arange(freq_count, dtype=jnp.int32)[None, :],
            freq_kappa[None, :],
            0.0,
        ),
        axis=1,
    )
    coupling = kappa[:, None, None, None] * conductivity[None]
    denominator = 36.0 + coupling * coupling
    source = local_source(
        recv_data, recv_weights, recv_x, recv_y, recv_z, first_x, layers_dev, size_y, size_z
    )
    colours = colour_table(first_x, layers_dev, size_y, size_z)
    field = adjoint_guess
    for colour in (0, 1, 0, 1):
        extended = with_halo(field, (("tile", 2),), 1)
        field = neighbour_update(extended, source, coupling, denominator, colours == colour)
    products = forward_field[:, 0] * field[:, 1] + forward_field[:, 1] * field[:, 0]
    partial_terms = -conductivity * jnp.sum(kappa[:, None, None, None] * products, axis=0)
    gradient = lax.psum_scatter(partial_terms, "src", scatter_dimension=1, tiled=True)
    return (field, gradient)


def solution(mesh):
    placed = (
        P(("job", "src"), None, "tile", None, None),
        P(("job", "src"), None, "tile", None, None),
        P(("job", "tile"), None, None),
        P("job"),
        P(("job", "src")),
        P(("job", "src"), None, None),
        P("job", None),
        P("job"),
        P("job"),
        P("job"),
    )
    return jax.shard_map(
        body,
        mesh=mesh,
        in_specs=placed,
        out_specs=(P(("job", "src"), None, "tile", None, None), P(("job", "tile"), "src", None)),
        check_vma=False,
    )
```

profile of v0, /device:TPU:0, one launch (start us, length us, event | category | flops | bytes accessed | tf_op | source)
XLA Modules:
  0.0 113.9 jit_solution(8431818215590295439)
XLA Ops:
  7.3 1.9 %fusion.49 = (f32[1,2,1,256,128]{4,3,2,1,0:T(8,128)}, f32[1,2,1,256,128]{4,3,2,1,0:T(8,128)}) fusion(f32[1,2,4,256,128]{4,3,2,1,0:T(8,128)} %param.13), kind=kLoop, calls=%fused_computation.110 | loop fusion | bytes 1048576 | tf_op jit(solution)/shard_map/slice | solution.py:11
  9.1 1.3 %collective-permute-start = (f32[1,2,1,256,128]{4,3,2,1,0:T(8,128)}, f32[1,2,1,256,128]{4,3,2,1,0:T(8,128)}, u32[]{:S(2)}, u32[]{:S(2)}) collective-permute-start(f32[1,2,1,256,128]{4,3,2,1,0:T(8,128)} %get-tuple-element.154), channel_id=1, source_target_pairs={{4,0},{8,4},{12,8},{5,1},{9,5},{13,9},{6,2},{10,6},{14,10},{7,3},{... | collective-permute-start | bytes 786440 | tf_op jit(solution)/shard_map/ppermute | solution.py:17
  10.4 6.3 %collective-permute-start.1 = (f32[1,2,1,256,128]{4,3,2,1,0:T(8,128)}, f32[1,2,1,256,128]{4,3,2,1,0:T(8,128)}, u32[]{:S(2)}, u32[]{:S(2)}) collective-permute-start(f32[1,2,1,256,128]{4,3,2,1,0:T(8,128)} %get-tuple-element.155), channel_id=1, source_target_pairs={{0,4},{4,8},{8,12},{1,5},{5,9},{9,13},{2,6},{6,10},{10,14},{3,7},{... | collective-permute-start | bytes 786440 | tf_op jit(solution)/shard_map/ppermute | solution.py:15
  18.0 21.1 %while.13 = (s32[]{:T(128)}, f32[4,1,2,256,128]{4,3,0,2,1:T(8,128)S(1)}, f32[1,2,256]{2,1,0:T(2,128)S(1)}, s32[4]{0:T(128)S(1)}, s32[]{:T(128)}, /*index=5*/s32[...) while((s32[]{:T(128)}, ...), condition=%wide.region_2.3_spmd.clone.clone, body=%wide.region_0.0_spmd.clone.clone.sunk | while | flops 812677376 | bytes 3593373 | solution.py:62
  19.9 1.9 %fusion.60 = f32[256,4,128]{2,1,0:T(4,128)S(1)} fusion(f32[256,4,4]{2,1,0:T(4,128)S(1)} %copy.29, s32[256,4]{1,0:T(8,128)S(1)} %get-tuple-element.240), kind=kOutput, calls=%fused_computation.8.clone.1 | convolution fusion | flops 6553600 | bytes 544768 | tf_op jit(solution)/shard_map/while/body/eval_jaxpr/rbk,rkz->rbz/dot_general | solution.py:56
  22.0 1.1 convolution_bitcast_fusion.2
  25.2 1.9 %fusion.60 = f32[256,4,128]{2,1,0:T(4,128)S(1)} fusion(f32[256,4,4]{2,1,0:T(4,128)S(1)} %copy.29, s32[256,4]{1,0:T(8,128)S(1)} %get-tuple-element.240), kind=kOutput, calls=%fused_computation.8.clone.1 | convolution fusion | flops 6553600 | bytes 544768 | tf_op jit(solution)/shard_map/while/body/eval_jaxpr/rbk,rkz->rbz/dot_general | solution.py:56
  30.5 1.9 %fusion.60 = f32[256,4,128]{2,1,0:T(4,128)S(1)} fusion(f32[256,4,4]{2,1,0:T(4,128)S(1)} %copy.29, s32[256,4]{1,0:T(8,128)S(1)} %get-tuple-element.240), kind=kOutput, calls=%fused_computation.8.clone.1 | convolution fusion | flops 6553600 | bytes 544768 | tf_op jit(solution)/shard_map/while/body/eval_jaxpr/rbk,rkz->rbz/dot_general | solution.py:56
  35.8 1.9 %fusion.60 = f32[256,4,128]{2,1,0:T(4,128)S(1)} fusion(f32[256,4,4]{2,1,0:T(4,128)S(1)} %copy.29, s32[256,4]{1,0:T(8,128)S(1)} %get-tuple-element.240), kind=kOutput, calls=%fused_computation.8.clone.1 | convolution fusion | flops 6553600 | bytes 544768 | tf_op jit(solution)/shard_map/while/body/eval_jaxpr/rbk,rkz->rbz/dot_general | solution.py:56
  40.2 1.7 %fusion.17 = f32[1,2,4,256,128]{4,3,2,1,0:T(8,128)S(1)} fusion(f32[1,2,4,256,128]{4,3,2,1,0:T(8,128)S(1)} %copy-done, f32[1,2,1,256,128]{4,3,2,1,0:T(8,128)} %collective-permute-done.1, f32[1,2,1,256,128]{4,3,2,1,0:T(8,128)} %collective-permute-done, f32[4,1,2,256,128]{4,3,0,2,1:T(8,128)S(1)} %get-tuple-element.76), kind=kLoop, calls=%fused_computation.38 | loop fusion | flops 2097152 | bytes 3670016 | tf_op jit(solution)/shard_map/add | solution.py:30
  43.0 1.3 %collective-permute-start.2 = (f32[1,2,1,256,128]{4,3,2,1,0:T(8,128)S(1)}, f32[1,2,1,256,128]{4,3,2,1,0:T(8,128)S(1)}, u32[]{:S(2)}, u32[]{:S(2)}) collective-permute-start(f32[1,2,1,256,128]{4,3,2,1,0:T(8,128)S(1)} %get-tuple-element.152), channel_id=1, source_target_pairs={{4,0},{8,4},{12,8},{5,1},{9,5},{13,9},{6,2},{10,6},{14,10},{7,3},{... | collective-permute-start | bytes 786440 | tf_op jit(solution)/shard_map/ppermute | solution.py:17
  44.3 4.6 %collective-permute-start.3 = (f32[1,2,1,256,128]{4,3,2,1,0:T(8,128)S(1)}, f32[1,2,1,256,128]{4,3,2,1,0:T(8,128)S(1)}, u32[]{:S(2)}, u32[]{:S(2)}) collective-permute-start(f32[1,2,1,256,128]{4,3,2,1,0:T(8,128)S(1)} %get-tuple-element.153), channel_id=1, source_target_pairs={{0,4},{4,8},{8,12},{1,5},{5,9},{9,13},{2,6},{6,10},{10,14},{3,7},{... | collective-permute-start | bytes 786440 | tf_op jit(solution)/shard_map/ppermute | solution.py:15
  48.8 3.8 %collective-permute-done.2 = f32[1,2,1,256,128]{4,3,2,1,0:T(8,128)S(1)} collective-permute-done((f32[1,2,1,256,128]{4,3,2,1,0:T(8,128)S(1)}, f32[1,2,1,256,128]{4,3,2,1,0:T(8,128)S(1)}, u32[]{:S(2)}, u32[]{:S(2)}) %collective-permute-start.2) | collective-permute-done | bytes 262176 | tf_op jit(solution)/shard_map/ppermute | solution.py:17
  52.6 1.2 %collective-permute-done.3 = f32[1,2,1,256,128]{4,3,2,1,0:T(8,128)S(1)} collective-permute-done((f32[1,2,1,256,128]{4,3,2,1,0:T(8,128)S(1)}, f32[1,2,1,256,128]{4,3,2,1,0:T(8,128)S(1)}, u32[]{:S(2)}, u32[]{:S(2)}) %collective-permute-start.3) | collective-permute-done | bytes 262176 | tf_op jit(solution)/shard_map/ppermute | solution.py:15
  55.5 1.3 %collective-permute-start.4 = (f32[1,2,1,256,128]{4,3,2,1,0:T(8,128)S(1)}, f32[1,2,1,256,128]{4,3,2,1,0:T(8,128)S(1)}, u32[]{:S(2)}, u32[]{:S(2)}) collective-permute-start(f32[1,2,1,256,128]{4,3,2,1,0:T(8,128)S(1)} %get-tuple-element.150), channel_id=1, source_target_pairs={{4,0},{8,4},{12,8},{5,1},{9,5},{13,9},{6,2},{10,6},{14,10},{7,3},{... | collective-permute-start | bytes 786440 | tf_op jit(solution)/shard_map/ppermute | solution.py:17
  56.8 5.0 %collective-permute-start.5 = (f32[1,2,1,256,128]{4,3,2,1,0:T(8,128)S(1)}, f32[1,2,1,256,128]{4,3,2,1,0:T(8,128)S(1)}, u32[]{:S(2)}, u32[]{:S(2)}) collective-permute-start(f32[1,2,1,256,128]{4,3,2,1,0:T(8,128)S(1)} %get-tuple-element.151), channel_id=1, source_target_pairs={{0,4},{4,8},{8,12},{1,5},{5,9},{9,13},{2,6},{6,10},{10,14},{3,7},{... | collective-permute-start | bytes 786440 | tf_op jit(solution)/shard_map/ppermute | solution.py:15
  61.8 2.9 %collective-permute-done.4 = f32[1,2,1,256,128]{4,3,2,1,0:T(8,128)S(1)} collective-permute-done((f32[1,2,1,256,128]{4,3,2,1,0:T(8,128)S(1)}, f32[1,2,1,256,128]{4,3,2,1,0:T(8,128)S(1)}, u32[]{:S(2)}, u32[]{:S(2)}) %collective-permute-start.4) | collective-permute-done | bytes 262176 | tf_op jit(solution)/shard_map/ppermute | solution.py:17
  64.8 1.2 %collective-permute-done.5 = f32[1,2,1,256,128]{4,3,2,1,0:T(8,128)S(1)} collective-permute-done((f32[1,2,1,256,128]{4,3,2,1,0:T(8,128)S(1)}, f32[1,2,1,256,128]{4,3,2,1,0:T(8,128)S(1)}, u32[]{:S(2)}, u32[]{:S(2)}) %collective-permute-start.5) | collective-permute-done | bytes 262176 | tf_op jit(solution)/shard_map/ppermute | solution.py:15
  67.7 1.3 %collective-permute-start.6 = (f32[1,2,1,256,128]{4,3,2,1,0:T(8,128)S(1)}, f32[1,2,1,256,128]{4,3,2,1,0:T(8,128)S(1)}, u32[]{:S(2)}, u32[]{:S(2)}) collective-permute-start(f32[1,2,1,256,128]{4,3,2,1,0:T(8,128)S(1)} %get-tuple-element.148), channel_id=1, source_target_pairs={{4,0},{8,4},{12,8},{5,1},{9,5},{13,9},{6,2},{10,6},{14,10},{7,3},{... | collective-permute-start | bytes 786440 | tf_op jit(solution)/shard_map/ppermute | solution.py:17
  69.0 5.0 %collective-permute-start.7 = (f32[1,2,1,256,128]{4,3,2,1,0:T(8,128)S(1)}, f32[1,2,1,256,128]{4,3,2,1,0:T(8,128)S(1)}, u32[]{:S(2)}, u32[]{:S(2)}) collective-permute-start(f32[1,2,1,256,128]{4,3,2,1,0:T(8,128)S(1)} %get-tuple-element.149), channel_id=1, source_target_pairs={{0,4},{4,8},{8,12},{1,5},{5,9},{9,13},{2,6},{6,10},{10,14},{3,7},{... | collective-permute-start | bytes 786440 | tf_op jit(solution)/shard_map/ppermute | solution.py:15
  74.1 2.4 %collective-permute-done.6 = f32[1,2,1,256,128]{4,3,2,1,0:T(8,128)S(1)} collective-permute-done((f32[1,2,1,256,128]{4,3,2,1,0:T(8,128)S(1)}, f32[1,2,1,256,128]{4,3,2,1,0:T(8,128)S(1)}, u32[]{:S(2)}, u32[]{:S(2)}) %collective-permute-start.6) | collective-permute-done | bytes 262176 | tf_op jit(solution)/shard_map/ppermute | solution.py:17
  76.5 1.5 %collective-permute-done.7 = f32[1,2,1,256,128]{4,3,2,1,0:T(8,128)S(1)} collective-permute-done((f32[1,2,1,256,128]{4,3,2,1,0:T(8,128)S(1)}, f32[1,2,1,256,128]{4,3,2,1,0:T(8,128)S(1)}, u32[]{:S(2)}, u32[]{:S(2)}) %collective-permute-start.7) | collective-permute-done | bytes 262176 | tf_op jit(solution)/shard_map/ppermute | solution.py:15
  80.6 1.6 %fusion.41 = f32[4,256,128]{2,1,0:T(8,128)} fusion(f32[1,2,4,256,128]{4,3,2,1,0:T(8,128)S(1)} %maximum_select_fusion.3, f32[1,2,4,256,128]{4,3,2,1,0:T(8,128)S(1)} %copy-done.3, f32[4,256,128]{2,1,0:T(8,128)S(1)} %copy-done.1, f32[]{:T(128)} %fusion.45), kind=kLoop, calls=%fused_computation.78 | loop fusion | flops 786432 | bytes 3145732 | tf_op jit(solution)/shard_map/mul | solution.py:109
  82.3 24.7 %reduce-scatter.2.cloned.1.call-done = f32[4,64,128]{2,1,0:T(8,128)} async-done(((f32[4,256,128]{2,1,0:T(8,128)}), f32[4,64,128]{2,1,0:T(8,128)}) %reduce-scatter.2.cloned.1.call-update) | async-done | bytes 131088 | tf_op jit(solution)/shard_map/reduce_scatter | solution.py:110
  (94 shorter events, 18.5 us)
Async XLA Ops:
  7.2 10.3 %copy-start.4 = (f32[256,64]{0,1:T(8,128)S(1)}, f32[256,64]{0,1:T(8,128)}, u32[]{:S(2)}) copy-start(f32[256,64]{0,1:T(8,128)} %param.18) | copy-start | bytes 196612
  7.2 10.3 %copy-start.7 = (s32[256]{0:T(256)S(1)}, s32[256]{0:T(256)}, u32[]{:S(2)}) copy-start(s32[256]{0:T(256)} %param.20) | copy-start | bytes 3076
  7.2 10.5 %copy-start.8 = (s32[256]{0:T(256)S(1)}, s32[256]{0:T(256)}, u32[]{:S(2)}) copy-start(s32[256]{0:T(256)} %param.21) | copy-start | bytes 3076
  7.2 10.8 %copy-start.6 = (s32[256]{0:T(256)S(1)}, s32[256]{0:T(256)}, u32[]{:S(2)}) copy-start(s32[256]{0:T(256)} %param.19) | copy-start | bytes 3076
  7.2 10.8 %copy-start.5 = (f32[1,2,256]{2,1,0:T(2,128)S(1)}, f32[1,2,256]{2,1,0:T(2,128)}, u32[]{:S(2)}) copy-start(f32[1,2,256]{2,1,0:T(2,128)} %param.17) | copy-start | bytes 6148
  7.2 99.8 %reduce-scatter.2.cloned.1.call-start = ((), (), s32[]{:S(2)}) async-start(), calls=%async_computation.1 | async-start | bytes 655360 | tf_op jit(solution)/shard_map/reduce_scatter | solution.py:110
  9.1 31.1 %collective-permute-start = (f32[1,2,1,256,128]{4,3,2,1,0:T(8,128)}, f32[1,2,1,256,128]{4,3,2,1,0:T(8,128)}, u32[]{:S(2)}, u32[]{:S(2)}) collective-permute-start(f32[1,2,1,256,128]{4,3,2,1,0:T(8,128)} %get-tuple-element.154), channel_id=1, source_target_pairs={{4,0},{8,4},{12,8},{5,1},{9,5},{13,9},{6,2},{10,6},{14,10},{7,3},{... | collective-permute-start | bytes 786440 | tf_op jit(solution)/shard_map/ppermute | solution.py:17
  10.4 29.8 %collective-permute-start.1 = (f32[1,2,1,256,128]{4,3,2,1,0:T(8,128)}, f32[1,2,1,256,128]{4,3,2,1,0:T(8,128)}, u32[]{:S(2)}, u32[]{:S(2)}) collective-permute-start(f32[1,2,1,256,128]{4,3,2,1,0:T(8,128)} %get-tuple-element.155), channel_id=1, source_target_pairs={{0,4},{4,8},{8,12},{1,5},{5,9},{9,13},{2,6},{6,10},{10,14},{3,7},{... | collective-permute-start | bytes 786440 | tf_op jit(solution)/shard_map/ppermute | solution.py:15
  18.0 21.2 %copy-start.9 = (f32[4]{0:T(128)S(1)}, f32[4]{0:T(128)}, u32[]{:S(2)}) copy-start(f32[4]{0:T(128)} %param.15) | copy-start | bytes 52
  18.0 22.2 %copy-start = (f32[1,2,4,256,128]{4,3,2,1,0:T(8,128)S(1)}, f32[1,2,4,256,128]{4,3,2,1,0:T(8,128)}, u32[]{:S(2)}) copy-start(f32[1,2,4,256,128]{4,3,2,1,0:T(8,128)} %param.13) | copy-start | bytes 3145732
  40.2 1.7 %copy-start.1 = (f32[4,256,128]{2,1,0:T(8,128)S(1)}, f32[4,256,128]{2,1,0:T(8,128)}, u32[]{:S(2)}) copy-start(f32[4,256,128]{2,1,0:T(8,128)} %param.14) | copy-start | bytes 1572868
  43.0 9.7 %collective-permute-start.2 = (f32[1,2,1,256,128]{4,3,2,1,0:T(8,128)S(1)}, f32[1,2,1,256,128]{4,3,2,1,0:T(8,128)S(1)}, u32[]{:S(2)}, u32[]{:S(2)}) collective-permute-start(f32[1,2,1,256,128]{4,3,2,1,0:T(8,128)S(1)} %get-tuple-element.152), channel_id=1, source_target_pairs={{4,0},{8,4},{12,8},{5,1},{9,5},{13,9},{6,2},{10,6},{14,10},{7,3},{... | collective-permute-start | bytes 786440 | tf_op jit(solution)/shard_map/ppermute | solution.py:17
  44.3 9.5 %collective-permute-start.3 = (f32[1,2,1,256,128]{4,3,2,1,0:T(8,128)S(1)}, f32[1,2,1,256,128]{4,3,2,1,0:T(8,128)S(1)}, u32[]{:S(2)}, u32[]{:S(2)}) collective-permute-start(f32[1,2,1,256,128]{4,3,2,1,0:T(8,128)S(1)} %get-tuple-element.153), channel_id=1, source_target_pairs={{0,4},{4,8},{8,12},{1,5},{5,9},{9,13},{2,6},{6,10},{10,14},{3,7},{... | collective-permute-start | bytes 786440 | tf_op jit(solution)/shard_map/ppermute | solution.py:15
  55.5 9.3 %collective-permute-start.4 = (f32[1,2,1,256,128]{4,3,2,1,0:T(8,128)S(1)}, f32[1,2,1,256,128]{4,3,2,1,0:T(8,128)S(1)}, u32[]{:S(2)}, u32[]{:S(2)}) collective-permute-start(f32[1,2,1,256,128]{4,3,2,1,0:T(8,128)S(1)} %get-tuple-element.150), channel_id=1, source_target_pairs={{4,0},{8,4},{12,8},{5,1},{9,5},{13,9},{6,2},{10,6},{14,10},{7,3},{... | collective-permute-start | bytes 786440 | tf_op jit(solution)/shard_map/ppermute | solution.py:17
  56.8 9.1 %collective-permute-start.5 = (f32[1,2,1,256,128]{4,3,2,1,0:T(8,128)S(1)}, f32[1,2,1,256,128]{4,3,2,1,0:T(8,128)S(1)}, u32[]{:S(2)}, u32[]{:S(2)}) collective-permute-start(f32[1,2,1,256,128]{4,3,2,1,0:T(8,128)S(1)} %get-tuple-element.151), channel_id=1, source_target_pairs={{0,4},{4,8},{8,12},{1,5},{5,9},{9,13},{2,6},{6,10},{10,14},{3,7},{... | collective-permute-start | bytes 786440 | tf_op jit(solution)/shard_map/ppermute | solution.py:15
  67.7 8.7 %collective-permute-start.6 = (f32[1,2,1,256,128]{4,3,2,1,0:T(8,128)S(1)}, f32[1,2,1,256,128]{4,3,2,1,0:T(8,128)S(1)}, u32[]{:S(2)}, u32[]{:S(2)}) collective-permute-start(f32[1,2,1,256,128]{4,3,2,1,0:T(8,128)S(1)} %get-tuple-element.148), channel_id=1, source_target_pairs={{4,0},{8,4},{12,8},{5,1},{9,5},{13,9},{6,2},{10,6},{14,10},{7,3},{... | collective-permute-start | bytes 786440 | tf_op jit(solution)/shard_map/ppermute | solution.py:17
  69.0 8.9 %collective-permute-start.7 = (f32[1,2,1,256,128]{4,3,2,1,0:T(8,128)S(1)}, f32[1,2,1,256,128]{4,3,2,1,0:T(8,128)S(1)}, u32[]{:S(2)}, u32[]{:S(2)}) collective-permute-start(f32[1,2,1,256,128]{4,3,2,1,0:T(8,128)S(1)} %get-tuple-element.149), channel_id=1, source_target_pairs={{0,4},{4,8},{8,12},{1,5},{5,9},{9,13},{2,6},{6,10},{10,14},{3,7},{... | collective-permute-start | bytes 786440 | tf_op jit(solution)/shard_map/ppermute | solution.py:15
  79.4 1.2 %copy-start.3 = (f32[1,2,4,256,128]{4,3,2,1,0:T(8,128)S(1)}, f32[1,2,4,256,128]{4,3,2,1,0:T(8,128)}, u32[]{:S(2)}) copy-start(f32[1,2,4,256,128]{4,3,2,1,0:T(8,128)} %param.12) | copy-start | bytes 3145732
  80.6 1.6 %copy-start.2 = (f32[1,2,4,256,128]{4,3,2,1,0:T(8,128)}, f32[1,2,4,256,128]{4,3,2,1,0:T(8,128)S(1)}, u32[]{:S(2)}) copy-start(f32[1,2,4,256,128]{4,3,2,1,0:T(8,128)S(1)} %maximum_select_fusion.3) | copy-start | bytes 3145732
Sparse Core Ops, SparseCore 0:
  82.4 24.5 reduce-scatter.1
where the time goes:
time: 114 us
  waiting for transfers between devices  37.7 us (33%)
  starting transfers between devices  26.1 us (23%)
  between operations  15.1 us (13%)
  matrix products  11.9 us (10%)
  other arithmetic  11 us (10%)
  local copies, waits for them, and re-layouts  9.25 us (8%)
  loops' own time  2.83 us (2%)
    reduce_scatter x1, waiting for transfers between devices, body(): lax.psum_scatter(partial_terms, 'src', scatter_dimension=1, tiled=True)  24.7 us
    ppermute x4, starting transfers between devices, with_halo(): lax.ppermute(tail, axis, [(i, (i + 1) % count) for i in range(ends)])  20.9 us
    ppermute x4, waiting for transfers between devices, with_halo(): lax.ppermute(head, axis, [((i + 1) % count, i) for i in range(ends)])  9.12 us
    dot_general x4, matrix products, one_layer(): jnp.einsum('rbk,rkz->rbz', plane, col_match, precision=lax.Precision.HIGH...  7.46 us
    ppermute x4, starting transfers between devices, with_halo(): lax.ppermute(head, axis, [((i + 1) % count, i) for i in range(ends)])  5.16 us
    dot_general x4, matrix products, one_layer(): jnp.einsum('ym,pcmz->pcyz', row_match, scaled, precision=lax.Precision.HI...  4.46 us
    ppermute x4, waiting for transfers between devices, with_halo(): lax.ppermute(tail, axis, [(i, (i + 1) % count) for i in range(ends)])  3.82 us
    add x4, other arithmetic, neighbour_update(): sums = source + beside_all  3.52 us
  transfers between devices with their start and end apart: 9, of which 7 were waited for; matrix products, arithmetic and copies ran while one was open for 17% of the time, Pallas kernels for 0%

commit v1 on v0

v1 whole, which is shorter than its diff:
```python
import functools

import jax
import jax.numpy as jnp
from jax import lax
from jax.experimental import pallas as pl
from jax.experimental.pallas import tpu as pltpu
from jax.sharding import PartitionSpec as P

SWEEPS = 4
COLOURS = tuple(k % 2 for k in range(SWEEPS))
HALO_CELLS = tuple(
    (d, c)
    for d in range(1, SWEEPS)
    for c in (0, 1)
    if any(COLOURS[k] == c and d <= SWEEPS - 1 - k for k in range(SWEEPS))
)
PAD = 8
ROWS = 32
UNROLL = 8
SMEM = pl.BlockSpec(memory_space=pltpu.SMEM)
VMEM = pl.BlockSpec(memory_space=pltpu.VMEM)


def odd_lanes(shift, rows, cols):
    return ((lax.broadcasted_iota(jnp.int32, (rows, cols), 1) + shift) & 1) == 1


def of_colour(colour, odd, even_rows, odd_rows):
    if colour == 0:
        return jnp.where(odd, odd_rows, even_rows)
    return jnp.where(odd, even_rows, odd_rows)


def kappa_of(kappa_ref, freq_ref):
    return kappa_ref[freq_ref[0]]


def coefficients(kappa, conductivity):
    coupling = kappa * conductivity
    inverse = 1.0 / (36.0 + coupling * coupling)
    return 6.0 * inverse, coupling * inverse


def pack_kernel(guess_ref, cond_ref, adj_ref, even_ref, odd_ref):
    layers, size_y, size_z = cond_ref.shape
    half = size_y // 2
    rows = min(ROWS, half)
    tile = lax.axis_index("tile")
    first = tile * layers

    for i, (d, c) in enumerate(HALO_CELLS):
        for ref, to_right in ((even_ref, tile % 2 == 0), (odd_ref, tile % 2 == 1)):
            layer = jnp.where(to_right, layers - d, d - 1)
            odd = odd_lanes(first + layer, rows, size_z)
            for r in range(0, half, rows):
                a = cond_ref[layer, pl.ds(2 * r, rows, stride=2), :]
                b = cond_ref[layer, pl.ds(2 * r + 1, rows, stride=2), :]
                ref[i, pl.ds(r, rows), :] = of_colour(c, odd, a, b)
    for layer in range(layers):
        odd = odd_lanes(first + layer, rows, size_z)
        for part in range(2):
            for r in range(0, half, rows):
                a = guess_ref[0, part, layer, pl.ds(2 * r, rows, stride=2), :]
                b = guess_ref[0, part, layer, pl.ds(2 * r + 1, rows, stride=2), :]
                adj_ref[part, layer, pl.ds(r, rows), :] = of_colour(1, odd, a, b)


def source_kernel(
    x_ref, y_ref, z_ref, kappa_ref, freq_ref, weight_ref, data_ref, cond_ref,
    source_ref, six_ref, cross_ref, terms_ref, total_ref,
):
    layers, size_y, size_z = cond_ref.shape
    half = size_y // 2
    rows = min(ROWS, half)
    taps, count = weight_ref.shape
    reach = source_ref.shape[2]
    halo = SWEEPS - 1
    first = lax.axis_index("tile") * layers
    kappa = kappa_of(kappa_ref, freq_ref)

    blank = jnp.zeros((size_z - taps, count), jnp.float32)
    weights = weight_ref[...]
    for c in range(2):
        terms = jnp.concatenate([weights * data_ref[0, c : c + 1, :], blank], axis=0).T
        for b in range(4):
            moved = pltpu.roll(terms, size_z - 4 * b, 1) if b else terms
            terms_ref[pl.ds(2 * b + c, count, stride=8), :] = moved
    for layer in range(reach):
        total_ref[4 + layer] = jnp.zeros(total_ref.shape[1:], jnp.float32)

    lane = lax.broadcasted_iota(jnp.int32, (8, size_z), 1)
    def add_block(r):
        z = z_ref[r]
        base = jnp.clip(x_ref[r] - first + halo, -4, reach) + 4
        row = 2 * y_ref[r]
        inside = (lane - z).astype(jnp.uint32) < 4
        both = terms_ref[pl.ds(pl.multiple_of(8 * r, 8), 8), :]
        terms = []
        for a in range(4):
            moved = pltpu.roll(both, lax.rem(z + size_z - 16 * a, size_z), 1)
            terms.append(jnp.where(inside, moved, 0.0))
        old = [total_ref[base + a, pl.ds(row, 8), :] for a in range(4)]
        for a in range(4):
            total_ref[base + a, pl.ds(row, 8), :] = old[a] + terms[a]

    def some_blocks(step, carry):
        for u in range(UNROLL):
            add_block(step * UNROLL + u)
        return carry

    lax.fori_loop(0, count // UNROLL, some_blocks, 0)

    for layer in range(layers):
        odd = odd_lanes(first + layer, rows, size_z)
        for r in range(0, half, rows):
            a = cond_ref[layer, pl.ds(2 * r, rows, stride=2), :]
            b = cond_ref[layer, pl.ds(2 * r + 1, rows, stride=2), :]
            for c in (0, 1):
                six, cross = coefficients(kappa, of_colour(c, odd, a, b))
                six_ref[c, layer, pl.ds(r, rows), :] = six
                cross_ref[c, layer, pl.ds(r, rows), :] = cross

    def pack_layer(layer, carry):
        odd = odd_lanes(first + layer - halo, rows, size_z)
        for part in range(2):
            for r in range(0, half, rows):
                a = total_ref[4 + layer, pl.ds(4 * r + part, rows, stride=4), :]
                b = total_ref[4 + layer, pl.ds(4 * r + 2 + part, rows, stride=4), :]
                for c in (0, 1):
                    source_ref[c, part, layer, pl.ds(r, rows), :] = of_colour(c, odd, a, b)
        return carry

    lax.fori_loop(0, reach, pack_layer, 0)


def sweep_kernel(
    kappa_ref, freq_ref, adj_ref, adj_even_ref, adj_odd_ref, cond_even_ref, cond_odd_ref,
    source_ref, six_own_ref, cross_own_ref, cond_ref, forward_ref,
    out_ref, send_ref, keep_ref, zero_ref, one_ref, six_ref, cross_ref,
):
    layers, size_y, size_z = cond_ref.shape
    half = size_y // 2
    rows = min(ROWS, half)
    tile = lax.axis_index("tile")
    tiles = lax.axis_size("tile")
    first = tile * layers
    kappa = kappa_of(kappa_ref, freq_ref)
    depth = SWEEPS
    slots = layers + 2 * depth
    packed = (zero_ref, one_ref)

    edge = jnp.zeros((PAD, size_z), jnp.float32)
    for ref in packed:
        for part in range(2):
            for slot in range(slots):
                ref[part, slot, pl.ds(0, PAD), :] = edge
                ref[part, slot, pl.ds(PAD + half, PAD), :] = edge
    for part in range(2):
        for layer in range(layers):
            one_ref[part, depth + layer, pl.ds(PAD, half), :] = adj_ref[part, layer]
    for c in (0, 1):
        for layer in range(layers):
            six_ref[c, depth + layer] = six_own_ref[c, layer]
            cross_ref[c, depth + layer] = cross_own_ref[c, layer]
    for near, cells, on_right in (
        (adj_even_ref, cond_even_ref, tile % 2 == 0),
        (adj_odd_ref, cond_odd_ref, tile % 2 == 1),
    ):
        base = jnp.where(on_right, depth + layers, 0)
        there = jnp.where(jnp.where(on_right, tile < tiles - 1, tile > 0), 1.0, 0.0)
        for part in range(2):
            for layer in range(depth):
                one_ref[part, base + layer, pl.ds(PAD, half), :] = near[part, layer]
        for i, (d, c) in enumerate(HALO_CELLS):
            slot = jnp.where(on_right, depth + layers - 1 + d, depth - d)
            for r in range(0, half, rows):
                six, cross = coefficients(kappa, cells[i, pl.ds(r, rows), :])
                six_ref[c, slot, pl.ds(r, rows), :] = six * there
                cross_ref[c, slot, pl.ds(r, rows), :] = cross * there

    lane = lax.broadcasted_iota(jnp.int32, (rows, size_z), 1)

    def update_layer(c, slot):
        old, new = packed[1 - c], packed[c]
        odd = odd_lanes(first + slot - depth + c, rows, size_z)
        for r in range(0, half, rows):
            sums = []
            for part in range(2):
                here = old[part, slot, pl.ds(PAD + r, rows), :]
                above = old[part, slot, pl.ds(PAD + r + 1, rows), :]
                below = old[part, slot, pl.ds(PAD + r - 1, rows), :]
                total = old[part, slot - 1, pl.ds(PAD + r, rows), :]
                total += old[part, slot + 1, pl.ds(PAD + r, rows), :]
                total += here + jnp.where(odd, above, below)
                total += jnp.where(lane > 0, pltpu.roll(here, 1, 1), 0.0)
                total += jnp.where(lane < size_z - 1, pltpu.roll(here, size_z - 1, 1), 0.0)
                sums.append(total + source_ref[c, part, slot - 1, pl.ds(r, rows), :])
            six = six_ref[c, slot, pl.ds(r, rows), :]
            cross = cross_ref[c, slot, pl.ds(r, rows), :]
            new[0, slot, pl.ds(PAD + r, rows), :] = six * sums[0] + cross * sums[1]
            new[1, slot, pl.ds(PAD + r, rows), :] = six * sums[1] - cross * sums[0]

    for k, c in enumerate(COLOURS):

        def one_layer(slot, carry, c=c):
            update_layer(c, slot)
            return carry

        lax.fori_loop(1 + k, slots - 1 - k, one_layer, 0)

    shards = 2 * send_ref.shape[0]
    shard_rows = size_y // shards
    shard = lax.axis_index("src")
    for layer in range(layers):
        odd = odd_lanes(first + layer, rows, size_z)
        for part in range(2):
            for r in range(0, half, rows):
                a = zero_ref[part, depth + layer, pl.ds(PAD + r, rows), :]
                b = one_ref[part, depth + layer, pl.ds(PAD + r, rows), :]
                out_ref[0, part, layer, pl.ds(2 * r, rows, stride=2), :] = jnp.where(odd, b, a)
                out_ref[0, part, layer, pl.ds(2 * r + 1, rows, stride=2), :] = jnp.where(odd, a, b)

    def one_gradient(layer, carry):
        for m in range(shards):
            ref = send_ref if m % 2 else keep_ref
            start = pl.multiple_of((shard ^ m) * shard_rows, shard_rows)
            at = pl.ds(start, shard_rows)
            products = forward_ref[0, 0, layer, at, :] * out_ref[0, 1, layer, at, :]
            products += forward_ref[0, 1, layer, at, :] * out_ref[0, 0, layer, at, :]
            ref[m // 2, layer] = -cond_ref[layer, at, :] * (kappa * products)
        return carry

    lax.fori_loop(0, layers, one_gradient, 0)


def call(kernel, outs, scratch, specs, out_specs, flops):
    return pl.pallas_call(
        kernel,
        out_shape=[jax.ShapeDtypeStruct(s, jnp.float32) for s in outs],
        in_specs=specs,
        out_specs=out_specs,
        scratch_shapes=[pltpu.VMEM(s, jnp.float32) for s in scratch],
        compiler_params=pltpu.CompilerParams(vmem_limit_bytes=32 << 20),
        cost_estimate=pl.CostEstimate(flops=flops, bytes_accessed=4 << 20, transcendentals=0),
    )


def swap_even(count):
    return [(i, i ^ 1) for i in range(count) if i ^ 1 < count]


def swap_odd(count):
    pairs = [(i, i + 1) for i in range(1, count - 1, 2)]
    return pairs + [(b, a) for a, b in pairs]


def body(
    forward_field,
    adjoint_guess,
    conductivity,
    freq_kappa,
    pair_freq,
    recv_data,
    recv_weights,
    recv_x,
    recv_y,
    recv_z,
):
    pairs, _, layers, size_y, size_z = adjoint_guess.shape
    half = size_y // 2
    count, taps = recv_weights.shape
    tiles = lax.axis_size("tile")
    shards = lax.axis_size("src")
    assert pairs == 1 and layers == SWEEPS and count % UNROLL == 0
    cells = len(HALO_CELLS)
    reach = layers + 2 * (SWEEPS - 1)

    adj, cond_even, cond_odd = call(
        pack_kernel,
        [(2, layers, half, size_z), (cells, half, size_z), (cells, half, size_z)],
        [],
        [VMEM, VMEM],
        [VMEM] * 3,
        1 << 20,
    )(adjoint_guess, conductivity)

    evens, odds = swap_even(tiles), swap_odd(tiles)
    cond_odd = lax.ppermute(cond_odd, "tile", odds)
    cond_even = lax.ppermute(cond_even, "tile", evens)
    adj_odd = lax.ppermute(adj, "tile", odds)
    adj_even = lax.ppermute(adj, "tile", evens)

    source, six, cross = call(
        source_kernel,
        [(2, 2, reach, half, size_z), (2, layers, half, size_z), (2, layers, half, size_z)],
        [(8 * count, size_z), (reach + 8, 2 * size_y, size_z)],
        [SMEM] * 5 + [VMEM] * 3,
        [VMEM] * 3,
        1 << 30,
    )(
        recv_x, recv_y, recv_z, freq_kappa, pair_freq, recv_weights.T, recv_data, conductivity
    )

    slots = layers + 2 * SWEEPS
    shard_rows = size_y // shards
    field, send, keep = call(
        sweep_kernel,
        [
            (1, 2, layers, size_y, size_z),
            (shards // 2, layers, shard_rows, size_z),
            (shards // 2, layers, shard_rows, size_z),
        ],
        [(2, slots, half + 2 * PAD, size_z)] * 2 + [(2, slots, half, size_z)] * 2,
        [SMEM] * 2 + [VMEM] * 10,
        [VMEM] * 3,
        1 << 26,
    )(
        freq_kappa, pair_freq, adj, adj_even, adj_odd, cond_even, cond_odd,
        source, six, cross, conductivity, forward_field,
    )

    bit = 1
    while True:
        swap = [(i, i ^ bit) for i in range(shards)]
        keep = keep + lax.ppermute(send, "src", swap)
        bit *= 2
        if bit == shards:
            break
        send, keep = keep[1::2], keep[0::2]
    return (field, keep[0])


def solution(mesh):
    placed = (
        P(("job", "src"), None, "tile", None, None),
        P(("job", "src"), None, "tile", None, None),
        P(("job", "tile"), None, None),
        P("job"),
        P(("job", "src")),
        P(("job", "src"), None, None),
        P("job", None),
        P("job"),
        P("job"),
        P("job"),
    )
    return jax.shard_map(
        body,
        mesh=mesh,
        in_specs=placed,
        out_specs=(P(("job", "src"), None, "tile", None, None), P(("job", "tile"), "src", None)),
        check_vma=False,
    )
```

time: 114 us -> 43.1 us (0.38)
  waiting for transfers between devices: 37.7 us -> 12.5 us
  starting transfers between devices: 26.1 us -> 9.04 us
  between operations: 15.1 us -> 1.36 us
  Pallas kernels: 0 us -> 12.6 us
  matrix products: 11.9 us -> 0 us
  other arithmetic: 11 us -> 0.7 us
  loops' own time: 2.83 us -> 0 us
  local copies, waits for them, and re-layouts: 9.25 us -> 6.48 us
    reduce_scatter x1 -> x0, waiting for transfers between devices: 24.7 us -> none  [body(): lax.psum_scatter(partial_terms, 'src', scatter_dimension=1, tiled=True)]
    ppermute x8 -> x6, starting transfers between devices: 26.1 us -> 9.04 us  [the longest x1 5.91 us: body(): adj_even = lax.ppermute(adj, 'tile', evens)]
    pallas_call x0 -> x3, Pallas kernels: none -> 12.6 us  [the longest x1 6.41 us: body(): call(sweep_kernel, [(1, 2, layers, size_y, size_z), (shards // 2, layers,...]
    dot_general x8 -> x0, matrix products: 11.9 us -> none  [the longest x4 7.46 us: one_layer(): jnp.einsum('rbk,rkz->rbz', plane, col_match, precision=lax.Precision.HIGH...]
    unnamed x20, local copies, waits for them, and re-layouts: 0.95 us -> 6.47 us
    add x8 -> x1, other arithmetic: 3.7 us -> 0.03 us  [body(): keep = keep + lax.ppermute(send, 'src', swap)]
    another operation x4 -> x0, other arithmetic: 3.43 us -> none  [neighbour_update(): jnp.stack([real_part, imag_part], axis=1)]
    another operation x1 -> x0, loops' own time: 2.83 us -> none  [local_source(): stacked = lax.map(one_layer, jnp.arange(layers, dtype=jnp.int32))]
  transfers between devices with their start and end apart: 9 -> 6, of which waited for: 7 -> 3; matrix products, arithmetic and copies ran while one was open for 17% -> 0% of each run, Pallas kernels for 0% -> 14%
where the time goes in v1:
time: 43.1 us; the launch traced here: 42.7 us
  Pallas kernels  12.6 us (29%)
  waiting for transfers between devices  12.5 us (29%)
  starting transfers between devices  9.04 us (21%)
  local copies, waits for them, and re-layouts  6.48 us (15%)
  between operations  1.36 us (3%)
  other arithmetic  0.7 us (2%)
    ppermute x1, waiting for transfers between devices, body(): cond_even = lax.ppermute(cond_even, 'tile', evens)  6.96 us
    unnamed x20, local copies, waits for them, and re-layouts  6.47 us
    pallas_call x1, Pallas kernels, body(): call(sweep_kernel, [(1, 2, layers, size_y, size_z), (shards // 2, layers,...  6.41 us
    pallas_call x1, Pallas kernels, body(): call(source_kernel, [(2, 2, reach, half, size_z), (2, layers, half, size_...  6.07 us
    ppermute x1, starting transfers between devices, body(): adj_even = lax.ppermute(adj, 'tile', evens)  5.91 us
    ppermute x2, waiting for transfers between devices, body(): keep = keep + lax.ppermute(send, 'src', swap)  5.58 us
    ppermute x2, starting transfers between devices, body(): keep = keep + lax.ppermute(send, 'src', swap)  1.56 us
  transfers between devices with their start and end apart: 6, of which 3 were waited for; matrix products, arithmetic and copies ran while one was open for 0% of the time, Pallas kernels for 14%

profile of v1, /device:TPU:0, one launch (start us, length us, event | category | flops | bytes accessed | tf_op | source)
XLA Modules:
  0.0 42.7 jit_solution(3672660457877130888)
XLA Ops:
  0.6 1.0 %copy-done = f32[4,256,128]{2,1,0:T(8,128)S(1)} copy-done((f32[4,256,128]{2,1,0:T(8,128)S(1)}, f32[4,256,128]{2,1,0:T(8,128)}, u32[]{:S(2)}) %copy-start) | copy-done | bytes 524312
  1.7 1.2 %copy-done.2 = f32[1,2,4,256,128]{4,3,2,1,0:T(8,128)S(1)} copy-done((f32[1,2,4,256,128]{4,3,2,1,0:T(8,128)S(1)}, f32[1,2,4,256,128]{4,3,2,1,0:T(8,128)}, u32[]{:S(2)}) %copy-start.2) | copy-done | bytes 1048600
  2.9 0.1 shard_map.113
  3.0 0.8 %collective-permute-start.1 = (f32[2,4,128,128]{3,2,1,0:T(8,128)S(1)}, f32[2,4,128,128]{3,2,1,0:T(8,128)S(1)}, u32[]{:S(2)}, u32[]{:S(2)}) collective-permute-start(f32[2,4,128,128]{3,2,1,0:T(8,128)S(1)} %get-tuple-element.11.adj_ref), channel_id=1, source_target_pairs={{4,8},{8,4},{5,9},{9,5},{6,10},{10,6},{7,11},{11,7},{20,24},{24,20... | collective-permute-start | bytes 1572872 | tf_op jit(solution)/shard_map/ppermute | solution.py:291
  3.9 5.9 %collective-permute-start = (f32[2,4,128,128]{3,2,1,0:T(8,128)S(1)}, f32[2,4,128,128]{3,2,1,0:T(8,128)S(1)}, u32[]{:S(2)}, u32[]{:S(2)}) collective-permute-start(f32[2,4,128,128]{3,2,1,0:T(8,128)S(1)} %get-tuple-element.11.adj_ref), channel_id=1, source_target_pairs={{0,4},{4,0},{8,12},{12,8},{1,5},{5,1},{9,13},{13,9},{2,6},{6,2},{1... | collective-permute-start | bytes 1572872 | tf_op jit(solution)/shard_map/ppermute | solution.py:292
  9.8 0.1 collective-permute-start.2
  9.8 0.7 %collective-permute-start.3 = (f32[5,128,128]{2,1,0:T(8,128)S(1)}, f32[5,128,128]{2,1,0:T(8,128)S(1)}, u32[]{:S(2)}, u32[]{:S(2)}) collective-permute-start(f32[5,128,128]{2,1,0:T(8,128)S(1)} %get-tuple-element.13), channel_id=1, source_target_pairs={{4,8},{8,4},{5,9},{9,5},{6,10},{10,6},{7,11},{11,7},{20,24},{24,20... | collective-permute-start | bytes 983048 | tf_op jit(solution)/shard_map/ppermute | solution.py:289
  11.2 0.0 copy-start.4
  11.2 0.6 %copy-done.4 = f32[4]{0:T(128)S(1)} copy-done((f32[4]{0:T(128)S(1)}, f32[4]{0:T(128)}, u32[]{:S(2)}) %copy-start.4) | copy-done | bytes 40
  11.8 0.8 %copy-done.5 = f32[256,64]{0,1:T(8,128)S(1)} copy-done((f32[256,64]{0,1:T(8,128)S(1)}, f32[256,64]{0,1:T(8,128)}, u32[]{:S(2)}) %copy-start.5) | copy-done | bytes 65560
  12.7 0.7 %copy-done.6 = f32[1,2,256]{2,1,0:T(2,128)S(1)} copy-done((f32[1,2,256]{2,1,0:T(2,128)S(1)}, f32[1,2,256]{2,1,0:T(2,128)}, u32[]{:S(2)}) %copy-start.6) | copy-done | bytes 2072
  13.4 0.7 %copy-done.7 = s32[256]{0:T(256)S(1)} copy-done((s32[256]{0:T(256)S(1)}, s32[256]{0:T(256)}, u32[]{:S(2)}) %copy-start.7) | copy-done | bytes 1048
  14.0 0.7 %copy-done.8 = s32[256]{0:T(256)S(1)} copy-done((s32[256]{0:T(256)S(1)}, s32[256]{0:T(256)}, u32[]{:S(2)}) %copy-start.8) | copy-done | bytes 1048
  14.7 0.7 %copy-done.9 = s32[256]{0:T(256)S(1)} copy-done((s32[256]{0:T(256)S(1)}, s32[256]{0:T(256)}, u32[]{:S(2)}) %copy-start.9) | copy-done | bytes 1048
  15.4 6.1 %shard_map.114 = (f32[2,2,10,128,128]{4,3,2,1,0:T(8,128)S(1)}, f32[2,4,128,128]{3,2,1,0:T(8,128)S(1)}, f32[2,4,128,128]{3,2,1,0:T(8,128)S(1)}) custom-call(s32[256]{0:T(256)S(1)} %copy-done.7, s32[256]{0:T(256)S(1)} %copy-done.8, s32[256]{0:T(256)S(1)} %copy-done.9, f32[4]{0:T(128)S(1)} %copy-done.4, s32[1]{0:T(128)S(6)} %copy.12.freq_ref, ...), custom_call_target="tpu_custom_call" | custom-call | flops 1073741824 | bytes 4194304 | tf_op jit(solution)/shard_map/pallas_call | solution.py:294
  21.5 7.0 %collective-permute-done.2.cond_even_ref = f32[5,128,128]{2,1,0:T(8,128)S(1)} collective-permute-done((f32[5,128,128]{2,1,0:T(8,128)S(1)}, f32[5,128,128]{2,1,0:T(8,128)S(1)}, u32[]{:S(2)}, u32[]{:S(2)}) %collective-permute-start.2) | collective-permute-done | bytes 327712 | tf_op jit(solution)/shard_map/ppermute | solution.py:290
  28.4 0.0 collective-permute-done.3.cond_odd_ref
  28.4 0.0 collective-permute-done.1.adj_odd_ref
  28.4 0.0 collective-permute-done.adj_even_ref
  28.5 6.4 %shard_map.115 = (f32[1,2,4,256,128]{4,3,2,1,0:T(8,128)}, f32[2,4,64,128]{3,2,1,0:T(8,128)S(1)}, f32[2,4,64,128]{3,2,1,0:T(8,128)S(1)}) custom-call(f32[4]{0:T(128)S(1)} %copy-done.4, s32[1]{0:T(128)S(6)} %copy.12.freq_ref, f32[2,4,128,128]{3,2,1,0:T(8,128)S(1)} %get-tuple-element.11.adj_ref, f32[2,4,128,128]{3,2,1,0:T(8,128)S(1)} %collective-permute-done.adj_even_ref, ...), custom_call_target="tpu_custom_call" | custom-call | flops 67108864 | bytes 4194304 | tf_op jit(solution)/shard_map/pallas_call | solution.py:307
  34.9 1.5 %collective-permute-done.4 = f32[2,4,64,128]{3,2,1,0:T(8,128)S(1)} collective-permute-done((f32[2,4,64,128]{3,2,1,0:T(8,128)S(1)}, f32[2,4,64,128]{3,2,1,0:T(8,128)S(1)}, u32[]{:S(2)}, u32[]{:S(2)}) %collective-permute-start.4) | collective-permute-done | bytes 262176 | tf_op jit(solution)/shard_map/ppermute | solution.py:326
  36.5 1.6 %collective-permute-start.5 = (f32[1,4,64,128]{3,2,1,0:T(8,128)S(1)}, f32[1,4,64,128]{3,2,1,0:T(8,128)S(1)}, u32[]{:S(2)}, u32[]{:S(2)}) collective-permute-start(f32[1,4,64,128]{3,2,1,0:T(8,128)S(1)} %slice.11), channel_id=1, source_target_pairs={{0,2},{1,3},{2,0},{3,1},{4,6},{5,7},{6,4},{7,5},{8,10},{9,11},{10,... | collective-permute-start | bytes 393224 | tf_op jit(solution)/shard_map/ppermute | solution.py:326
  38.0 4.0 %collective-permute-done.5 = f32[1,4,64,128]{3,2,1,0:T(8,128)S(1)} collective-permute-done((f32[1,4,64,128]{3,2,1,0:T(8,128)S(1)}, f32[1,4,64,128]{3,2,1,0:T(8,128)S(1)}, u32[]{:S(2)}, u32[]{:S(2)}) %collective-permute-start.5) | collective-permute-done | bytes 131104 | tf_op jit(solution)/shard_map/ppermute | solution.py:326
  42.1 0.7 %fusion = f32[4,64,128]{2,1,0:T(8,128)} fusion(f32[1,4,64,128]{3,2,1,0:T(8,128)S(1)} %collective-permute-done.5, f32[2,4,64,128]{3,2,1,0:T(8,128)S(1)} %add.6), kind=kLoop, calls=%fused_computation.1 | loop fusion | flops 32768 | bytes 393216 | tf_op jit(solution)/shard_map/squeeze | solution.py:331
  (14 shorter events, 0.1 us)
Async XLA Ops:
  0.6 1.0 %copy-start = (f32[4,256,128]{2,1,0:T(8,128)S(1)}, f32[4,256,128]{2,1,0:T(8,128)}, u32[]{:S(2)}) copy-start(f32[4,256,128]{2,1,0:T(8,128)} %cond_ref.5) | copy-start | bytes 1572868
  1.7 1.2 %copy-start.2 = (f32[1,2,4,256,128]{4,3,2,1,0:T(8,128)S(1)}, f32[1,2,4,256,128]{4,3,2,1,0:T(8,128)}, u32[]{:S(2)}) copy-start(f32[1,2,4,256,128]{4,3,2,1,0:T(8,128)} %guess_ref.1) | copy-start | bytes 3145732
  2.9 25.6 %copy-start.1 = (f32[4,256,128]{2,1,0:T(8,128)S(1)}, f32[4,256,128]{2,1,0:T(8,128)}, u32[]{:S(2)}) copy-start(f32[4,256,128]{2,1,0:T(8,128)} %cond_ref.5) | copy-start | bytes 1572868
  2.9 25.6 %copy-start.3 = (f32[1,2,4,256,128]{4,3,2,1,0:T(8,128)S(1)}, f32[1,2,4,256,128]{4,3,2,1,0:T(8,128)}, u32[]{:S(2)}) copy-start(f32[1,2,4,256,128]{4,3,2,1,0:T(8,128)} %forward_ref.1) | copy-start | bytes 3145732
  3.0 25.4 %collective-permute-start.1 = (f32[2,4,128,128]{3,2,1,0:T(8,128)S(1)}, f32[2,4,128,128]{3,2,1,0:T(8,128)S(1)}, u32[]{:S(2)}, u32[]{:S(2)}) collective-permute-start(f32[2,4,128,128]{3,2,1,0:T(8,128)S(1)} %get-tuple-element.11.adj_ref), channel_id=1, source_target_pairs={{4,8},{8,4},{5,9},{9,5},{6,10},{10,6},{7,11},{11,7},{20,24},{24,20... | collective-permute-start | bytes 1572872 | tf_op jit(solution)/shard_map/ppermute | solution.py:291
  3.9 24.6 %collective-permute-start = (f32[2,4,128,128]{3,2,1,0:T(8,128)S(1)}, f32[2,4,128,128]{3,2,1,0:T(8,128)S(1)}, u32[]{:S(2)}, u32[]{:S(2)}) collective-permute-start(f32[2,4,128,128]{3,2,1,0:T(8,128)S(1)} %get-tuple-element.11.adj_ref), channel_id=1, source_target_pairs={{0,4},{4,0},{8,12},{12,8},{1,5},{5,1},{9,13},{13,9},{2,6},{6,2},{1... | collective-permute-start | bytes 1572872 | tf_op jit(solution)/shard_map/ppermute | solution.py:292
  9.8 18.7 %collective-permute-start.2 = (f32[5,128,128]{2,1,0:T(8,128)S(1)}, f32[5,128,128]{2,1,0:T(8,128)S(1)}, u32[]{:S(2)}, u32[]{:S(2)}) collective-permute-start(f32[5,128,128]{2,1,0:T(8,128)S(1)} %get-tuple-element.12), channel_id=1, source_target_pairs={{0,4},{4,0},{8,12},{12,8},{1,5},{5,1},{9,13},{13,9},{2,6},{6,2},{1... | collective-permute-start | bytes 983048 | tf_op jit(solution)/shard_map/ppermute | solution.py:290
  9.8 18.6 %collective-permute-start.3 = (f32[5,128,128]{2,1,0:T(8,128)S(1)}, f32[5,128,128]{2,1,0:T(8,128)S(1)}, u32[]{:S(2)}, u32[]{:S(2)}) collective-permute-start(f32[5,128,128]{2,1,0:T(8,128)S(1)} %get-tuple-element.13), channel_id=1, source_target_pairs={{4,8},{8,4},{5,9},{9,5},{6,10},{10,6},{7,11},{11,7},{20,24},{24,20... | collective-permute-start | bytes 983048 | tf_op jit(solution)/shard_map/ppermute | solution.py:289
  11.2 0.7 %copy-start.4 = (f32[4]{0:T(128)S(1)}, f32[4]{0:T(128)}, u32[]{:S(2)}) copy-start(f32[4]{0:T(128)} %kappa_ref.3) | copy-start | bytes 52
  11.8 0.8 %copy-start.5 = (f32[256,64]{0,1:T(8,128)S(1)}, f32[256,64]{0,1:T(8,128)}, u32[]{:S(2)}) copy-start(f32[256,64]{0,1:T(8,128)} %param.16) | copy-start | bytes 196612
  12.7 0.7 %copy-start.6 = (f32[1,2,256]{2,1,0:T(2,128)S(1)}, f32[1,2,256]{2,1,0:T(2,128)}, u32[]{:S(2)}) copy-start(f32[1,2,256]{2,1,0:T(2,128)} %data_ref.1) | copy-start | bytes 6148
  13.4 0.7 %copy-start.7 = (s32[256]{0:T(256)S(1)}, s32[256]{0:T(256)}, u32[]{:S(2)}) copy-start(s32[256]{0:T(256)} %x_ref.1) | copy-start | bytes 3076
  14.0 0.7 %copy-start.8 = (s32[256]{0:T(256)S(1)}, s32[256]{0:T(256)}, u32[]{:S(2)}) copy-start(s32[256]{0:T(256)} %y_ref.1) | copy-start | bytes 3076
  14.7 0.7 %copy-start.9 = (s32[256]{0:T(256)S(1)}, s32[256]{0:T(256)}, u32[]{:S(2)}) copy-start(s32[256]{0:T(256)} %z_ref.1) | copy-start | bytes 3076
  34.9 1.5 %collective-permute-start.4 = (f32[2,4,64,128]{3,2,1,0:T(8,128)S(1)}, f32[2,4,64,128]{3,2,1,0:T(8,128)S(1)}, u32[]{:S(2)}, u32[]{:S(2)}) collective-permute-start(f32[2,4,64,128]{3,2,1,0:T(8,128)S(1)} %get-tuple-element.19), channel_id=1, source_target_pairs={{0,1},{1,0},{2,3},{3,2},{4,5},{5,4},{6,7},{7,6},{8,9},{9,8},{10,11... | collective-permute-start | bytes 786440 | tf_op jit(solution)/shard_map/ppermute | solution.py:326
  36.5 5.6 %collective-permute-start.5 = (f32[1,4,64,128]{3,2,1,0:T(8,128)S(1)}, f32[1,4,64,128]{3,2,1,0:T(8,128)S(1)}, u32[]{:S(2)}, u32[]{:S(2)}) collective-permute-start(f32[1,4,64,128]{3,2,1,0:T(8,128)S(1)} %slice.11), channel_id=1, source_target_pairs={{0,2},{1,3},{2,0},{3,1},{4,6},{5,7},{6,4},{7,5},{8,10},{9,11},{10,... | collective-permute-start | bytes 393224 | tf_op jit(solution)/shard_map/ppermute | solution.py:326

commit v2 on v1

v2 whole, which is shorter than its diff:
```python
import jax
import jax.numpy as jnp
from jax import lax
from jax.experimental import pallas as pl
from jax.experimental.pallas import tpu as pltpu
from jax.sharding import PartitionSpec as P


SWEEPS = 4
COLOURS = tuple(k % 2 for k in range(SWEEPS))
HALO_CELLS = tuple(
    (d, c)
    for d in range(1, SWEEPS)
    for c in (0, 1)
    if any(COLOURS[k] == c and d <= SWEEPS - 1 - k for k in range(SWEEPS))
)
PAD = 8
ROWS = 32
UNROLL = 8
SMEM = pl.BlockSpec(memory_space=pltpu.SMEM)
VMEM = pl.BlockSpec(memory_space=pltpu.VMEM)
HBM = pl.BlockSpec(memory_space=pltpu.HBM)


def odd_lanes(shift, rows, cols):
    return ((lax.broadcasted_iota(jnp.int32, (rows, cols), 1) + shift) & 1) == 1


def of_colour(colour, odd, even_rows, odd_rows):
    if colour == 0:
        return jnp.where(odd, odd_rows, even_rows)
    return jnp.where(odd, even_rows, odd_rows)


def coefficients(kappa, conductivity):
    coupling = kappa * conductivity
    inverse = 1.0 / (36.0 + coupling * coupling)
    return 6.0 * inverse, coupling * inverse


def even_side_on_right():
    return lax.axis_index("tile") % 2 == 0


def layer_of(slot, layers):
    ahead = slot - SWEEPS
    return jnp.where(even_side_on_right(), layers - 1 - ahead, ahead)


def start_all(copies):
    for copy in copies:
        copy.start()
    return copies


def pack_kernel(guess_hbm, cond_hbm, adj_ref, even_ref, odd_ref, guess_ref, cond_ref, sems):
    layers, size_y, size_z = cond_ref.shape
    half = size_y // 2
    shared = even_ref.shape[1]
    rows = min(ROWS, shared)
    first = lax.axis_index("tile") * layers
    cond_copy = pltpu.make_async_copy(cond_hbm, cond_ref, sems.at[0])
    cond_copy.start()
    guess_copies = start_all(
        [
            pltpu.make_async_copy(guess_hbm.at[0, :, i], guess_ref.at[:, i], sems.at[1 + i])
            for i in range(layers)
        ]
    )
    on_right = even_side_on_right()
    offset = lax.axis_index("src") % 2 * shared
    cond_copy.wait()
    for i, (d, c) in enumerate(HALO_CELLS):
        for ref, to_right in ((even_ref, on_right), (odd_ref, jnp.logical_not(on_right))):
            layer = jnp.where(to_right, layers - d, d - 1)
            odd = odd_lanes(first + layer, rows, size_z)
            for r in range(0, shared, rows):
                at = pl.multiple_of(2 * (offset + r), 2 * rows)
                a = cond_ref[layer, pl.ds(at, rows, stride=2), :]
                b = cond_ref[layer, pl.ds(at + 1, rows, stride=2), :]
                ref[i, pl.ds(r, rows), :] = of_colour(c, odd, a, b)
    for layer in range(layers):
        odd = odd_lanes(first + layer, rows, size_z)
        guess_copies[layer].wait()
        for part in range(2):
            for r in range(0, half, rows):
                a = guess_ref[part, layer, pl.ds(2 * r, rows, stride=2), :]
                b = guess_ref[part, layer, pl.ds(2 * r + 1, rows, stride=2), :]
                adj_ref[part, layer, pl.ds(r, rows), :] = of_colour(1, odd, a, b)


def source_kernel(
    x_hbm, y_hbm, z_hbm, kappas_hbm, freq_hbm, weight_hbm, data_hbm, cond_hbm,
    source_ref, six_ref, cross_ref, scale_ref, kappa_ref,
    x_ref, y_ref, z_ref, kappas_ref, freq_ref, weight_ref, data_ref, cond_ref,
    terms_ref, total_ref, sems,
):
    layers, size_y, size_z = cond_ref.shape
    half = size_y // 2
    rows = min(ROWS, half)
    taps, count = weight_ref.shape
    reach = source_ref.shape[2]
    halo = SWEEPS - 1
    first = lax.axis_index("tile") * layers
    copies = start_all(
        [
            pltpu.make_async_copy(a, b, sems.at[i])
            for i, (a, b) in enumerate(
                (
                    (x_hbm, x_ref), (y_hbm, y_ref), (z_hbm, z_ref), (kappas_hbm, kappas_ref),
                    (freq_hbm, freq_ref), (weight_hbm, weight_ref), (data_hbm, data_ref),
                    (cond_hbm, cond_ref),
                )
            )
        ]
    )
    for layer in range(reach):
        total_ref[4 + layer] = jnp.zeros(total_ref.shape[1:], jnp.float32)
    for copy in copies:
        copy.wait()
    kappa = kappas_ref[freq_ref[0]]
    kappa_ref[...] = jnp.full(kappa_ref.shape, kappa, jnp.float32)

    blank = jnp.zeros((size_z - taps, count), jnp.float32)
    weights = weight_ref[...]
    for c in range(2):
        terms = jnp.concatenate([weights * data_ref[0, c : c + 1, :], blank], axis=0).T
        for b in range(4):
            moved = pltpu.roll(terms, size_z - 4 * b, 1) if b else terms
            terms_ref[pl.ds(2 * b + c, count, stride=8), :] = moved

    lane = lax.broadcasted_iota(jnp.int32, (8, size_z), 1)

    def add_block(r):
        z = z_ref[r]
        base = jnp.clip(x_ref[r] - first + halo, -4, reach) + 4
        row = 2 * y_ref[r]
        inside = (lane - z).astype(jnp.uint32) < 4
        both = terms_ref[pl.ds(pl.multiple_of(8 * r, 8), 8), :]
        terms = []
        for a in range(4):
            moved = pltpu.roll(both, lax.rem(z + size_z - 16 * a, size_z), 1)
            terms.append(jnp.where(inside, moved, 0.0))
        old = [total_ref[base + a, pl.ds(row, 8), :] for a in range(4)]
        for a in range(4):
            total_ref[base + a, pl.ds(row, 8), :] = old[a] + terms[a]

    def some_blocks(step, carry):
        for u in range(UNROLL):
            add_block(step * UNROLL + u)
        return carry

    lax.fori_loop(0, count // UNROLL, some_blocks, 0)

    for ahead in range(layers):
        layer = layer_of(SWEEPS + ahead, layers)
        odd = odd_lanes(first + layer, rows, size_z)
        for r in range(0, half, rows):
            a = cond_ref[layer, pl.ds(2 * r, rows, stride=2), :]
            b = cond_ref[layer, pl.ds(2 * r + 1, rows, stride=2), :]
            for c in (0, 1):
                six, cross = coefficients(kappa, of_colour(c, odd, a, b))
                six_ref[c, ahead, pl.ds(r, rows), :] = six
                cross_ref[c, ahead, pl.ds(r, rows), :] = cross
        scale_ref[ahead] = -(kappa * cond_ref[layer])

    def pack_layer(i, carry):
        layer = layer_of(i + 1, layers)
        odd = odd_lanes(first + layer, rows, size_z)
        for part in range(2):
            for r in range(0, half, rows):
                a = total_ref[4 + halo + layer, pl.ds(4 * r + part, rows, stride=4), :]
                b = total_ref[4 + halo + layer, pl.ds(4 * r + 2 + part, rows, stride=4), :]
                for c in (0, 1):
                    source_ref[c, part, i, pl.ds(r, rows), :] = of_colour(c, odd, a, b)
        return carry

    lax.fori_loop(0, reach, pack_layer, 0)


class Sweeper:
    def __init__(self, half, size_z, layers, source, six, cross):
        self.half, self.size_z = half, size_z
        self.source, self.six, self.cross = source, six, cross
        self.where = ({}, {})
        first = lax.axis_index("tile") * layers
        self.rows = min(ROWS, half)
        base = first + jnp.where(even_side_on_right(), layers - 1, 0)
        self.odd = odd_lanes(base, self.rows, size_z)
        lane = lax.broadcasted_iota(jnp.int32, (self.rows, size_z), 1)
        self.after, self.before = lane > 0, lane < size_z - 1
        near = lax.broadcasted_iota(jnp.int32, (size_z, size_z), 0)
        near = jnp.abs(near - lax.broadcasted_iota(jnp.int32, (size_z, size_z), 1)) <= 1
        near = jnp.where(near, 1.0, 0.0).astype(jnp.bfloat16)
        self.near = jnp.concatenate([near] * 3, axis=0)

    def along_z(self, values):
        high = values.astype(jnp.bfloat16)
        rest = values - high.astype(jnp.float32)
        middle = rest.astype(jnp.bfloat16)
        low = (rest - middle.astype(jnp.float32)).astype(jnp.bfloat16)
        pieces = jnp.concatenate([high, middle, low], axis=1)
        return jnp.dot(pieces, self.near, preferred_element_type=jnp.float32)

    def sums(self, c, part, slot):
        old = self.where[1 - c]
        here, left, right = old[slot], old[slot - 1], old[slot + 1]
        rows = self.rows
        by_matrix = part == 1
        if by_matrix:
            beside = self.along_z(here[part, slot, pl.ds(PAD, self.half), :])
        out = []
        for r in range(0, self.half, rows):
            above = here[part, slot, pl.ds(PAD + r + 1, rows), :]
            below = here[part, slot, pl.ds(PAD + r - 1, rows), :]
            if (slot + c) % 2:
                above, below = below, above
            total = left[part, slot - 1, pl.ds(PAD + r, rows), :]
            total += right[part, slot + 1, pl.ds(PAD + r, rows), :]
            total += jnp.where(self.odd, above, below)
            if by_matrix:
                total += beside[r : r + rows]
            else:
                centre = here[part, slot, pl.ds(PAD + r, rows), :]
                total += centre
                total += jnp.where(self.after, pltpu.roll(centre, 1, 1), 0.0)
                total += jnp.where(self.before, pltpu.roll(centre, self.size_z - 1, 1), 0.0)
            out.append(total + self.source[c, part, slot - 1, pl.ds(r, rows), :])
        return out

    def update(self, c, slot, new):
        sums = [self.sums(c, part, slot) for part in range(2)]
        for i, r in enumerate(range(0, self.half, self.rows)):
            six = self.six[c, slot, pl.ds(r, self.rows), :]
            cross = self.cross[c, slot, pl.ds(r, self.rows), :]
            at = pl.ds(PAD + r, self.rows)
            new[0, slot, at, :] = six * sums[0][i] + cross * sums[1][i]
            new[1, slot, at, :] = six * sums[1][i] - cross * sums[0][i]
        self.where[c][slot] = new


def clear_edges(ref, slots, half):
    edge = jnp.zeros((PAD, ref.shape[-1]), jnp.float32)
    for part in range(2):
        for slot in slots:
            ref[part, slot, pl.ds(0, PAD), :] = edge
            ref[part, slot, pl.ds(PAD + half, PAD), :] = edge


def near_kernel(
    adj_ref, even_ref, ce_own_ref, co_own_ref, ce_other_ref, co_other_ref,
    source_ref, six_own_ref, cross_own_ref, kappa_ref,
    zero_ref, one_ref, six_ref, cross_ref,
):
    _, layers, half, size_z = adj_ref.shape
    tile, tiles = lax.axis_index("tile"), lax.axis_size("tile")
    on_right = even_side_on_right()
    shared = ce_own_ref.shape[1]
    rows = min(ROWS, shared)
    reached = layers + SWEEPS
    clear_edges(zero_ref, range(1, reached - 1), half)
    clear_edges(one_ref, range(reached), half)
    for part in range(2):
        for slot in range(reached):
            layer = layer_of(slot, layers)
            if slot < SWEEPS:
                values = even_ref[part, jnp.where(on_right, layer - layers, layer + SWEEPS)]
            else:
                values = adj_ref[part, layer]
            one_ref[part, slot, pl.ds(PAD, half), :] = values
    for c in (0, 1):
        for layer in range(layers):
            six_ref[c, SWEEPS + layer] = six_own_ref[c, layer]
            cross_ref[c, SWEEPS + layer] = cross_own_ref[c, layer]
    kappa = jnp.broadcast_to(kappa_ref[0:1, :], (rows, size_z))
    parity = lax.axis_index("src") % 2
    is_last, is_first = tile == tiles - 1, tile == 0
    for own, other, outer, missing in (
        (ce_own_ref, ce_other_ref, -1, jnp.where(on_right, is_last, is_first)),
        (co_own_ref, co_other_ref, 1, jnp.where(on_right, is_first, is_last)),
    ):
        there = jnp.where(missing, 0.0, 1.0)
        for i, (d, c) in enumerate(HALO_CELLS):
            slot = SWEEPS - d if outer < 0 else SWEEPS + layers - 1 + d
            for ref, start in ((own, parity * shared), (other, (1 - parity) * shared)):
                for r in range(0, shared, rows):
                    six, cross = coefficients(kappa, ref[i, pl.ds(r, rows), :])
                    at = pl.ds(pl.multiple_of(start + r, rows), rows)
                    six_ref[c, slot, at, :] = six * there
                    cross_ref[c, slot, at, :] = cross * there
    sweeper = Sweeper(half, size_z, layers, source_ref, six_ref, cross_ref)
    sweeper.where[1].update({slot: one_ref for slot in range(reached)})
    for k, c in enumerate(COLOURS):
        for slot in range(1 + k, reached - 1 - k):
            sweeper.update(c, slot, (zero_ref, one_ref)[c])


def far_kernel(
    zero_in_ref, one_in_ref, odd_ref, source_ref, six_ref, cross_ref, scale_ref, forward_ref,
    zero_ref, one_ref, send_ref, keep_ref,
):
    _, slots, _, size_z = zero_in_ref.shape
    layers, size_y, _ = scale_ref.shape
    half = size_y // 2
    on_right = even_side_on_right()
    reached = layers + SWEEPS
    clear_edges(zero_ref, range(SWEEPS, slots - 1), half)
    clear_edges(one_ref, range(SWEEPS, slots), half)
    for part in range(2):
        for slot in range(reached, slots):
            layer = layer_of(slot, layers)
            values = odd_ref[part, jnp.where(on_right, layer + SWEEPS, layer - layers)]
            one_ref[part, slot, pl.ds(PAD, half), :] = values
    sweeper = Sweeper(half, size_z, layers, source_ref, six_ref, cross_ref)
    sweeper.where[0].update({slot: zero_in_ref for slot in range(1, reached - 1)})
    sweeper.where[1].update({slot: one_in_ref for slot in range(reached)})
    sweeper.where[1].update({slot: one_ref for slot in range(reached, slots)})
    for k, c in enumerate(COLOURS):
        for slot in range(reached - 1 - k, slots - 1 - k):
            sweeper.update(c, slot, (zero_ref, one_ref)[c])
    for slot in range(SWEEPS, SWEEPS + layers):
        if sweeper.where[0][slot] is zero_in_ref:
            for part in range(2):
                zero_ref[part, slot, pl.ds(PAD, half), :] = zero_in_ref[part, slot, pl.ds(PAD, half), :]

    shards = 2 * send_ref.shape[0]
    shard = lax.axis_index("src")
    shard_rows = size_y // shards
    rows = min(ROWS, shard_rows // 2)
    for slot in range(SWEEPS, SWEEPS + layers):
        layer = layer_of(slot, layers)
        swap = odd_lanes(lax.axis_index("tile") * layers + layer, rows, size_z)
        for m in range(shards):
            ref = send_ref if m % 2 else keep_ref
            start = (shard ^ m) * shard_rows
            for r in range(0, shard_rows // 2, rows):
                at = pl.ds(pl.multiple_of(PAD + start // 2 + r, PAD), rows)
                a = [zero_ref[part, slot, at, :] for part in range(2)]
                b = [one_ref[part, slot, at, :] for part in range(2)]
                for second in range(2):
                    if second:
                        a, b = b, a
                    field = [jnp.where(swap, b[part], a[part]) for part in range(2)]
                    cells = pl.ds(pl.multiple_of(start + 2 * r, 2 * rows) + second, rows, stride=2)
                    products = forward_ref[0, 0, layer, cells, :] * field[1]
                    products += forward_ref[0, 1, layer, cells, :] * field[0]
                    into = pl.ds(2 * r + second, rows, stride=2)
                    ref[m // 2, layer, into, :] = scale_ref[slot - SWEEPS, cells, :] * products


def unpack_kernel(zero_ref, one_ref, out_hbm, out_ref, sems):
    _, layers, size_y, size_z = out_ref.shape
    half = size_y // 2
    rows = min(ROWS, half)
    first = lax.axis_index("tile") * layers
    copies = []
    for slot in range(SWEEPS, SWEEPS + layers):
        layer = layer_of(slot, layers)
        odd = odd_lanes(first + layer, rows, size_z)
        for part in range(2):
            for r in range(0, half, rows):
                a = zero_ref[part, slot, pl.ds(PAD + r, rows), :]
                b = one_ref[part, slot, pl.ds(PAD + r, rows), :]
                out_ref[part, slot - SWEEPS, pl.ds(2 * r, rows, stride=2), :] = jnp.where(odd, b, a)
                out_ref[part, slot - SWEEPS, pl.ds(2 * r + 1, rows, stride=2), :] = jnp.where(odd, a, b)
        i = slot - SWEEPS
        copies.append(
            pltpu.make_async_copy(out_ref.at[:, i], out_hbm.at[0, :, layer], sems.at[i])
        )
        copies[-1].start()
    for copy in copies:
        copy.wait()


def call(kernel, outs, scratch, specs, out_specs, flops):
    return pl.pallas_call(
        kernel,
        out_shape=[jax.ShapeDtypeStruct(s, jnp.float32) for s in outs],
        in_specs=specs,
        out_specs=out_specs,
        scratch_shapes=scratch,
        compiler_params=pltpu.CompilerParams(vmem_limit_bytes=20 << 20),
        cost_estimate=pl.CostEstimate(flops=flops, bytes_accessed=4 << 20, transcendentals=0),
    )


def floats(*shapes):
    return [pltpu.VMEM(s, jnp.float32) for s in shapes]


def swap_even(count):
    return [(i, i ^ 1) for i in range(count) if i ^ 1 < count]


def swap_odd(count):
    pairs = [(i, i + 1) for i in range(1, count - 1, 2)]
    return pairs + [(b, a) for a, b in pairs]


def body(
    forward_field,
    adjoint_guess,
    conductivity,
    freq_kappa,
    pair_freq,
    recv_data,
    recv_weights,
    recv_x,
    recv_y,
    recv_z,
):
    pairs, _, layers, size_y, size_z = adjoint_guess.shape
    half = size_y // 2
    count, taps = recv_weights.shape
    tiles = lax.axis_size("tile")
    shards = lax.axis_size("src")
    assert pairs == 1 and layers == SWEEPS and count % UNROLL == 0
    cells = len(HALO_CELLS)
    reach = layers + 2 * (SWEEPS - 1)
    slots = layers + 2 * SWEEPS
    evens, odds = swap_even(tiles), swap_odd(tiles)
    flip = [(i, i ^ 1) for i in range(shards)]

    adj, cond_even, cond_odd = call(
        pack_kernel,
        [(2, layers, half, size_z), (cells, half // 2, size_z), (cells, half // 2, size_z)],
        floats((2, layers, size_y, size_z), (layers, size_y, size_z))
        + [pltpu.SemaphoreType.DMA((1 + layers,))],
        [HBM, HBM],
        [VMEM] * 3,
        1 << 20,
    )(adjoint_guess, conductivity)

    cond_even = lax.ppermute(cond_even, "tile", evens)
    cond_odd = lax.ppermute(cond_odd, "tile", odds)
    adj_even = lax.ppermute(adj, "tile", evens)
    adj_odd = lax.ppermute(adj, "tile", odds)

    source, six_own, cross_own, scale, kappa = call(
        source_kernel,
        [
            (2, 2, reach, half, size_z),
            (2, layers, half, size_z),
            (2, layers, half, size_z),
            (layers, size_y, size_z),
            (8, size_z),
        ],
        [pltpu.SMEM((count,), jnp.int32)] * 3
        + [pltpu.SMEM(freq_kappa.shape, jnp.float32), pltpu.SMEM(pair_freq.shape, jnp.int32)]
        + floats(
            (taps, count),
            recv_data.shape,
            (layers, size_y, size_z),
            (8 * count, size_z),
            (reach + 8, 2 * size_y, size_z),
        )
        + [pltpu.SemaphoreType.DMA((8,))],
        [HBM] * 8,
        [VMEM] * 5,
        1 << 30,
    )(
        recv_x, recv_y, recv_z, freq_kappa, pair_freq, recv_weights.T, recv_data, conductivity
    )

    other_even = lax.ppermute(cond_even, "src", flip)
    other_odd = lax.ppermute(cond_odd, "src", flip)

    state = (2, slots, half + 2 * PAD, size_z)
    weights = (2, slots, half, size_z)
    zero, one, six, cross = call(
        near_kernel, [state, state, weights, weights], [], [VMEM] * 10, [VMEM] * 4, 1 << 26
    )(
        adj, adj_even, cond_even, cond_odd, other_even, other_odd,
        source, six_own, cross_own, kappa,
    )

    shard_rows = size_y // shards
    part_shape = (shards // 2, layers, shard_rows, size_z)
    zero, one, send, keep = call(
        far_kernel, [state, state, part_shape, part_shape], [], [VMEM] * 8, [VMEM] * 4, 1 << 26
    )(zero, one, adj_odd, source, six, cross, scale, forward_field)

    (field,) = call(
        unpack_kernel,
        [(1, 2, layers, size_y, size_z)],
        floats((2, layers, size_y, size_z)) + [pltpu.SemaphoreType.DMA((layers,))],
        [VMEM] * 2,
        [HBM],
        1 << 20,
    )(zero, one)

    bit = 1
    while True:
        keep = keep + lax.ppermute(send, "src", [(i, i ^ bit) for i in range(shards)])
        bit *= 2
        if bit == shards:
            break
        send, keep = keep[1::2], keep[0::2]
    return (field, keep[0])


def solution(mesh):
    placed = (
        P(("job", "src"), None, "tile", None, None),
        P(("job", "src"), None, "tile", None, None),
        P(("job", "tile"), None, None),
        P("job"),
        P(("job", "src")),
        P(("job", "src"), None, None),
        P("job", None),
        P("job"),
        P("job"),
        P("job"),
    )
    return jax.shard_map(
        body,
        mesh=mesh,
        in_specs=placed,
        out_specs=(P(("job", "src"), None, "tile", None, None), P(("job", "tile"), "src", None)),
        check_vma=False,
    )
```

time: 43.1 us -> 46 us (1.067)
  the two profiles are of different devices: /device:TPU:0 before, /device:TPU:22 now
where the time goes in v2:
time: 46 us; the launch traced here: 45.7 us
  waiting for transfers between devices  18.2 us (40%)
  Pallas kernels  10.1 us (22%)
  starting transfers between devices  8.73 us (19%)
  local copies, waits for them, and re-layouts  6.48 us (14%)
  between operations  1.43 us (3%)
  other arithmetic  0.7 us (2%)
    ppermute x1, waiting for transfers between devices, body(): cond_even = lax.ppermute(cond_even, 'tile', evens)  9.67 us
    unnamed x18, local copies, waits for them, and re-layouts  6.47 us
    pallas_call x1, Pallas kernels, body(): call(source_kernel, [(2, 2, reach, half, size_z), (2, layers, half, size_...  6.04 us
    ppermute x2, waiting for transfers between devices, body(): lax.ppermute(send, 'src', [(i, i ^ bit) for i in range(shards)])  5.38 us
    ppermute x1, starting transfers between devices, body(): cond_odd = lax.ppermute(cond_odd, 'tile', odds)  3.92 us
    ppermute x1, waiting for transfers between devices, body(): cond_odd = lax.ppermute(cond_odd, 'tile', odds)  3.17 us
    ppermute x1, starting transfers between devices, body(): adj_odd = lax.ppermute(adj, 'tile', odds)  1.91 us
    ppermute x1, starting transfers between devices, body(): adj_even = lax.ppermute(adj, 'tile', evens)  1.64 us
  transfers between devices with their start and end apart: 8, of which 4 were waited for; matrix products, arithmetic and copies ran while one was open for 0% of the time, Pallas kernels for 18%

profile of v2, /device:TPU:22, one launch (start us, length us, event | category | flops | bytes accessed | tf_op | source)
XLA Modules:
  0.0 45.7 jit_solution(1622291065468997004)
XLA Ops:
  0.6 1.2 %copy-done = f32[1,2,4,256,128]{4,3,2,1,0:T(8,128)S(1)} copy-done((f32[1,2,4,256,128]{4,3,2,1,0:T(8,128)S(1)}, f32[1,2,4,256,128]{4,3,2,1,0:T(8,128)}, u32[]{:S(2)}) %copy-start) | copy-done | bytes 1048600
  1.9 1.0 %copy-done.2 = f32[4,256,128]{2,1,0:T(8,128)S(1)} copy-done((f32[4,256,128]{2,1,0:T(8,128)S(1)}, f32[4,256,128]{2,1,0:T(8,128)}, u32[]{:S(2)}) %copy-start.2) | copy-done | bytes 524312
  2.9 0.3 shard_map.113
  3.2 1.6 %collective-permute-start = (f32[2,4,128,128]{3,2,1,0:T(8,128)S(1)}, f32[2,4,128,128]{3,2,1,0:T(8,128)S(1)}, u32[]{:S(2)}, u32[]{:S(2)}) collective-permute-start(f32[2,4,128,128]{3,2,1,0:T(8,128)S(1)} %get-tuple-element.18.adj_ref), channel_id=1, source_target_pairs={{0,4},{4,0},{8,12},{12,8},{1,5},{5,1},{9,13},{13,9},{2,6},{6,2},{1... | collective-permute-start | bytes 1572872 | tf_op jit(solution)/shard_map/ppermute | solution.py:436
  4.8 1.9 %collective-permute-start.5 = (f32[2,4,128,128]{3,2,1,0:T(8,128)S(1)}, f32[2,4,128,128]{3,2,1,0:T(8,128)S(1)}, u32[]{:S(2)}, u32[]{:S(2)}) collective-permute-start(f32[2,4,128,128]{3,2,1,0:T(8,128)S(1)} %get-tuple-element.18.adj_ref), channel_id=1, source_target_pairs={{4,8},{8,4},{5,9},{9,5},{6,10},{10,6},{7,11},{11,7},{20,24},{24,20... | collective-permute-start | bytes 1572872 | tf_op jit(solution)/shard_map/ppermute | solution.py:437
  6.7 0.1 collective-permute-start.1
  6.8 3.9 %collective-permute-start.2 = (f32[5,64,128]{2,1,0:T(8,128)S(1)}, f32[5,64,128]{2,1,0:T(8,128)S(1)}, u32[]{:S(2)}, u32[]{:S(2)}) collective-permute-start(f32[5,64,128]{2,1,0:T(8,128)S(1)} %get-tuple-element.20), channel_id=1, source_target_pairs={{4,8},{8,4},{5,9},{9,5},{6,10},{10,6},{7,11},{11,7},{20,24},{24,20... | collective-permute-start | bytes 491528 | tf_op jit(solution)/shard_map/ppermute | solution.py:435
  10.7 9.7 %collective-permute-done.1.ce_own_ref = f32[5,64,128]{2,1,0:T(8,128)S(1)} collective-permute-done((f32[5,64,128]{2,1,0:T(8,128)S(1)}, f32[5,64,128]{2,1,0:T(8,128)S(1)}, u32[]{:S(2)}, u32[]{:S(2)}) %collective-permute-start.1) | collective-permute-done | bytes 163872 | tf_op jit(solution)/shard_map/ppermute | solution.py:434
  20.4 3.2 %collective-permute-done.2.co_own_ref = f32[5,64,128]{2,1,0:T(8,128)S(1)} collective-permute-done((f32[5,64,128]{2,1,0:T(8,128)S(1)}, f32[5,64,128]{2,1,0:T(8,128)S(1)}, u32[]{:S(2)}, u32[]{:S(2)}) %collective-permute-start.2) | collective-permute-done | bytes 163872 | tf_op jit(solution)/shard_map/ppermute | solution.py:435
  24.3 0.8 %copy-done.3 = f32[256,64]{0,1:T(8,128)S(1)} copy-done((f32[256,64]{0,1:T(8,128)S(1)}, f32[256,64]{0,1:T(8,128)}, u32[]{:S(2)}) %copy-start.3) | copy-done | bytes 65560
  25.1 0.7 %copy-done.4 = f32[1,2,256]{2,1,0:T(2,128)S(1)} copy-done((f32[1,2,256]{2,1,0:T(2,128)S(1)}, f32[1,2,256]{2,1,0:T(2,128)}, u32[]{:S(2)}) %copy-start.4) | copy-done | bytes 2072
  25.8 0.7 %copy-done.5 = s32[256]{0:T(256)S(1)} copy-done((s32[256]{0:T(256)S(1)}, s32[256]{0:T(256)}, u32[]{:S(2)}) %copy-start.5) | copy-done | bytes 1048
  26.4 0.7 %copy-done.6 = s32[256]{0:T(256)S(1)} copy-done((s32[256]{0:T(256)S(1)}, s32[256]{0:T(256)}, u32[]{:S(2)}) %copy-start.6) | copy-done | bytes 1048
  27.1 0.7 %copy-done.7 = s32[256]{0:T(256)S(1)} copy-done((s32[256]{0:T(256)S(1)}, s32[256]{0:T(256)}, u32[]{:S(2)}) %copy-start.7) | copy-done | bytes 1048
  27.8 0.7 %copy-done.8 = f32[4]{0:T(128)S(1)} copy-done((f32[4]{0:T(128)S(1)}, f32[4]{0:T(128)}, u32[]{:S(2)}) %copy-start.8) | copy-done | bytes 40
  28.5 6.0 %shard_map.114 = (f32[2,2,10,128,128]{4,3,2,1,0:T(8,128)S(1)}, f32[2,4,128,128]{3,2,1,0:T(8,128)S(1)}, f32[2,4,128,128]{3,2,1,0:T(8,128)S(1)}, f32[4,256,128]{2,1,0:T(8,128)S(1)}, f32[8,128]{1,0:T(8,128)S(1)}) custom-call(s32[256]{0:T(256)S(1)} %copy-done.5, s32[256]{0:T(256)S(1)} %copy-done.6, s32[256]{0:T(256)S(1)} %copy-done.7, f32[4]{0:T(128)S(1)} %copy-done.8, ...), custom_call_target="tpu_custom_call" | custom-call | flops 1073741824 | bytes 4194304 | tf_op jit(solution)/shard_map/pallas_call | solution.py:439
  34.6 1.3 %shard_map.115 = (f32[2,12,144,128]{3,2,1,0:T(8,128)S(1)}, f32[2,12,144,128]{3,2,1,0:T(8,128)S(1)}, f32[2,12,128,128]{3,2,1,0:T(8,128)S(1)}, f32[2,12,128,128]{3,2,1,0:T(8,128)S(1)}) custom-call(f32[2,4,128,128]{3,2,1,0:T(8,128)S(1)} %get-tuple-element.18.adj_ref, f32[2,4,128,128]{3,2,1,0:T(8,128)S(1)} %collective-permute-done.even_ref, ...), custom_call_target="tpu_custom_call" | custom-call | flops 67108864 | bytes 4194304 | tf_op jit(solution)/shard_map/pallas_call | solution.py:470
  35.9 1.5 %shard_map.116 = (f32[2,12,144,128]{3,2,1,0:T(8,128)S(1)}, f32[2,12,144,128]{3,2,1,0:T(8,128)S(1)}, f32[2,4,64,128]{3,2,1,0:T(8,128)S(1)}, f32[2,4,64,128]{3,2,1,0:T(8,128)S(1)}) custom-call(f32[2,12,144,128]{3,2,1,0:T(8,128)S(1)} %get-tuple-element.25.zero_in_ref, f32[2,12,144,128]{3,2,1,0:T(8,128)S(1)} %get-tuple-element.26.one_in_ref, ...), custom_call_target="tpu_custom_call" | custom-call | flops 67108864 | bytes 4194304 | tf_op jit(solution)/shard_map/pallas_call | solution.py:479
  37.4 0.6 %collective-permute-start.6 = (f32[2,4,64,128]{3,2,1,0:T(8,128)S(1)}, f32[2,4,64,128]{3,2,1,0:T(8,128)S(1)}, u32[]{:S(2)}, u32[]{:S(2)}) collective-permute-start(f32[2,4,64,128]{3,2,1,0:T(8,128)S(1)} %get-tuple-element.33), channel_id=1, source_target_pairs={{0,1},{1,0},{2,3},{3,2},{4,5},{5,4},{6,7},{7,6},{8,9},{9,8},{10,11... | collective-permute-start | bytes 786440 | tf_op jit(solution)/shard_map/ppermute | solution.py:494
  38.0 1.2 %collective-permute-done.6 = f32[2,4,64,128]{3,2,1,0:T(8,128)S(1)} collective-permute-done((f32[2,4,64,128]{3,2,1,0:T(8,128)S(1)}, f32[2,4,64,128]{3,2,1,0:T(8,128)S(1)}, u32[]{:S(2)}, u32[]{:S(2)}) %collective-permute-start.6) | collective-permute-done | bytes 262176 | tf_op jit(solution)/shard_map/ppermute | solution.py:494
  39.2 0.6 %collective-permute-start.7 = (f32[1,4,64,128]{3,2,1,0:T(8,128)S(1)}, f32[1,4,64,128]{3,2,1,0:T(8,128)S(1)}, u32[]{:S(2)}, u32[]{:S(2)}) collective-permute-start(f32[1,4,64,128]{3,2,1,0:T(8,128)S(1)} %slice.11), channel_id=1, source_target_pairs={{0,2},{1,3},{2,0},{3,1},{4,6},{5,7},{6,4},{7,5},{8,10},{9,11},{10,... | collective-permute-start | bytes 393224 | tf_op jit(solution)/shard_map/ppermute | solution.py:494
  39.8 1.0 %shard_map.117 = f32[1,2,4,256,128]{4,3,2,1,0:T(8,128)} custom-call(f32[2,12,144,128]{3,2,1,0:T(8,128)S(1)} %get-tuple-element.30.zero_ref, f32[2,12,144,128]{3,2,1,0:T(8,128)S(1)} %get-tuple-element.31.one_ref), custom_call_target="tpu_custom_call" | custom-call | flops 1048576 | bytes 4194304 | tf_op jit(solution)/shard_map/pallas_call | solution.py:483
  40.8 4.2 %collective-permute-done.7 = f32[1,4,64,128]{3,2,1,0:T(8,128)S(1)} collective-permute-done((f32[1,4,64,128]{3,2,1,0:T(8,128)S(1)}, f32[1,4,64,128]{3,2,1,0:T(8,128)S(1)}, u32[]{:S(2)}, u32[]{:S(2)}) %collective-permute-start.7) | collective-permute-done | bytes 131104 | tf_op jit(solution)/shard_map/ppermute | solution.py:494
  45.0 0.7 %fusion = f32[4,64,128]{2,1,0:T(8,128)} fusion(f32[1,4,64,128]{3,2,1,0:T(8,128)S(1)} %collective-permute-done.7, f32[2,4,64,128]{3,2,1,0:T(8,128)S(1)} %add.6), kind=kLoop, calls=%fused_computation.1 | loop fusion | flops 32768 | bytes 393216 | tf_op jit(solution)/shard_map/squeeze | solution.py:499
  (18 shorter events, 0.1 us)
Async XLA Ops:
  0.6 1.2 %copy-start = (f32[1,2,4,256,128]{4,3,2,1,0:T(8,128)S(1)}, f32[1,2,4,256,128]{4,3,2,1,0:T(8,128)}, u32[]{:S(2)}) copy-start(f32[1,2,4,256,128]{4,3,2,1,0:T(8,128)} %guess_hbm.1) | copy-start | bytes 3145732
  1.9 1.0 %copy-start.2 = (f32[4,256,128]{2,1,0:T(8,128)S(1)}, f32[4,256,128]{2,1,0:T(8,128)}, u32[]{:S(2)}) copy-start(f32[4,256,128]{2,1,0:T(8,128)} %cond_hbm.3) | copy-start | bytes 1572868
  3.2 31.4 %collective-permute-start = (f32[2,4,128,128]{3,2,1,0:T(8,128)S(1)}, f32[2,4,128,128]{3,2,1,0:T(8,128)S(1)}, u32[]{:S(2)}, u32[]{:S(2)}) collective-permute-start(f32[2,4,128,128]{3,2,1,0:T(8,128)S(1)} %get-tuple-element.18.adj_ref), channel_id=1, source_target_pairs={{0,4},{4,0},{8,12},{12,8},{1,5},{5,1},{9,13},{13,9},{2,6},{6,2},{1... | collective-permute-start | bytes 1572872 | tf_op jit(solution)/shard_map/ppermute | solution.py:436
  4.8 31.1 %collective-permute-start.5 = (f32[2,4,128,128]{3,2,1,0:T(8,128)S(1)}, f32[2,4,128,128]{3,2,1,0:T(8,128)S(1)}, u32[]{:S(2)}, u32[]{:S(2)}) collective-permute-start(f32[2,4,128,128]{3,2,1,0:T(8,128)S(1)} %get-tuple-element.18.adj_ref), channel_id=1, source_target_pairs={{4,8},{8,4},{5,9},{9,5},{6,10},{10,6},{7,11},{11,7},{20,24},{24,20... | collective-permute-start | bytes 1572872 | tf_op jit(solution)/shard_map/ppermute | solution.py:437
  6.7 13.7 %collective-permute-start.1 = (f32[5,64,128]{2,1,0:T(8,128)S(1)}, f32[5,64,128]{2,1,0:T(8,128)S(1)}, u32[]{:S(2)}, u32[]{:S(2)}) collective-permute-start(f32[5,64,128]{2,1,0:T(8,128)S(1)} %get-tuple-element.19), channel_id=1, source_target_pairs={{0,4},{4,0},{8,12},{12,8},{1,5},{5,1},{9,13},{13,9},{2,6},{6,2},{1... | collective-permute-start | bytes 491528 | tf_op jit(solution)/shard_map/ppermute | solution.py:434
  6.8 16.8 %collective-permute-start.2 = (f32[5,64,128]{2,1,0:T(8,128)S(1)}, f32[5,64,128]{2,1,0:T(8,128)S(1)}, u32[]{:S(2)}, u32[]{:S(2)}) collective-permute-start(f32[5,64,128]{2,1,0:T(8,128)S(1)} %get-tuple-element.20), channel_id=1, source_target_pairs={{4,8},{8,4},{5,9},{9,5},{6,10},{10,6},{7,11},{11,7},{20,24},{24,20... | collective-permute-start | bytes 491528 | tf_op jit(solution)/shard_map/ppermute | solution.py:435
  20.4 14.1 %collective-permute-start.3 = (f32[5,64,128]{2,1,0:T(8,128)S(1)}, f32[5,64,128]{2,1,0:T(8,128)S(1)}, u32[]{:S(2)}, u32[]{:S(2)}) collective-permute-start(f32[5,64,128]{2,1,0:T(8,128)S(1)} %collective-permute-done.1.ce_own_ref), channel_id=1, source_target_pairs={{0,1},{1,0},{2,3},{3,2},{4,5},{5,4},{6,7},{7,6},{8,9},{9,8},{10,11... | collective-permute-start | bytes 491528 | tf_op jit(solution)/shard_map/ppermute | solution.py:465
  23.6 10.9 %collective-permute-start.4 = (f32[5,64,128]{2,1,0:T(8,128)S(1)}, f32[5,64,128]{2,1,0:T(8,128)S(1)}, u32[]{:S(2)}, u32[]{:S(2)}) collective-permute-start(f32[5,64,128]{2,1,0:T(8,128)S(1)} %collective-permute-done.2.co_own_ref), channel_id=1, source_target_pairs={{0,1},{1,0},{2,3},{3,2},{4,5},{5,4},{6,7},{7,6},{8,9},{9,8},{10,11... | collective-permute-start | bytes 491528 | tf_op jit(solution)/shard_map/ppermute | solution.py:466
  24.2 0.8 %copy-start.3 = (f32[256,64]{0,1:T(8,128)S(1)}, f32[256,64]{0,1:T(8,128)}, u32[]{:S(2)}) copy-start(f32[256,64]{0,1:T(8,128)} %param.16) | copy-start | bytes 196612
  25.1 0.7 %copy-start.4 = (f32[1,2,256]{2,1,0:T(2,128)S(1)}, f32[1,2,256]{2,1,0:T(2,128)}, u32[]{:S(2)}) copy-start(f32[1,2,256]{2,1,0:T(2,128)} %data_hbm.1) | copy-start | bytes 6148
  25.8 0.7 %copy-start.5 = (s32[256]{0:T(256)S(1)}, s32[256]{0:T(256)}, u32[]{:S(2)}) copy-start(s32[256]{0:T(256)} %x_hbm.1) | copy-start | bytes 3076
  26.4 0.7 %copy-start.6 = (s32[256]{0:T(256)S(1)}, s32[256]{0:T(256)}, u32[]{:S(2)}) copy-start(s32[256]{0:T(256)} %y_hbm.1) | copy-start | bytes 3076
  27.1 0.7 %copy-start.7 = (s32[256]{0:T(256)S(1)}, s32[256]{0:T(256)}, u32[]{:S(2)}) copy-start(s32[256]{0:T(256)} %z_hbm.1) | copy-start | bytes 3076
  27.8 0.7 %copy-start.8 = (f32[4]{0:T(128)S(1)}, f32[4]{0:T(128)}, u32[]{:S(2)}) copy-start(f32[4]{0:T(128)} %kappas_hbm.1) | copy-start | bytes 52
  34.5 1.3 %copy-start.1 = (f32[1,2,4,256,128]{4,3,2,1,0:T(8,128)S(1)}, f32[1,2,4,256,128]{4,3,2,1,0:T(8,128)}, u32[]{:S(2)}) copy-start(f32[1,2,4,256,128]{4,3,2,1,0:T(8,128)} %forward_ref.1) | copy-start | bytes 3145732
  37.4 1.7 %collective-permute-start.6 = (f32[2,4,64,128]{3,2,1,0:T(8,128)S(1)}, f32[2,4,64,128]{3,2,1,0:T(8,128)S(1)}, u32[]{:S(2)}, u32[]{:S(2)}) collective-permute-start(f32[2,4,64,128]{3,2,1,0:T(8,128)S(1)} %get-tuple-element.33), channel_id=1, source_target_pairs={{0,1},{1,0},{2,3},{3,2},{4,5},{5,4},{6,7},{7,6},{8,9},{9,8},{10,11... | collective-permute-start | bytes 786440 | tf_op jit(solution)/shard_map/ppermute | solution.py:494
  39.2 5.8 %collective-permute-start.7 = (f32[1,4,64,128]{3,2,1,0:T(8,128)S(1)}, f32[1,4,64,128]{3,2,1,0:T(8,128)S(1)}, u32[]{:S(2)}, u32[]{:S(2)}) collective-permute-start(f32[1,4,64,128]{3,2,1,0:T(8,128)S(1)} %slice.11), channel_id=1, source_target_pairs={{0,2},{1,3},{2,0},{3,1},{4,6},{5,7},{6,4},{7,5},{8,10},{9,11},{10,... | collective-permute-start | bytes 393224 | tf_op jit(solution)/shard_map/ppermute | solution.py:494

commit v3 on v2

--- a/solution.py
+++ b/solution.py
@@ -53,11 +53,10 @@
     return copies
 
 
-def pack_kernel(guess_hbm, cond_hbm, adj_ref, even_ref, odd_ref, guess_ref, cond_ref, sems):
+def pack_kernel(guess_hbm, cond_hbm, adj_ref, cells_ref, guess_ref, cond_ref, sems):
     layers, size_y, size_z = cond_ref.shape
     half = size_y // 2
-    shared = even_ref.shape[1]
-    rows = min(ROWS, shared)
+    rows = min(ROWS, half)
     first = lax.axis_index("tile") * layers
     cond_copy = pltpu.make_async_copy(cond_hbm, cond_ref, sems.at[0])
     cond_copy.start()
@@ -67,18 +66,15 @@
             for i in range(layers)
         ]
     )
-    on_right = even_side_on_right()
-    offset = lax.axis_index("src") % 2 * shared
+    to_right = even_side_on_right() == (lax.axis_index("src") % 2 == 0)
     cond_copy.wait()
     for i, (d, c) in enumerate(HALO_CELLS):
-        for ref, to_right in ((even_ref, on_right), (odd_ref, jnp.logical_not(on_right))):
-            layer = jnp.where(to_right, layers - d, d - 1)
-            odd = odd_lanes(first + layer, rows, size_z)
-            for r in range(0, shared, rows):
-                at = pl.multiple_of(2 * (offset + r), 2 * rows)
-                a = cond_ref[layer, pl.ds(at, rows, stride=2), :]
-                b = cond_ref[layer, pl.ds(at + 1, rows, stride=2), :]
-                ref[i, pl.ds(r, rows), :] = of_colour(c, odd, a, b)
+        layer = jnp.where(to_right, layers - d, d - 1)
+        odd = odd_lanes(first + layer, rows, size_z)
+        for r in range(0, half, rows):
+            a = cond_ref[layer, pl.ds(2 * r, rows, stride=2), :]
+            b = cond_ref[layer, pl.ds(2 * r + 1, rows, stride=2), :]
+            cells_ref[i, pl.ds(r, rows), :] = of_colour(c, odd, a, b)
     for layer in range(layers):
         odd = odd_lanes(first + layer, rows, size_z)
         guess_copies[layer].wait()
@@ -90,9 +86,9 @@
 
 
 def source_kernel(
-    x_hbm, y_hbm, z_hbm, kappas_hbm, freq_hbm, weight_hbm, data_hbm, cond_hbm,
+    x_hbm, y_hbm, z_hbm, kappas_hbm, freq_ref, weight_hbm, data_hbm, cond_hbm,
     source_ref, six_ref, cross_ref, scale_ref, kappa_ref,
-    x_ref, y_ref, z_ref, kappas_ref, freq_ref, weight_ref, data_ref, cond_ref,
+    x_ref, y_ref, z_ref, kappas_ref, weight_ref, data_ref, cond_ref,
     terms_ref, total_ref, sems,
 ):
     layers, size_y, size_z = cond_ref.shape
@@ -108,7 +104,7 @@
             for i, (a, b) in enumerate(
                 (
                     (x_hbm, x_ref), (y_hbm, y_ref), (z_hbm, z_ref), (kappas_hbm, kappas_ref),
-                    (freq_hbm, freq_ref), (weight_hbm, weight_ref), (data_hbm, data_ref),
+                    (weight_hbm, weight_ref), (data_hbm, data_ref),
                     (cond_hbm, cond_ref),
                 )
             )
@@ -248,15 +244,14 @@
 
 
 def near_kernel(
-    adj_ref, even_ref, ce_own_ref, co_own_ref, ce_other_ref, co_other_ref,
+    adj_ref, even_ref, cells_ref, other_cells_ref,
     source_ref, six_own_ref, cross_own_ref, kappa_ref,
     zero_ref, one_ref, six_ref, cross_ref,
 ):
     _, layers, half, size_z = adj_ref.shape
     tile, tiles = lax.axis_index("tile"), lax.axis_size("tile")
     on_right = even_side_on_right()
-    shared = ce_own_ref.shape[1]
-    rows = min(ROWS, shared)
+    rows = min(ROWS, half)
     reached = layers + SWEEPS
     clear_edges(zero_ref, range(1, reached - 1), half)
     clear_edges(one_ref, range(reached), half)
@@ -274,20 +269,15 @@
             cross_ref[c, SWEEPS + layer] = cross_own_ref[c, layer]
     kappa = jnp.broadcast_to(kappa_ref[0:1, :], (rows, size_z))
     parity = lax.axis_index("src") % 2
-    is_last, is_first = tile == tiles - 1, tile == 0
-    for own, other, outer, missing in (
-        (ce_own_ref, ce_other_ref, -1, jnp.where(on_right, is_last, is_first)),
-        (co_own_ref, co_other_ref, 1, jnp.where(on_right, is_first, is_last)),
-    ):
+    for ref, even_side in ((cells_ref, parity == 0), (other_cells_ref, parity == 1)):
+        missing = jnp.where(on_right == even_side, tile == tiles - 1, tile == 0)
         there = jnp.where(missing, 0.0, 1.0)
         for i, (d, c) in enumerate(HALO_CELLS):
-            slot = SWEEPS - d if outer < 0 else SWEEPS + layers - 1 + d
-            for ref, start in ((own, parity * shared), (other, (1 - parity) * shared)):
-                for r in range(0, shared, rows):
-                    six, cross = coefficients(kappa, ref[i, pl.ds(r, rows), :])
-                    at = pl.ds(pl.multiple_of(start + r, rows), rows)
-                    six_ref[c, slot, at, :] = six * there
-                    cross_ref[c, slot, at, :] = cross * there
+            slot = jnp.where(even_side, SWEEPS - d, SWEEPS + layers - 1 + d)
+            for r in range(0, half, rows):
+                six, cross = coefficients(kappa, ref[i, pl.ds(r, rows), :])
+                six_ref[c, slot, pl.ds(r, rows), :] = six * there
+                cross_ref[c, slot, pl.ds(r, rows), :] = cross * there
     sweeper = Sweeper(half, size_z, layers, source_ref, six_ref, cross_ref)
     sweeper.where[1].update({slot: one_ref for slot in range(reached)})
     for k, c in enumerate(COLOURS):
@@ -372,16 +362,20 @@
         copy.wait()
 
 
-def call(kernel, outs, scratch, specs, out_specs, flops):
+def call(kernel, outs, scratch, specs, out_specs, flops, room=20):
     return pl.pallas_call(
         kernel,
         out_shape=[jax.ShapeDtypeStruct(s, jnp.float32) for s in outs],
         in_specs=specs,
         out_specs=out_specs,
         scratch_shapes=scratch,
-        compiler_params=pltpu.CompilerParams(vmem_limit_bytes=20 << 20),
+        compiler_params=pltpu.CompilerParams(vmem_limit_bytes=room << 20),
         cost_estimate=pl.CostEstimate(flops=flops, bytes_accessed=4 << 20, transcendentals=0),
     )
+
+
+def in_hbm(array):
+    return pltpu.with_memory_space_constraint(array, pltpu.HBM)
 
 
 def floats(*shapes):
@@ -421,20 +415,25 @@
     evens, odds = swap_even(tiles), swap_odd(tiles)
     flip = [(i, i ^ 1) for i in range(shards)]
 
-    adj, cond_even, cond_odd = call(
+    adj, cond_cells = call(
         pack_kernel,
-        [(2, layers, half, size_z), (cells, half // 2, size_z), (cells, half // 2, size_z)],
+        [(2, layers, half, size_z), (cells, half, size_z)],
         floats((2, layers, size_y, size_z), (layers, size_y, size_z))
         + [pltpu.SemaphoreType.DMA((1 + layers,))],
         [HBM, HBM],
-        [VMEM] * 3,
+        [VMEM] * 2,
         1 << 20,
-    )(adjoint_guess, conductivity)
-
-    cond_even = lax.ppermute(cond_even, "tile", evens)
-    cond_odd = lax.ppermute(cond_odd, "tile", odds)
+        room=20,
+    )(in_hbm(adjoint_guess), in_hbm(conductivity))
+
+    mixed = [
+        (a * shards + s, b * shards + s)
+        for s in range(shards)
+        for a, b in (odds if s % 2 else evens)
+    ]
+    cond_cells = lax.ppermute(cond_cells, ("tile", "src"), mixed)
+    adj_odd = lax.ppermute(adj, "tile", odds)
     adj_even = lax.ppermute(adj, "tile", evens)
-    adj_odd = lax.ppermute(adj, "tile", odds)
 
     source, six_own, cross_own, scale, kappa = call(
         source_kernel,
@@ -446,7 +445,7 @@
             (8, size_z),
         ],
         [pltpu.SMEM((count,), jnp.int32)] * 3
-        + [pltpu.SMEM(freq_kappa.shape, jnp.float32), pltpu.SMEM(pair_freq.shape, jnp.int32)]
+        + [pltpu.SMEM(freq_kappa.shape, jnp.float32)]
         + floats(
             (taps, count),
             recv_data.shape,
@@ -454,24 +453,24 @@
             (8 * count, size_z),
             (reach + 8, 2 * size_y, size_z),
         )
-        + [pltpu.SemaphoreType.DMA((8,))],
-        [HBM] * 8,
+        + [pltpu.SemaphoreType.DMA((7,))],
+        [HBM] * 4 + [SMEM] + [HBM] * 3,
         [VMEM] * 5,
         1 << 30,
+        room=20,
     )(
-        recv_x, recv_y, recv_z, freq_kappa, pair_freq, recv_weights.T, recv_data, conductivity
-    )
-
-    other_even = lax.ppermute(cond_even, "src", flip)
-    other_odd = lax.ppermute(cond_odd, "src", flip)
+        in_hbm(recv_x), in_hbm(recv_y), in_hbm(recv_z), in_hbm(freq_kappa), pair_freq,
+        in_hbm(recv_weights.T), in_hbm(recv_data), in_hbm(conductivity),
+    )
+
+    other_cells = lax.ppermute(cond_cells, "src", flip)
 
     state = (2, slots, half + 2 * PAD, size_z)
     weights = (2, slots, half, size_z)
     zero, one, six, cross = call(
-        near_kernel, [state, state, weights, weights], [], [VMEM] * 10, [VMEM] * 4, 1 << 26
+        near_kernel, [state, state, weights, weights], [], [VMEM] * 8, [VMEM] * 4, 1 << 26
     )(
-        adj, adj_even, cond_even, cond_odd, other_even, other_odd,
-        source, six_own, cross_own, kappa,
+        adj, adj_even, cond_cells, other_cells, source, six_own, cross_own, kappa
     )
 
     shard_rows = size_y // shards

time: 46 us -> 34.5 us (0.75)
  the two profiles are of different devices: /device:TPU:22 before, /device:TPU:0 now
where the time goes in v3:
time: 34.5 us; the launch traced here: 34.3 us
  waiting for transfers between devices  12.6 us (37%)
  Pallas kernels  11.8 us (34%)
  starting transfers between devices  7.8 us (23%)
  between operations  1.37 us (4%)
  other arithmetic  0.7 us (2%)
    ppermute x1, waiting for transfers between devices, body(): cond_cells = lax.ppermute(cond_cells, ('tile', 'src'), mixed)  7.24 us
    pallas_call x1, Pallas kernels, body(): call(source_kernel, [(2, 2, reach, half, size_z), (2, layers, half, size_...  6.55 us
    ppermute x1, starting transfers between devices, body(): cond_cells = lax.ppermute(cond_cells, ('tile', 'src'), mixed)  4.96 us
    ppermute x2, waiting for transfers between devices, body(): lax.ppermute(send, 'src', [(i, i ^ bit) for i in range(shards)])  4.29 us
    ppermute x2, starting transfers between devices, body(): lax.ppermute(send, 'src', [(i, i ^ bit) for i in range(shards)])  2.07 us
    pallas_call x1, Pallas kernels, body(): call(far_kernel, [state, state, part_shape, part_shape], [], [VMEM] * 8,...  1.49 us
    pallas_call x1, Pallas kernels, body(): call(pack_kernel, [(2, layers, half, size_z), (cells, half, size_z)], flo...  1.41 us
    pallas_call x1, Pallas kernels, body(): call(near_kernel, [state, state, weights, weights], [], [VMEM] * 8, [VMEM...  1.32 us
  transfers between devices with their start and end apart: 6, of which 4 were waited for; matrix products, arithmetic and copies ran while one was open for 0% of the time, Pallas kernels for 26%

profile of v3, /device:TPU:0, one launch (start us, length us, event | category | flops | bytes accessed | tf_op | source)
XLA Modules:
  0.0 34.3 jit_solution(14478234331315017082)
XLA Ops:
  0.6 1.4 %shard_map.113 = (f32[2,4,128,128]{3,2,1,0:T(8,128)S(1)}, f32[5,128,128]{2,1,0:T(8,128)S(1)}) custom-call(f32[1,2,4,256,128]{4,3,2,1,0:T(8,128)} %guess_hbm.1, f32[4,256,128]{2,1,0:T(8,128)} %cond_hbm.3), custom_call_target="tpu_custom_call" | custom-call | flops 1048576 | bytes 4194304 | tf_op jit(solution)/shard_map/pallas_call | solution.py:418
  2.0 5.0 %collective-permute-start.1 = (f32[5,128,128]{2,1,0:T(8,128)S(1)}, f32[5,128,128]{2,1,0:T(8,128)S(1)}, u32[]{:S(2)}, u32[]{:S(2)}) collective-permute-start(f32[5,128,128]{2,1,0:T(8,128)S(1)} %get-tuple-element.18), channel_id=1, source_target_pairs={{0,4},{4,0},{8,12},{12,8},{5,9},{9,5},{2,6},{6,2},{10,14},{14,10},... | collective-permute-start | bytes 983048 | tf_op jit(solution)/shard_map/ppermute | solution.py:434
  7.0 0.1 collective-permute-start
  7.1 0.7 %collective-permute-start.3 = (f32[2,4,128,128]{3,2,1,0:T(8,128)S(1)}, f32[2,4,128,128]{3,2,1,0:T(8,128)S(1)}, u32[]{:S(2)}, u32[]{:S(2)}) collective-permute-start(f32[2,4,128,128]{3,2,1,0:T(8,128)S(1)} %get-tuple-element.17.adj_ref), channel_id=1, source_target_pairs={{4,8},{8,4},{5,9},{9,5},{6,10},{10,6},{7,11},{11,7},{20,24},{24,20... | collective-permute-start | bytes 1572872 | tf_op jit(solution)/shard_map/ppermute | solution.py:435
  7.8 7.2 %collective-permute-done.1.cells_ref = f32[5,128,128]{2,1,0:T(8,128)S(1)} collective-permute-done((f32[5,128,128]{2,1,0:T(8,128)S(1)}, f32[5,128,128]{2,1,0:T(8,128)S(1)}, u32[]{:S(2)}, u32[]{:S(2)}) %collective-permute-start.1) | collective-permute-done | bytes 327712 | tf_op jit(solution)/shard_map/ppermute | solution.py:434
  15.0 0.0 collective-permute-start.2
  15.7 6.5 %shard_map.114 = (f32[2,2,10,128,128]{4,3,2,1,0:T(8,128)S(1)}, f32[2,4,128,128]{3,2,1,0:T(8,128)S(1)}, f32[2,4,128,128]{3,2,1,0:T(8,128)S(1)}, f32[4,256,128]{2,1,0:T(8,128)S(1)}, f32[8,128]{1,0:T(8,128)S(1)}) custom-call(s32[256]{0:T(256)} %x_hbm.1, s32[256]{0:T(256)} %y_hbm.1, s32[256]{0:T(256)} %z_hbm.1, f32[4]{0:T(128)} %kappas_hbm.1, ...), custom_call_target="tpu_custom_call" | custom-call | flops 1073741824 | bytes 4194304 | tf_op jit(solution)/shard_map/pallas_call | solution.py:438
  22.2 1.0 %collective-permute-done.even_ref = f32[2,4,128,128]{3,2,1,0:T(8,128)S(1)} collective-permute-done((f32[2,4,128,128]{3,2,1,0:T(8,128)S(1)}, f32[2,4,128,128]{3,2,1,0:T(8,128)S(1)}, u32[]{:S(2)}, u32[]{:S(2)}) %collective-permute-start) | collective-permute-done | bytes 524320 | tf_op jit(solution)/shard_map/ppermute | solution.py:436
  23.3 0.0 collective-permute-done.2.other_cells_ref
  23.3 0.0 copy-start
  23.3 1.3 %shard_map.115 = (f32[2,12,144,128]{3,2,1,0:T(8,128)S(1)}, f32[2,12,144,128]{3,2,1,0:T(8,128)S(1)}, f32[2,12,128,128]{3,2,1,0:T(8,128)S(1)}, f32[2,12,128,128]{3,2,1,0:T(8,128)S(1)}) custom-call(f32[2,4,128,128]{3,2,1,0:T(8,128)S(1)} %get-tuple-element.17.adj_ref, f32[2,4,128,128]{3,2,1,0:T(8,128)S(1)} %collective-permute-done.even_ref, ...), custom_call_target="tpu_custom_call" | custom-call | flops 67108864 | bytes 4194304 | tf_op jit(solution)/shard_map/pallas_call | solution.py:470
  24.6 0.0 collective-permute-done.3.odd_ref
  24.6 0.0 copy-done
  24.6 1.5 %shard_map.116 = (f32[2,12,144,128]{3,2,1,0:T(8,128)S(1)}, f32[2,12,144,128]{3,2,1,0:T(8,128)S(1)}, f32[2,4,64,128]{3,2,1,0:T(8,128)S(1)}, f32[2,4,64,128]{3,2,1,0:T(8,128)S(1)}) custom-call(f32[2,12,144,128]{3,2,1,0:T(8,128)S(1)} %get-tuple-element.23.zero_in_ref, f32[2,12,144,128]{3,2,1,0:T(8,128)S(1)} %get-tuple-element.24.one_in_ref, ...), custom_call_target="tpu_custom_call" | custom-call | flops 67108864 | bytes 4194304 | tf_op jit(solution)/shard_map/pallas_call | solution.py:478
  26.1 0.1 collective-permute-start.4
  26.2 1.5 %collective-permute-done.4 = f32[2,4,64,128]{3,2,1,0:T(8,128)S(1)} collective-permute-done((f32[2,4,64,128]{3,2,1,0:T(8,128)S(1)}, f32[2,4,64,128]{3,2,1,0:T(8,128)S(1)}, u32[]{:S(2)}, u32[]{:S(2)}) %collective-permute-start.4) | collective-permute-done | bytes 262176 | tf_op jit(solution)/shard_map/ppermute | solution.py:493
  27.8 2.0 %collective-permute-start.5 = (f32[1,4,64,128]{3,2,1,0:T(8,128)S(1)}, f32[1,4,64,128]{3,2,1,0:T(8,128)S(1)}, u32[]{:S(2)}, u32[]{:S(2)}) collective-permute-start(f32[1,4,64,128]{3,2,1,0:T(8,128)S(1)} %slice.11), channel_id=1, source_target_pairs={{0,2},{1,3},{2,0},{3,1},{4,6},{5,7},{6,4},{7,5},{8,10},{9,11},{10,... | collective-permute-start | bytes 393224 | tf_op jit(solution)/shard_map/ppermute | solution.py:493
  29.8 1.0 %shard_map.117 = f32[1,2,4,256,128]{4,3,2,1,0:T(8,128)} custom-call(f32[2,12,144,128]{3,2,1,0:T(8,128)S(1)} %get-tuple-element.28.zero_ref, f32[2,12,144,128]{3,2,1,0:T(8,128)S(1)} %get-tuple-element.29.one_ref), custom_call_target="tpu_custom_call" | custom-call | flops 1048576 | bytes 4194304 | tf_op jit(solution)/shard_map/pallas_call | solution.py:482
  30.8 2.8 %collective-permute-done.5 = f32[1,4,64,128]{3,2,1,0:T(8,128)S(1)} collective-permute-done((f32[1,4,64,128]{3,2,1,0:T(8,128)S(1)}, f32[1,4,64,128]{3,2,1,0:T(8,128)S(1)}, u32[]{:S(2)}, u32[]{:S(2)}) %collective-permute-start.5) | collective-permute-done | bytes 131104 | tf_op jit(solution)/shard_map/ppermute | solution.py:493
  33.6 0.7 %fusion = f32[4,64,128]{2,1,0:T(8,128)} fusion(f32[1,4,64,128]{3,2,1,0:T(8,128)S(1)} %collective-permute-done.5, f32[2,4,64,128]{3,2,1,0:T(8,128)S(1)} %add.6), kind=kLoop, calls=%fused_computation.1 | loop fusion | flops 32768 | bytes 393216 | tf_op jit(solution)/shard_map/squeeze | solution.py:498
  (2 shorter events, 0.0 us)
Async XLA Ops:
  2.0 13.0 %collective-permute-start.1 = (f32[5,128,128]{2,1,0:T(8,128)S(1)}, f32[5,128,128]{2,1,0:T(8,128)S(1)}, u32[]{:S(2)}, u32[]{:S(2)}) collective-permute-start(f32[5,128,128]{2,1,0:T(8,128)S(1)} %get-tuple-element.18), channel_id=1, source_target_pairs={{0,4},{4,0},{8,12},{12,8},{5,9},{9,5},{2,6},{6,2},{10,14},{14,10},... | collective-permute-start | bytes 983048 | tf_op jit(solution)/shard_map/ppermute | solution.py:434
  7.0 16.3 %collective-permute-start = (f32[2,4,128,128]{3,2,1,0:T(8,128)S(1)}, f32[2,4,128,128]{3,2,1,0:T(8,128)S(1)}, u32[]{:S(2)}, u32[]{:S(2)}) collective-permute-start(f32[2,4,128,128]{3,2,1,0:T(8,128)S(1)} %get-tuple-element.17.adj_ref), channel_id=1, source_target_pairs={{0,4},{4,0},{8,12},{12,8},{1,5},{5,1},{9,13},{13,9},{2,6},{6,2},{1... | collective-permute-start | bytes 1572872 | tf_op jit(solution)/shard_map/ppermute | solution.py:436
  7.1 17.5 %collective-permute-start.3 = (f32[2,4,128,128]{3,2,1,0:T(8,128)S(1)}, f32[2,4,128,128]{3,2,1,0:T(8,128)S(1)}, u32[]{:S(2)}, u32[]{:S(2)}) collective-permute-start(f32[2,4,128,128]{3,2,1,0:T(8,128)S(1)} %get-tuple-element.17.adj_ref), channel_id=1, source_target_pairs={{4,8},{8,4},{5,9},{9,5},{6,10},{10,6},{7,11},{11,7},{20,24},{24,20... | collective-permute-start | bytes 1572872 | tf_op jit(solution)/shard_map/ppermute | solution.py:435
  15.0 8.3 %collective-permute-start.2 = (f32[5,128,128]{2,1,0:T(8,128)S(1)}, f32[5,128,128]{2,1,0:T(8,128)S(1)}, u32[]{:S(2)}, u32[]{:S(2)}) collective-permute-start(f32[5,128,128]{2,1,0:T(8,128)S(1)} %collective-permute-done.1.cells_ref), channel_id=1, source_target_pairs={{0,1},{1,0},{2,3},{3,2},{4,5},{5,4},{6,7},{7,6},{8,9},{9,8},{10,11... | collective-permute-start | bytes 983048 | tf_op jit(solution)/shard_map/ppermute | solution.py:466
  23.3 1.3 %copy-start = (f32[1,2,4,256,128]{4,3,2,1,0:T(8,128)S(1)}, f32[1,2,4,256,128]{4,3,2,1,0:T(8,128)}, u32[]{:S(2)}) copy-start(f32[1,2,4,256,128]{4,3,2,1,0:T(8,128)} %forward_ref.1) | copy-start | bytes 3145732
  26.1 1.6 %collective-permute-start.4 = (f32[2,4,64,128]{3,2,1,0:T(8,128)S(1)}, f32[2,4,64,128]{3,2,1,0:T(8,128)S(1)}, u32[]{:S(2)}, u32[]{:S(2)}) collective-permute-start(f32[2,4,64,128]{3,2,1,0:T(8,128)S(1)} %get-tuple-element.31), channel_id=1, source_target_pairs={{0,1},{1,0},{2,3},{3,2},{4,5},{5,4},{6,7},{7,6},{8,9},{9,8},{10,11... | collective-permute-start | bytes 786440 | tf_op jit(solution)/shard_map/ppermute | solution.py:493
  27.8 5.8 %collective-permute-start.5 = (f32[1,4,64,128]{3,2,1,0:T(8,128)S(1)}, f32[1,4,64,128]{3,2,1,0:T(8,128)S(1)}, u32[]{:S(2)}, u32[]{:S(2)}) collective-permute-start(f32[1,4,64,128]{3,2,1,0:T(8,128)S(1)} %slice.11), channel_id=1, source_target_pairs={{0,2},{1,3},{2,0},{3,1},{4,6},{5,7},{6,4},{7,5},{8,10},{9,11},{10,... | collective-permute-start | bytes 393224 | tf_op jit(solution)/shard_map/ppermute | solution.py:493

commit v4 on v3

--- a/solution.py
+++ b/solution.py
@@ -38,13 +38,21 @@
     return 6.0 * inverse, coupling * inverse
 
 
-def even_side_on_right():
-    return lax.axis_index("tile") % 2 == 0
+def is_odd(shard):
+    return shard % 2 == 1
+
+
+def is_even(shard):
+    return shard % 2 == 0
+
+
+def near_on_right():
+    return (lax.axis_index("tile") % 2 == 0) == is_odd(lax.axis_index("src"))
 
 
 def layer_of(slot, layers):
     ahead = slot - SWEEPS
-    return jnp.where(even_side_on_right(), layers - 1 - ahead, ahead)
+    return jnp.where(near_on_right(), layers - 1 - ahead, ahead)
 
 
 def start_all(copies):
@@ -66,7 +74,7 @@
             for i in range(layers)
         ]
     )
-    to_right = even_side_on_right() == (lax.axis_index("src") % 2 == 0)
+    to_right = jnp.logical_not(near_on_right())
     cond_copy.wait()
     for i, (d, c) in enumerate(HALO_CELLS):
         layer = jnp.where(to_right, layers - d, d - 1)
@@ -181,7 +189,7 @@
         self.where = ({}, {})
         first = lax.axis_index("tile") * layers
         self.rows = min(ROWS, half)
-        base = first + jnp.where(even_side_on_right(), layers - 1, 0)
+        base = first + jnp.where(near_on_right(), layers - 1, 0)
         self.odd = odd_lanes(base, self.rows, size_z)
         lane = lax.broadcasted_iota(jnp.int32, (self.rows, size_z), 1)
         self.after, self.before = lane > 0, lane < size_z - 1
@@ -244,22 +252,24 @@
 
 
 def near_kernel(
-    adj_ref, even_ref, cells_ref, other_cells_ref,
+    adj_ref, halo_ref, far_cells_ref, near_cells_ref,
     source_ref, six_own_ref, cross_own_ref, kappa_ref,
     zero_ref, one_ref, six_ref, cross_ref,
 ):
     _, layers, half, size_z = adj_ref.shape
     tile, tiles = lax.axis_index("tile"), lax.axis_size("tile")
-    on_right = even_side_on_right()
+    on_right = near_on_right()
     rows = min(ROWS, half)
     reached = layers + SWEEPS
+    is_last, is_first = tile == tiles - 1, tile == 0
     clear_edges(zero_ref, range(1, reached - 1), half)
     clear_edges(one_ref, range(reached), half)
     for part in range(2):
         for slot in range(reached):
             layer = layer_of(slot, layers)
             if slot < SWEEPS:
-                values = even_ref[part, jnp.where(on_right, layer - layers, layer + SWEEPS)]
+                values = halo_ref[part, jnp.where(on_right, layer - layers, layer + SWEEPS)]
+                values = jnp.where(jnp.where(on_right, is_last, is_first), 0.0, values)
             else:
                 values = adj_ref[part, layer]
             one_ref[part, slot, pl.ds(PAD, half), :] = values
@@ -268,12 +278,13 @@
             six_ref[c, SWEEPS + layer] = six_own_ref[c, layer]
             cross_ref[c, SWEEPS + layer] = cross_own_ref[c, layer]
     kappa = jnp.broadcast_to(kappa_ref[0:1, :], (rows, size_z))
-    parity = lax.axis_index("src") % 2
-    for ref, even_side in ((cells_ref, parity == 0), (other_cells_ref, parity == 1)):
-        missing = jnp.where(on_right == even_side, tile == tiles - 1, tile == 0)
+    for ref, is_near in ((near_cells_ref, True), (far_cells_ref, False)):
+        missing = jnp.where(on_right, is_last, is_first)
+        if not is_near:
+            missing = jnp.where(on_right, is_first, is_last)
         there = jnp.where(missing, 0.0, 1.0)
         for i, (d, c) in enumerate(HALO_CELLS):
-            slot = jnp.where(even_side, SWEEPS - d, SWEEPS + layers - 1 + d)
+            slot = SWEEPS - d if is_near else SWEEPS + layers - 1 + d
             for r in range(0, half, rows):
                 six, cross = coefficients(kappa, ref[i, pl.ds(r, rows), :])
                 six_ref[c, slot, pl.ds(r, rows), :] = six * there
@@ -286,20 +297,22 @@
 
 
 def far_kernel(
-    zero_in_ref, one_in_ref, odd_ref, source_ref, six_ref, cross_ref, scale_ref, forward_ref,
+    zero_in_ref, one_in_ref, halo_ref, source_ref, six_ref, cross_ref, scale_ref, forward_ref,
     zero_ref, one_ref, send_ref, keep_ref,
 ):
     _, slots, _, size_z = zero_in_ref.shape
     layers, size_y, _ = scale_ref.shape
     half = size_y // 2
-    on_right = even_side_on_right()
+    tile, tiles = lax.axis_index("tile"), lax.axis_size("tile")
+    on_right = near_on_right()
     reached = layers + SWEEPS
     clear_edges(zero_ref, range(SWEEPS, slots - 1), half)
     clear_edges(one_ref, range(SWEEPS, slots), half)
     for part in range(2):
         for slot in range(reached, slots):
             layer = layer_of(slot, layers)
-            values = odd_ref[part, jnp.where(on_right, layer + SWEEPS, layer - layers)]
+            values = halo_ref[part, jnp.where(on_right, layer + SWEEPS, layer - layers)]
+            values = jnp.where(jnp.where(on_right, tile == 0, tile == tiles - 1), 0.0, values)
             one_ref[part, slot, pl.ds(PAD, half), :] = values
     sweeper = Sweeper(half, size_z, layers, source_ref, six_ref, cross_ref)
     sweeper.where[0].update({slot: zero_in_ref for slot in range(1, reached - 1)})
@@ -382,13 +395,18 @@
     return [pltpu.VMEM(s, jnp.float32) for s in shapes]
 
 
-def swap_even(count):
-    return [(i, i ^ 1) for i in range(count) if i ^ 1 < count]
-
-
-def swap_odd(count):
-    pairs = [(i, i + 1) for i in range(1, count - 1, 2)]
-    return pairs + [(b, a) for a, b in pairs]
+def swaps(tiles, shards, odd_of):
+    pairs = []
+    for t in range(tiles):
+        for s in range(shards):
+            other = (t + 1 ^ 1) - 1 if odd_of(s) else t ^ 1
+            to = (other, s) if 0 <= other < tiles else (t, spare(s, shards, odd_of))
+            pairs.append((t * shards + s, to[0] * shards + to[1]))
+    return pairs
+
+
+def spare(s, shards, odd_of):
+    return next((o for o in (s ^ 1, s ^ 2) if o < shards and odd_of(o) == odd_of(s)), s)
 
 
 def body(
@@ -412,10 +430,9 @@
     cells = len(HALO_CELLS)
     reach = layers + 2 * (SWEEPS - 1)
     slots = layers + 2 * SWEEPS
-    evens, odds = swap_even(tiles), swap_odd(tiles)
     flip = [(i, i ^ 1) for i in range(shards)]
 
-    adj, cond_cells = call(
+    adj, cells_out = call(
         pack_kernel,
         [(2, layers, half, size_z), (cells, half, size_z)],
         floats((2, layers, size_y, size_z), (layers, size_y, size_z))
@@ -426,14 +443,12 @@
         room=20,
     )(in_hbm(adjoint_guess), in_hbm(conductivity))
 
-    mixed = [
-        (a * shards + s, b * shards + s)
-        for s in range(shards)
-        for a, b in (odds if s % 2 else evens)
-    ]
-    cond_cells = lax.ppermute(cond_cells, ("tile", "src"), mixed)
-    adj_odd = lax.ppermute(adj, "tile", odds)
-    adj_even = lax.ppermute(adj, "tile", evens)
+    both = ("tile", "src")
+    to_near = swaps(tiles, shards, is_even)
+    to_far = swaps(tiles, shards, is_odd)
+    far_cells = lax.ppermute(cells_out, both, to_far)
+    near_halo = lax.ppermute(adj, both, to_near)
+    far_halo = lax.ppermute(adj, both, to_far)
 
     source, six_own, cross_own, scale, kappa = call(
         source_kernel,
@@ -463,21 +478,21 @@
         in_hbm(recv_weights.T), in_hbm(recv_data), in_hbm(conductivity),
     )
 
-    other_cells = lax.ppermute(cond_cells, "src", flip)
+    near_cells = lax.ppermute(far_cells, "src", flip)
 
     state = (2, slots, half + 2 * PAD, size_z)
     weights = (2, slots, half, size_z)
     zero, one, six, cross = call(
         near_kernel, [state, state, weights, weights], [], [VMEM] * 8, [VMEM] * 4, 1 << 26
     )(
-        adj, adj_even, cond_cells, other_cells, source, six_own, cross_own, kappa
+        adj, near_halo, far_cells, near_cells, source, six_own, cross_own, kappa
     )
 
     shard_rows = size_y // shards
     part_shape = (shards // 2, layers, shard_rows, size_z)
     zero, one, send, keep = call(
         far_kernel, [state, state, part_shape, part_shape], [], [VMEM] * 8, [VMEM] * 4, 1 << 26
-    )(zero, one, adj_odd, source, six, cross, scale, forward_field)
+    )(zero, one, far_halo, source, six, cross, scale, forward_field)
 
     (field,) = call(
         unpack_kernel,

time: 34.5 us -> 32.4 us (0.939)
  waiting for transfers between devices: 12.6 us -> 9.07 us
  starting transfers between devices: 7.8 us -> 9.36 us
    ppermute x4, waiting for transfers between devices: 8.29 us -> 4.9 us  [the longest x1 4.89 us: body(): far_cells = lax.ppermute(cells_out, both, to_far)]
    ppermute x2, starting transfers between devices: 2.07 us -> 3.08 us  [body(): lax.ppermute(send, 'src', [(i, i ^ bit) for i in range(shards)])]
    ppermute x4, starting transfers between devices: 5.73 us -> 6.27 us  [the longest x1 3.12 us: body(): far_cells = lax.ppermute(cells_out, both, to_far)]
  transfers between devices with their start and end apart: 6 -> 6, of which waited for: 4 -> 3; matrix products, arithmetic and copies ran while one was open for 0% -> 0% of each run, Pallas kernels for 26% -> 27%
where the time goes in v4:
time: 32.4 us; the launch traced here: 32.2 us
  Pallas kernels  11.7 us (36%)
  starting transfers between devices  9.36 us (29%)
  waiting for transfers between devices  9.07 us (28%)
  between operations  1.37 us (4%)
  other arithmetic  0.7 us (2%)
    pallas_call x1, Pallas kernels, body(): call(source_kernel, [(2, 2, reach, half, size_z), (2, layers, half, size_...  6.55 us
    ppermute x1, waiting for transfers between devices, body(): far_cells = lax.ppermute(cells_out, both, to_far)  4.89 us
    ppermute x2, waiting for transfers between devices, body(): lax.ppermute(send, 'src', [(i, i ^ bit) for i in range(shards)])  4.17 us
    ppermute x1, starting transfers between devices, body(): far_cells = lax.ppermute(cells_out, both, to_far)  3.12 us
    ppermute x2, starting transfers between devices, body(): lax.ppermute(send, 'src', [(i, i ^ bit) for i in range(shards)])  3.08 us
    ppermute x1, starting transfers between devices, body(): far_halo = lax.ppermute(adj, both, to_far)  1.66 us
    pallas_call x1, Pallas kernels, body(): call(far_kernel, [state, state, part_shape, part_shape], [], [VMEM] * 8,...  1.5 us
    ppermute x1, starting transfers between devices, body(): near_halo = lax.ppermute(adj, both, to_near)  1.49 us
  transfers between devices with their start and end apart: 6, of which 3 were waited for; matrix products, arithmetic and copies ran while one was open for 0% of the time, Pallas kernels for 27%

profile of v4, /device:TPU:0, one launch (start us, length us, event | category | flops | bytes accessed | tf_op | source)
XLA Modules:
  0.0 32.2 jit_solution(14962323876564373771)
XLA Ops:
  0.6 1.4 %shard_map.113 = (f32[2,4,128,128]{3,2,1,0:T(8,128)S(1)}, f32[5,128,128]{2,1,0:T(8,128)S(1)}) custom-call(f32[1,2,4,256,128]{4,3,2,1,0:T(8,128)} %guess_hbm.1, f32[4,256,128]{2,1,0:T(8,128)} %cond_hbm.3), custom_call_target="tpu_custom_call" | custom-call | flops 1048576 | bytes 4194304 | tf_op jit(solution)/shard_map/pallas_call | solution.py:435
  2.0 3.1 %collective-permute-start.1 = (f32[5,128,128]{2,1,0:T(8,128)S(1)}, f32[5,128,128]{2,1,0:T(8,128)S(1)}, u32[]{:S(2)}, u32[]{:S(2)}) collective-permute-start(f32[5,128,128]{2,1,0:T(8,128)S(1)} %get-tuple-element.18), channel_id=1, source_target_pairs={{0,4},{1,3},{2,6},{3,1},{4,0},{5,9},{6,2},{7,11},{8,12},{9,5},{10,... | collective-permute-start | bytes 983048 | tf_op jit(solution)/shard_map/ppermute | solution.py:449
  5.2 1.5 %collective-permute-start = (f32[2,4,128,128]{3,2,1,0:T(8,128)S(1)}, f32[2,4,128,128]{3,2,1,0:T(8,128)S(1)}, u32[]{:S(2)}, u32[]{:S(2)}) collective-permute-start(f32[2,4,128,128]{3,2,1,0:T(8,128)S(1)} %get-tuple-element.17.adj_ref), channel_id=1, source_target_pairs={{0,2},{1,5},{2,0},{3,7},{4,8},{5,1},{6,10},{7,3},{8,4},{9,13},{10,... | collective-permute-start | bytes 1572872 | tf_op jit(solution)/shard_map/ppermute | solution.py:450
  6.7 1.7 %collective-permute-start.3 = (f32[2,4,128,128]{3,2,1,0:T(8,128)S(1)}, f32[2,4,128,128]{3,2,1,0:T(8,128)S(1)}, u32[]{:S(2)}, u32[]{:S(2)}) collective-permute-start(f32[2,4,128,128]{3,2,1,0:T(8,128)S(1)} %get-tuple-element.17.adj_ref), channel_id=1, source_target_pairs={{0,4},{1,3},{2,6},{3,1},{4,0},{5,9},{6,2},{7,11},{8,12},{9,5},{10,... | collective-permute-start | bytes 1572872 | tf_op jit(solution)/shard_map/ppermute | solution.py:451
  8.3 4.9 %collective-permute-done.1.far_cells_ref = f32[5,128,128]{2,1,0:T(8,128)S(1)} collective-permute-done((f32[5,128,128]{2,1,0:T(8,128)S(1)}, f32[5,128,128]{2,1,0:T(8,128)S(1)}, u32[]{:S(2)}, u32[]{:S(2)}) %collective-permute-start.1) | collective-permute-done | bytes 327712 | tf_op jit(solution)/shard_map/ppermute | solution.py:449
  13.2 0.0 collective-permute-start.2
  13.9 6.5 %shard_map.114 = (f32[2,2,10,128,128]{4,3,2,1,0:T(8,128)S(1)}, f32[2,4,128,128]{3,2,1,0:T(8,128)S(1)}, f32[2,4,128,128]{3,2,1,0:T(8,128)S(1)}, f32[4,256,128]{2,1,0:T(8,128)S(1)}, f32[8,128]{1,0:T(8,128)S(1)}) custom-call(s32[256]{0:T(256)} %x_hbm.1, s32[256]{0:T(256)} %y_hbm.1, s32[256]{0:T(256)} %z_hbm.1, f32[4]{0:T(128)} %kappas_hbm.1, ...), custom_call_target="tpu_custom_call" | custom-call | flops 1073741824 | bytes 4194304 | tf_op jit(solution)/shard_map/pallas_call | solution.py:453
  20.4 0.0 collective-permute-done.halo_ref
  20.4 0.0 collective-permute-done.2.near_cells_ref
  20.4 0.0 copy-start
  20.5 1.2 %shard_map.115 = (f32[2,12,144,128]{3,2,1,0:T(8,128)S(1)}, f32[2,12,144,128]{3,2,1,0:T(8,128)S(1)}, f32[2,12,128,128]{3,2,1,0:T(8,128)S(1)}, f32[2,12,128,128]{3,2,1,0:T(8,128)S(1)}) custom-call(f32[2,4,128,128]{3,2,1,0:T(8,128)S(1)} %get-tuple-element.17.adj_ref, f32[2,4,128,128]{3,2,1,0:T(8,128)S(1)} %collective-permute-done.halo_ref, ...), custom_call_target="tpu_custom_call" | custom-call | flops 67108864 | bytes 4194304 | tf_op jit(solution)/shard_map/pallas_call | solution.py:485
  21.7 0.0 collective-permute-done.3.halo_ref
  21.7 0.0 copy-done
  21.7 1.5 %shard_map.116 = (f32[2,12,144,128]{3,2,1,0:T(8,128)S(1)}, f32[2,12,144,128]{3,2,1,0:T(8,128)S(1)}, f32[2,4,64,128]{3,2,1,0:T(8,128)S(1)}, f32[2,4,64,128]{3,2,1,0:T(8,128)S(1)}) custom-call(f32[2,12,144,128]{3,2,1,0:T(8,128)S(1)} %get-tuple-element.23.zero_in_ref, f32[2,12,144,128]{3,2,1,0:T(8,128)S(1)} %get-tuple-element.24.one_in_ref, ...), custom_call_target="tpu_custom_call" | custom-call | flops 67108864 | bytes 4194304 | tf_op jit(solution)/shard_map/pallas_call | solution.py:493
  23.2 0.6 %collective-permute-start.4 = (f32[2,4,64,128]{3,2,1,0:T(8,128)S(1)}, f32[2,4,64,128]{3,2,1,0:T(8,128)S(1)}, u32[]{:S(2)}, u32[]{:S(2)}) collective-permute-start(f32[2,4,64,128]{3,2,1,0:T(8,128)S(1)} %get-tuple-element.31), channel_id=1, source_target_pairs={{0,1},{1,0},{2,3},{3,2},{4,5},{5,4},{6,7},{7,6},{8,9},{9,8},{10,11... | collective-permute-start | bytes 786440 | tf_op jit(solution)/shard_map/ppermute | solution.py:508
  23.8 1.2 %collective-permute-done.4 = f32[2,4,64,128]{3,2,1,0:T(8,128)S(1)} collective-permute-done((f32[2,4,64,128]{3,2,1,0:T(8,128)S(1)}, f32[2,4,64,128]{3,2,1,0:T(8,128)S(1)}, u32[]{:S(2)}, u32[]{:S(2)}) %collective-permute-start.4) | collective-permute-done | bytes 262176 | tf_op jit(solution)/shard_map/ppermute | solution.py:508
  25.0 2.5 %collective-permute-start.5 = (f32[1,4,64,128]{3,2,1,0:T(8,128)S(1)}, f32[1,4,64,128]{3,2,1,0:T(8,128)S(1)}, u32[]{:S(2)}, u32[]{:S(2)}) collective-permute-start(f32[1,4,64,128]{3,2,1,0:T(8,128)S(1)} %slice.11), channel_id=1, source_target_pairs={{0,2},{1,3},{2,0},{3,1},{4,6},{5,7},{6,4},{7,5},{8,10},{9,11},{10,... | collective-permute-start | bytes 393224 | tf_op jit(solution)/shard_map/ppermute | solution.py:508
  27.5 1.0 %shard_map.117 = f32[1,2,4,256,128]{4,3,2,1,0:T(8,128)} custom-call(f32[2,12,144,128]{3,2,1,0:T(8,128)S(1)} %get-tuple-element.28.zero_ref, f32[2,12,144,128]{3,2,1,0:T(8,128)S(1)} %get-tuple-element.29.one_ref), custom_call_target="tpu_custom_call" | custom-call | flops 1048576 | bytes 4194304 | tf_op jit(solution)/shard_map/pallas_call | solution.py:497
  28.5 3.0 %collective-permute-done.5 = f32[1,4,64,128]{3,2,1,0:T(8,128)S(1)} collective-permute-done((f32[1,4,64,128]{3,2,1,0:T(8,128)S(1)}, f32[1,4,64,128]{3,2,1,0:T(8,128)S(1)}, u32[]{:S(2)}, u32[]{:S(2)}) %collective-permute-start.5) | collective-permute-done | bytes 131104 | tf_op jit(solution)/shard_map/ppermute | solution.py:508
  31.5 0.7 %fusion = f32[4,64,128]{2,1,0:T(8,128)} fusion(f32[1,4,64,128]{3,2,1,0:T(8,128)S(1)} %collective-permute-done.5, f32[2,4,64,128]{3,2,1,0:T(8,128)S(1)} %add.6), kind=kLoop, calls=%fused_computation.1 | loop fusion | flops 32768 | bytes 393216 | tf_op jit(solution)/shard_map/squeeze | solution.py:513
  (2 shorter events, 0.0 us)
Async XLA Ops:
  2.0 11.2 %collective-permute-start.1 = (f32[5,128,128]{2,1,0:T(8,128)S(1)}, f32[5,128,128]{2,1,0:T(8,128)S(1)}, u32[]{:S(2)}, u32[]{:S(2)}) collective-permute-start(f32[5,128,128]{2,1,0:T(8,128)S(1)} %get-tuple-element.18), channel_id=1, source_target_pairs={{0,4},{1,3},{2,6},{3,1},{4,0},{5,9},{6,2},{7,11},{8,12},{9,5},{10,... | collective-permute-start | bytes 983048 | tf_op jit(solution)/shard_map/ppermute | solution.py:449
  5.2 15.3 %collective-permute-start = (f32[2,4,128,128]{3,2,1,0:T(8,128)S(1)}, f32[2,4,128,128]{3,2,1,0:T(8,128)S(1)}, u32[]{:S(2)}, u32[]{:S(2)}) collective-permute-start(f32[2,4,128,128]{3,2,1,0:T(8,128)S(1)} %get-tuple-element.17.adj_ref), channel_id=1, source_target_pairs={{0,2},{1,5},{2,0},{3,7},{4,8},{5,1},{6,10},{7,3},{8,4},{9,13},{10,... | collective-permute-start | bytes 1572872 | tf_op jit(solution)/shard_map/ppermute | solution.py:450
  6.7 15.0 %collective-permute-start.3 = (f32[2,4,128,128]{3,2,1,0:T(8,128)S(1)}, f32[2,4,128,128]{3,2,1,0:T(8,128)S(1)}, u32[]{:S(2)}, u32[]{:S(2)}) collective-permute-start(f32[2,4,128,128]{3,2,1,0:T(8,128)S(1)} %get-tuple-element.17.adj_ref), channel_id=1, source_target_pairs={{0,4},{1,3},{2,6},{3,1},{4,0},{5,9},{6,2},{7,11},{8,12},{9,5},{10,... | collective-permute-start | bytes 1572872 | tf_op jit(solution)/shard_map/ppermute | solution.py:451
  13.2 7.2 %collective-permute-start.2 = (f32[5,128,128]{2,1,0:T(8,128)S(1)}, f32[5,128,128]{2,1,0:T(8,128)S(1)}, u32[]{:S(2)}, u32[]{:S(2)}) collective-permute-start(f32[5,128,128]{2,1,0:T(8,128)S(1)} %collective-permute-done.1.far_cells_ref), channel_id=1, source_target_pairs={{0,1},{1,0},{2,3},{3,2},{4,5},{5,4},{6,7},{7,6},{8,9},{9,8},{10,11... | collective-permute-start | bytes 983048 | tf_op jit(solution)/shard_map/ppermute | solution.py:481
  20.4 1.3 %copy-start = (f32[1,2,4,256,128]{4,3,2,1,0:T(8,128)S(1)}, f32[1,2,4,256,128]{4,3,2,1,0:T(8,128)}, u32[]{:S(2)}) copy-start(f32[1,2,4,256,128]{4,3,2,1,0:T(8,128)} %forward_ref.1) | copy-start | bytes 3145732
  23.2 1.7 %collective-permute-start.4 = (f32[2,4,64,128]{3,2,1,0:T(8,128)S(1)}, f32[2,4,64,128]{3,2,1,0:T(8,128)S(1)}, u32[]{:S(2)}, u32[]{:S(2)}) collective-permute-start(f32[2,4,64,128]{3,2,1,0:T(8,128)S(1)} %get-tuple-element.31), channel_id=1, source_target_pairs={{0,1},{1,0},{2,3},{3,2},{4,5},{5,4},{6,7},{7,6},{8,9},{9,8},{10,11... | collective-permute-start | bytes 786440 | tf_op jit(solution)/shard_map/ppermute | solution.py:508
  25.0 6.6 %collective-permute-start.5 = (f32[1,4,64,128]{3,2,1,0:T(8,128)S(1)}, f32[1,4,64,128]{3,2,1,0:T(8,128)S(1)}, u32[]{:S(2)}, u32[]{:S(2)}) collective-permute-start(f32[1,4,64,128]{3,2,1,0:T(8,128)S(1)} %slice.11), channel_id=1, source_target_pairs={{0,2},{1,3},{2,0},{3,1},{4,6},{5,7},{6,4},{7,5},{8,10},{9,11},{10,... | collective-permute-start | bytes 393224 | tf_op jit(solution)/shard_map/ppermute | solution.py:508

commit v5 on v4

--- a/solution.py
+++ b/solution.py
@@ -16,7 +16,7 @@
 )
 PAD = 8
 ROWS = 32
-UNROLL = 8
+UNROLL = 32
 SMEM = pl.BlockSpec(memory_space=pltpu.SMEM)
 VMEM = pl.BlockSpec(memory_space=pltpu.VMEM)
 HBM = pl.BlockSpec(memory_space=pltpu.HBM)
@@ -61,36 +61,50 @@
     return copies
 
 
-def pack_kernel(guess_hbm, cond_hbm, adj_ref, cells_ref, guess_ref, cond_ref, sems):
-    layers, size_y, size_z = cond_ref.shape
+def pack_kernel(guess_hbm, adj_ref, first_ref, second_ref, guess_ref, sems):
+    _, layers, half, size_z = adj_ref.shape
+    rows = min(ROWS, half)
+    first = lax.axis_index("tile") * layers
+    depth = first_ref.shape[1]
+    copies = start_all(
+        [
+            pltpu.make_async_copy(guess_hbm.at[0, :, i], guess_ref.at[:, i], sems.at[i])
+            for i in range(layers)
+        ]
+    )
+    for layer in range(layers):
+        odd = odd_lanes(first + layer, rows, size_z)
+        copies[layer].wait()
+        for part in range(2):
+            for r in range(0, half, rows):
+                a = guess_ref[part, layer, pl.ds(2 * r, rows, stride=2), :]
+                b = guess_ref[part, layer, pl.ds(2 * r + 1, rows, stride=2), :]
+                adj_ref[part, layer, pl.ds(r, rows), :] = of_colour(1, odd, a, b)
+    for d in range(SWEEPS):
+        layer = layer_of(SWEEPS + layers - 1 - d, layers)
+        ref = (first_ref, second_ref)[d // depth]
+        for part in range(2):
+            ref[part, d % depth] = adj_ref[part, layer]
+
+
+def cells_kernel(cond_hbm, cells_ref, cond_ref, sems):
+    layers = cond_hbm.shape[0]
+    deep, size_y, size_z = cond_ref.shape
     half = size_y // 2
     rows = min(ROWS, half)
-    first = lax.axis_index("tile") * layers
-    cond_copy = pltpu.make_async_copy(cond_hbm, cond_ref, sems.at[0])
-    cond_copy.start()
-    guess_copies = start_all(
-        [
-            pltpu.make_async_copy(guess_hbm.at[0, :, i], guess_ref.at[:, i], sems.at[1 + i])
-            for i in range(layers)
-        ]
-    )
     to_right = jnp.logical_not(near_on_right())
-    cond_copy.wait()
+    base = jnp.where(to_right, layers - deep, 0)
+    copy = pltpu.make_async_copy(cond_hbm.at[pl.ds(base, deep)], cond_ref, sems.at[0])
+    copy.start()
+    copy.wait()
+    first = lax.axis_index("tile") * layers + base
     for i, (d, c) in enumerate(HALO_CELLS):
-        layer = jnp.where(to_right, layers - d, d - 1)
+        layer = jnp.where(to_right, deep - d, d - 1)
         odd = odd_lanes(first + layer, rows, size_z)
         for r in range(0, half, rows):
             a = cond_ref[layer, pl.ds(2 * r, rows, stride=2), :]
             b = cond_ref[layer, pl.ds(2 * r + 1, rows, stride=2), :]
             cells_ref[i, pl.ds(r, rows), :] = of_colour(c, odd, a, b)
-    for layer in range(layers):
-        odd = odd_lanes(first + layer, rows, size_z)
-        guess_copies[layer].wait()
-        for part in range(2):
-            for r in range(0, half, rows):
-                a = guess_ref[part, layer, pl.ds(2 * r, rows, stride=2), :]
-                b = guess_ref[part, layer, pl.ds(2 * r + 1, rows, stride=2), :]
-                adj_ref[part, layer, pl.ds(r, rows), :] = of_colour(1, odd, a, b)
 
 
 def source_kernel(
@@ -140,10 +154,10 @@
         base = jnp.clip(x_ref[r] - first + halo, -4, reach) + 4
         row = 2 * y_ref[r]
         inside = (lane - z).astype(jnp.uint32) < 4
-        both = terms_ref[pl.ds(pl.multiple_of(8 * r, 8), 8), :]
+        first_tap = pltpu.roll(terms_ref[pl.ds(pl.multiple_of(8 * r, 8), 8), :], z, 1)
         terms = []
         for a in range(4):
-            moved = pltpu.roll(both, lax.rem(z + size_z - 16 * a, size_z), 1)
+            moved = pltpu.roll(first_tap, size_z - 16 * a, 1) if a else first_tap
             terms.append(jnp.where(inside, moved, 0.0))
         old = [total_ref[base + a, pl.ds(row, 8), :] for a in range(4)]
         for a in range(4):
@@ -208,39 +222,39 @@
 
     def sums(self, c, part, slot):
         old = self.where[1 - c]
-        here, left, right = old[slot], old[slot - 1], old[slot + 1]
+        (here, at_here), (left, at_left), (right, at_right) = old[slot], old[slot - 1], old[slot + 1]
         rows = self.rows
         by_matrix = part == 1
         if by_matrix:
-            beside = self.along_z(here[part, slot, pl.ds(PAD, self.half), :])
+            beside = self.along_z(here[part, at_here, pl.ds(PAD, self.half), :])
         out = []
         for r in range(0, self.half, rows):
-            above = here[part, slot, pl.ds(PAD + r + 1, rows), :]
-            below = here[part, slot, pl.ds(PAD + r - 1, rows), :]
+            above = here[part, at_here, pl.ds(PAD + r + 1, rows), :]
+            below = here[part, at_here, pl.ds(PAD + r - 1, rows), :]
             if (slot + c) % 2:
                 above, below = below, above
-            total = left[part, slot - 1, pl.ds(PAD + r, rows), :]
-            total += right[part, slot + 1, pl.ds(PAD + r, rows), :]
+            total = left[part, at_left, pl.ds(PAD + r, rows), :]
+            total += right[part, at_right, pl.ds(PAD + r, rows), :]
             total += jnp.where(self.odd, above, below)
             if by_matrix:
                 total += beside[r : r + rows]
             else:
-                centre = here[part, slot, pl.ds(PAD + r, rows), :]
+                centre = here[part, at_here, pl.ds(PAD + r, rows), :]
                 total += centre
                 total += jnp.where(self.after, pltpu.roll(centre, 1, 1), 0.0)
                 total += jnp.where(self.before, pltpu.roll(centre, self.size_z - 1, 1), 0.0)
             out.append(total + self.source[c, part, slot - 1, pl.ds(r, rows), :])
         return out
 
-    def update(self, c, slot, new):
+    def update(self, c, slot, new, index):
         sums = [self.sums(c, part, slot) for part in range(2)]
         for i, r in enumerate(range(0, self.half, self.rows)):
             six = self.six[c, slot, pl.ds(r, self.rows), :]
             cross = self.cross[c, slot, pl.ds(r, self.rows), :]
             at = pl.ds(PAD + r, self.rows)
-            new[0, slot, at, :] = six * sums[0][i] + cross * sums[1][i]
-            new[1, slot, at, :] = six * sums[1][i] - cross * sums[0][i]
-        self.where[c][slot] = new
+            new[0, index, at, :] = six * sums[0][i] + cross * sums[1][i]
+            new[1, index, at, :] = six * sums[1][i] - cross * sums[0][i]
+        self.where[c][slot] = (new, index)
 
 
 def clear_edges(ref, slots, half):
@@ -290,47 +304,19 @@
                 six_ref[c, slot, pl.ds(r, rows), :] = six * there
                 cross_ref[c, slot, pl.ds(r, rows), :] = cross * there
     sweeper = Sweeper(half, size_z, layers, source_ref, six_ref, cross_ref)
-    sweeper.where[1].update({slot: one_ref for slot in range(reached)})
+    sweeper.where[1].update({slot: (one_ref, slot) for slot in range(reached)})
     for k, c in enumerate(COLOURS):
         for slot in range(1 + k, reached - 1 - k):
-            sweeper.update(c, slot, (zero_ref, one_ref)[c])
-
-
-def far_kernel(
-    zero_in_ref, one_in_ref, halo_ref, source_ref, six_ref, cross_ref, scale_ref, forward_ref,
-    zero_ref, one_ref, send_ref, keep_ref,
-):
-    _, slots, _, size_z = zero_in_ref.shape
-    layers, size_y, _ = scale_ref.shape
-    half = size_y // 2
-    tile, tiles = lax.axis_index("tile"), lax.axis_size("tile")
-    on_right = near_on_right()
-    reached = layers + SWEEPS
-    clear_edges(zero_ref, range(SWEEPS, slots - 1), half)
-    clear_edges(one_ref, range(SWEEPS, slots), half)
-    for part in range(2):
-        for slot in range(reached, slots):
-            layer = layer_of(slot, layers)
-            values = halo_ref[part, jnp.where(on_right, layer + SWEEPS, layer - layers)]
-            values = jnp.where(jnp.where(on_right, tile == 0, tile == tiles - 1), 0.0, values)
-            one_ref[part, slot, pl.ds(PAD, half), :] = values
-    sweeper = Sweeper(half, size_z, layers, source_ref, six_ref, cross_ref)
-    sweeper.where[0].update({slot: zero_in_ref for slot in range(1, reached - 1)})
-    sweeper.where[1].update({slot: one_in_ref for slot in range(reached)})
-    sweeper.where[1].update({slot: one_ref for slot in range(reached, slots)})
-    for k, c in enumerate(COLOURS):
-        for slot in range(reached - 1 - k, slots - 1 - k):
-            sweeper.update(c, slot, (zero_ref, one_ref)[c])
-    for slot in range(SWEEPS, SWEEPS + layers):
-        if sweeper.where[0][slot] is zero_in_ref:
-            for part in range(2):
-                zero_ref[part, slot, pl.ds(PAD, half), :] = zero_in_ref[part, slot, pl.ds(PAD, half), :]
-
+            sweeper.update(c, slot, (zero_ref, one_ref)[c], slot)
+
+
+def gradient_terms(slots, zeros, ones, scale_ref, forward_ref, send_ref, keep_ref):
+    layers, size_y, size_z = scale_ref.shape
     shards = 2 * send_ref.shape[0]
     shard = lax.axis_index("src")
     shard_rows = size_y // shards
     rows = min(ROWS, shard_rows // 2)
-    for slot in range(SWEEPS, SWEEPS + layers):
+    for slot in slots:
         layer = layer_of(slot, layers)
         swap = odd_lanes(lax.axis_index("tile") * layers + layer, rows, size_z)
         for m in range(shards):
@@ -338,8 +324,10 @@
             start = (shard ^ m) * shard_rows
             for r in range(0, shard_rows // 2, rows):
                 at = pl.ds(pl.multiple_of(PAD + start // 2 + r, PAD), rows)
-                a = [zero_ref[part, slot, at, :] for part in range(2)]
-                b = [one_ref[part, slot, at, :] for part in range(2)]
+                a, b = (
+                    [ref[part, i, at, :] for part in range(2)]
+                    for ref, i in (zeros[slot], ones[slot])
+                )
                 for second in range(2):
                     if second:
                         a, b = b, a
@@ -348,11 +336,77 @@
                     products = forward_ref[0, 0, layer, cells, :] * field[1]
                     products += forward_ref[0, 1, layer, cells, :] * field[0]
                     into = pl.ds(2 * r + second, rows, stride=2)
-                    ref[m // 2, layer, into, :] = scale_ref[slot - SWEEPS, cells, :] * products
-
-
-def unpack_kernel(zero_ref, one_ref, out_hbm, out_ref, sems):
+                    ref[m // 2, layer % len(slots), into, :] = (
+                        scale_ref[slot - SWEEPS, cells, :] * products
+                    )
+
+
+def far_sweeps(begin, depth, halo_ref, source_ref, six_ref, cross_ref, scale_ref, older, zero_ref, one_ref):
+    layers, size_y, size_z = scale_ref.shape
+    half = size_y // 2
+    tile, tiles = lax.axis_index("tile"), lax.axis_size("tile")
+    missing = jnp.where(near_on_right(), tile == 0, tile == tiles - 1)
+    bases = (begin - SWEEPS + 1, begin - SWEEPS)
+    clear_edges(zero_ref, range(zero_ref.shape[1]), half)
+    clear_edges(one_ref, range(one_ref.shape[1]), half)
+    for part in range(2):
+        for d in range(depth):
+            values = jnp.where(missing, 0.0, halo_ref[part, d])
+            one_ref[part, begin + d - bases[1], pl.ds(PAD, half), :] = values
+    sweeper = Sweeper(half, size_z, layers, source_ref, six_ref, cross_ref)
+    for c in (0, 1):
+        sweeper.where[c].update(older[c])
+    sweeper.where[1].update({begin + d: (one_ref, begin + d - bases[1]) for d in range(depth)})
+    for k, c in enumerate(COLOURS):
+        for slot in range(begin - 1 - k, begin + depth - 1 - k):
+            sweeper.update(c, slot, (zero_ref, one_ref)[c], slot - bases[c])
+    return sweeper.where
+
+
+def near_values(zero_ref, one_ref):
+    reached = 2 * SWEEPS
+    return (
+        {slot: (zero_ref, slot) for slot in range(1, reached - 1)},
+        {slot: (one_ref, slot) for slot in range(reached)},
+    )
+
+
+def first_kernel(
+    zero_in_ref, one_in_ref, halo_ref, source_ref, six_ref, cross_ref, scale_ref, forward_ref,
+    zero_ref, one_ref, send_ref, keep_ref,
+):
+    depth = halo_ref.shape[1]
+    zeros, ones = far_sweeps(
+        2 * SWEEPS, depth, halo_ref, source_ref, six_ref, cross_ref, scale_ref,
+        near_values(zero_in_ref, one_in_ref), zero_ref, one_ref,
+    )
+    done = range(SWEEPS, SWEEPS + depth)
+    gradient_terms(done, zeros, ones, scale_ref, forward_ref, send_ref, keep_ref)
+
+
+def second_kernel(
+    zero_in_ref, one_in_ref, halo_ref, source_ref, six_ref, cross_ref, scale_ref, forward_ref,
+    zero_ref, one_ref, send_ref, keep_ref,
+):
+    depth = halo_ref.shape[1]
+    begin = 2 * SWEEPS + depth
+    older = (
+        {SWEEPS + 1 + i: (zero_in_ref, i) for i in range(zero_in_ref.shape[1])},
+        {SWEEPS + i: (one_in_ref, i) for i in range(one_in_ref.shape[1])},
+    )
+    zeros, ones = far_sweeps(
+        begin, depth, halo_ref, source_ref, six_ref, cross_ref, scale_ref, older, zero_ref, one_ref
+    )
+    done = range(SWEEPS + depth, SWEEPS + 2 * depth)
+    gradient_terms(done, zeros, ones, scale_ref, forward_ref, send_ref, keep_ref)
+
+
+def unpack_kernel(near_ref, zero_a_ref, one_a_ref, zero_b_ref, one_b_ref, out_hbm, out_ref, sems):
     _, layers, size_y, size_z = out_ref.shape
+    depth = layers // 2
+    zeros = [(near_ref, SWEEPS)] + [(zero_a_ref, i) for i in range(depth)]
+    zeros += [(zero_b_ref, i) for i in range(depth - 1)]
+    ones = [(ref, i) for ref in (one_a_ref, one_b_ref) for i in range(depth)]
     half = size_y // 2
     rows = min(ROWS, half)
     first = lax.axis_index("tile") * layers
@@ -362,8 +416,8 @@
         odd = odd_lanes(first + layer, rows, size_z)
         for part in range(2):
             for r in range(0, half, rows):
-                a = zero_ref[part, slot, pl.ds(PAD + r, rows), :]
-                b = one_ref[part, slot, pl.ds(PAD + r, rows), :]
+                a = zeros[slot - SWEEPS][0][part, zeros[slot - SWEEPS][1], pl.ds(PAD + r, rows), :]
+                b = ones[slot - SWEEPS][0][part, ones[slot - SWEEPS][1], pl.ds(PAD + r, rows), :]
                 out_ref[part, slot - SWEEPS, pl.ds(2 * r, rows, stride=2), :] = jnp.where(odd, b, a)
                 out_ref[part, slot - SWEEPS, pl.ds(2 * r + 1, rows, stride=2), :] = jnp.where(odd, a, b)
         i = slot - SWEEPS
@@ -375,7 +429,17 @@
         copy.wait()
 
 
-def call(kernel, outs, scratch, specs, out_specs, flops, room=20):
+def join_kernel(keep_a_ref, got_a_ref, keep_b_ref, got_b_ref, send_ref, keep_ref):
+    depth = keep_a_ref.shape[1]
+    begun = jnp.where(near_on_right(), depth, 0)
+    for i in range(keep_a_ref.shape[0]):
+        ref = send_ref if i % 2 else keep_ref
+        for d in range(depth):
+            ref[i // 2, begun + d] = keep_a_ref[i, d] + got_a_ref[i, d]
+            ref[i // 2, depth - begun + d] = keep_b_ref[i, d] + got_b_ref[i, d]
+
+
+def call(kernel, outs, scratch, specs, out_specs, flops, room=8):
     return pl.pallas_call(
         kernel,
         out_shape=[jax.ShapeDtypeStruct(s, jnp.float32) for s in outs],
@@ -432,23 +496,31 @@
     slots = layers + 2 * SWEEPS
     flip = [(i, i ^ 1) for i in range(shards)]
 
-    adj, cells_out = call(
+    depth = layers // 2
+    piece = (2, depth, half, size_z)
+    adj, adj_first, adj_second = call(
         pack_kernel,
-        [(2, layers, half, size_z), (cells, half, size_z)],
-        floats((2, layers, size_y, size_z), (layers, size_y, size_z))
-        + [pltpu.SemaphoreType.DMA((1 + layers,))],
-        [HBM, HBM],
-        [VMEM] * 2,
+        [(2, layers, half, size_z), piece, piece],
+        floats((2, layers, size_y, size_z)) + [pltpu.SemaphoreType.DMA((layers,))],
+        [HBM],
+        [VMEM] * 3,
         1 << 20,
-        room=20,
-    )(in_hbm(adjoint_guess), in_hbm(conductivity))
-
+    )(in_hbm(adjoint_guess))
+    (cells_out,) = call(
+        cells_kernel,
+        [(cells, half, size_z)],
+        floats((SWEEPS - 1, size_y, size_z)) + [pltpu.SemaphoreType.DMA((1,))],
+        [HBM],
+        [VMEM],
+        1 << 20,
+    )(in_hbm(conductivity))
     both = ("tile", "src")
     to_near = swaps(tiles, shards, is_even)
     to_far = swaps(tiles, shards, is_odd)
     far_cells = lax.ppermute(cells_out, both, to_far)
     near_halo = lax.ppermute(adj, both, to_near)
-    far_halo = lax.ppermute(adj, both, to_far)
+    first_halo = lax.ppermute(adj_first, both, to_far)
+    second_halo = lax.ppermute(adj_second, both, to_far)
 
     source, six_own, cross_own, scale, kappa = call(
         source_kernel,
@@ -472,7 +544,7 @@
         [HBM] * 4 + [SMEM] + [HBM] * 3,
         [VMEM] * 5,
         1 << 30,
-        room=20,
+        room=16,
     )(
         in_hbm(recv_x), in_hbm(recv_y), in_hbm(recv_z), in_hbm(freq_kappa), pair_freq,
         in_hbm(recv_weights.T), in_hbm(recv_data), in_hbm(conductivity),
@@ -480,7 +552,7 @@
 
     near_cells = lax.ppermute(far_cells, "src", flip)
 
-    state = (2, slots, half + 2 * PAD, size_z)
+    state = (2, 2 * SWEEPS, half + 2 * PAD, size_z)
     weights = (2, slots, half, size_z)
     zero, one, six, cross = call(
         near_kernel, [state, state, weights, weights], [], [VMEM] * 8, [VMEM] * 4, 1 << 26
@@ -489,21 +561,40 @@
     )
 
     shard_rows = size_y // shards
-    part_shape = (shards // 2, layers, shard_rows, size_z)
-    zero, one, send, keep = call(
-        far_kernel, [state, state, part_shape, part_shape], [], [VMEM] * 8, [VMEM] * 4, 1 << 26
-    )(zero, one, far_halo, source, six, cross, scale, forward_field)
+    part_shape = (shards // 2, depth, shard_rows, size_z)
+
+    state_zero = (2, depth + SWEEPS - 2, half + 2 * PAD, size_z)
+    state_one = (2, depth + SWEEPS, half + 2 * PAD, size_z)
+
+    def far(kernel, *values):
+        return call(
+            kernel,
+            [state_zero, state_one, part_shape, part_shape],
+            [],
+            [VMEM] * 8,
+            [VMEM] * 4,
+            1 << 26,
+        )(*values, source, six, cross, scale, forward_field)
+
+    zero_a, one_a, send_a, keep_a = far(first_kernel, zero, one, first_halo)
+    got_b = lax.ppermute(send_a, "src", flip)
+    zero_b, one_b, send_b, keep_b = far(second_kernel, zero_a, one_a, second_halo)
+    got_a = lax.ppermute(send_b, "src", flip)
 
     (field,) = call(
         unpack_kernel,
         [(1, 2, layers, size_y, size_z)],
         floats((2, layers, size_y, size_z)) + [pltpu.SemaphoreType.DMA((layers,))],
-        [VMEM] * 2,
+        [VMEM] * 5,
         [HBM],
         1 << 20,
-    )(zero, one)
-
-    bit = 1
+    )(zero, zero_a, one_a, zero_b, one_b)
+
+    joined = (shards // 4, layers, shard_rows, size_z)
+    send, keep = call(
+        join_kernel, [joined, joined], [], [VMEM] * 4, [VMEM] * 2, 1 << 20
+    )(keep_a, got_a, keep_b, got_b)
+    bit = 2
     while True:
         keep = keep + lax.ppermute(send, "src", [(i, i ^ bit) for i in range(shards)])
         bit *= 2

time: 32.4 us -> 31.7 us (0.978)
  waiting for transfers between devices: 9.07 us -> 8 us
  starting transfers between devices: 9.36 us -> 9.7 us
    ppermute x1 -> x4, starting transfers between devices: 1.66 us -> 3.04 us  [the longest x1 2.38 us: body(): first_halo = lax.ppermute(adj_first, both, to_far)]
    ppermute x2 -> x1, waiting for transfers between devices: 4.17 us -> 2.99 us  [body(): lax.ppermute(send, 'src', [(i, i ^ bit) for i in range(shards)])]
    ppermute x1 -> x4, waiting for transfers between devices: 0.01 us -> 1.15 us  [the longest x1 1.14 us: body(): got_a = lax.ppermute(send_b, 'src', flip)]
    pallas_call x1, Pallas kernels: 6.55 us -> 5.41 us  [body(): call(source_kernel, [(2, 2, reach, half, size_z), (2, layers, half, size_...]
    pallas_call x2 -> x5, Pallas kernels: 2.91 us -> 4.04 us  [the longest x2 1.67 us: far(): call(kernel, [state_zero, state_one, part_shape, part_shape], [], [VMEM]...]
    ppermute x2 -> x1, starting transfers between devices: 3.08 us -> 1.99 us  [body(): lax.ppermute(send, 'src', [(i, i ^ bit) for i in range(shards)])]
    ppermute x1, waiting for transfers between devices: 4.89 us -> 3.86 us  [body(): far_cells = lax.ppermute(cells_out, both, to_far)]
  transfers between devices with their start and end apart: 6 -> 8, of which waited for: 3 -> 3; matrix products, arithmetic and copies ran while one was open for 0% -> 0% of each run, Pallas kernels for 27% -> 34%
where the time goes in v5:
time: 31.7 us; the launch traced here: 31.5 us
  Pallas kernels  11.8 us (37%)
  starting transfers between devices  9.7 us (31%)
  waiting for transfers between devices  8 us (25%)
  between operations  1.38 us (4%)
  other arithmetic  0.67 us (2%)
    pallas_call x1, Pallas kernels, body(): call(source_kernel, [(2, 2, reach, half, size_z), (2, layers, half, size_...  5.41 us
    ppermute x1, waiting for transfers between devices, body(): far_cells = lax.ppermute(cells_out, both, to_far)  3.86 us
    ppermute x1, starting transfers between devices, body(): far_cells = lax.ppermute(cells_out, both, to_far)  3.12 us
    ppermute x1, waiting for transfers between devices, body(): lax.ppermute(send, 'src', [(i, i ^ bit) for i in range(shards)])  2.99 us
    ppermute x1, starting transfers between devices, body(): first_halo = lax.ppermute(adj_first, both, to_far)  2.38 us
    ppermute x1, starting transfers between devices, body(): lax.ppermute(send, 'src', [(i, i ^ bit) for i in range(shards)])  1.99 us
    pallas_call x2, Pallas kernels, far(): call(kernel, [state_zero, state_one, part_shape, part_shape], [], [VMEM]...  1.67 us
    ppermute x1, starting transfers between devices, body(): near_halo = lax.ppermute(adj, both, to_near)  1.56 us
  transfers between devices with their start and end apart: 8, of which 3 were waited for; matrix products, arithmetic and copies ran while one was open for 0% of the time, Pallas kernels for 34%

profile of v5, /device:TPU:0, one launch (start us, length us, event | category | flops | bytes accessed | tf_op | source)
XLA Modules:
  0.0 31.5 jit_solution(13026824968902957587)
XLA Ops:
  0.6 1.1 %shard_map.114 = f32[5,128,128]{2,1,0:T(8,128)S(1)} custom-call(f32[4,256,128]{2,1,0:T(8,128)} %cond_hbm.3), custom_call_target="tpu_custom_call" | custom-call | flops 1048576 | bytes 4194304 | tf_op jit(solution)/shard_map/pallas_call | solution.py:509
  1.7 3.1 %collective-permute-start.1 = (f32[5,128,128]{2,1,0:T(8,128)S(1)}, f32[5,128,128]{2,1,0:T(8,128)S(1)}, u32[]{:S(2)}, u32[]{:S(2)}) collective-permute-start(f32[5,128,128]{2,1,0:T(8,128)S(1)} %shard_map.114), channel_id=1, source_target_pairs={{0,4},{1,3},{2,6},{3,1},{4,0},{5,9},{6,2},{7,11},{8,12},{9,5},{10,... | collective-permute-start | bytes 983048 | tf_op jit(solution)/shard_map/ppermute | solution.py:520
  4.8 1.3 %shard_map.113 = (f32[2,4,128,128]{3,2,1,0:T(8,128)S(1)}, f32[2,2,128,128]{3,2,1,0:T(8,128)S(1)}, f32[2,2,128,128]{3,2,1,0:T(8,128)S(1)}) custom-call(f32[1,2,4,256,128]{4,3,2,1,0:T(8,128)} %guess_hbm.1), custom_call_target="tpu_custom_call" | custom-call | flops 1048576 | bytes 4194304 | tf_op jit(solution)/shard_map/pallas_call | solution.py:501
  6.1 1.6 %collective-permute-start = (f32[2,4,128,128]{3,2,1,0:T(8,128)S(1)}, f32[2,4,128,128]{3,2,1,0:T(8,128)S(1)}, u32[]{:S(2)}, u32[]{:S(2)}) collective-permute-start(f32[2,4,128,128]{3,2,1,0:T(8,128)S(1)} %get-tuple-element.24.adj_ref), channel_id=1, source_target_pairs={{0,2},{1,5},{2,0},{3,7},{4,8},{5,1},{6,10},{7,3},{8,4},{9,13},{10,... | collective-permute-start | bytes 1572872 | tf_op jit(solution)/shard_map/ppermute | solution.py:521
  7.6 3.9 %collective-permute-done.1.far_cells_ref = f32[5,128,128]{2,1,0:T(8,128)S(1)} collective-permute-done((f32[5,128,128]{2,1,0:T(8,128)S(1)}, f32[5,128,128]{2,1,0:T(8,128)S(1)}, u32[]{:S(2)}, u32[]{:S(2)}) %collective-permute-start.1) | collective-permute-done | bytes 327712 | tf_op jit(solution)/shard_map/ppermute | solution.py:520
  11.5 0.0 collective-permute-start.2
  11.5 2.4 %collective-permute-start.3 = (f32[2,2,128,128]{3,2,1,0:T(8,128)S(1)}, f32[2,2,128,128]{3,2,1,0:T(8,128)S(1)}, u32[]{:S(2)}, u32[]{:S(2)}) collective-permute-start(f32[2,2,128,128]{3,2,1,0:T(8,128)S(1)} %get-tuple-element.31), channel_id=1, source_target_pairs={{0,4},{1,3},{2,6},{3,1},{4,0},{5,9},{6,2},{7,11},{8,12},{9,5},{10,... | collective-permute-start | bytes 786440 | tf_op jit(solution)/shard_map/ppermute | solution.py:522
  13.9 0.0 collective-permute-start.4
  14.6 5.4 %shard_map.115 = (f32[2,2,10,128,128]{4,3,2,1,0:T(8,128)S(1)}, f32[2,4,128,128]{3,2,1,0:T(8,128)S(1)}, f32[2,4,128,128]{3,2,1,0:T(8,128)S(1)}, f32[4,256,128]{2,1,0:T(8,128)S(1)}, f32[8,128]{1,0:T(8,128)S(1)}) custom-call(s32[256]{0:T(256)} %x_hbm.1, s32[256]{0:T(256)} %y_hbm.1, s32[256]{0:T(256)} %z_hbm.1, f32[4]{0:T(128)} %kappas_hbm.1, ...), custom_call_target="tpu_custom_call" | custom-call | flops 1073741824 | bytes 4194304 | tf_op jit(solution)/shard_map/pallas_call | solution.py:525
  20.0 0.0 collective-permute-done.2.near_cells_ref
  20.0 0.0 copy-start
  20.0 1.3 %shard_map.116 = (f32[2,8,144,128]{3,2,1,0:T(8,128)S(1)}, f32[2,8,144,128]{3,2,1,0:T(8,128)S(1)}, f32[2,12,128,128]{3,2,1,0:T(8,128)S(1)}, f32[2,12,128,128]{3,2,1,0:T(8,128)S(1)}) custom-call(f32[2,4,128,128]{3,2,1,0:T(8,128)S(1)} %get-tuple-element.24.adj_ref, f32[2,4,128,128]{3,2,1,0:T(8,128)S(1)} %collective-permute-done.halo_ref, ...), custom_call_target="tpu_custom_call" | custom-call | flops 67108864 | bytes 4194304 | tf_op jit(solution)/shard_map/pallas_call | solution.py:557
  21.3 0.0 collective-permute-done.3.halo_ref
  21.3 0.9 %shard_map.117 = (f32[2,4,144,128]{3,2,1,0:T(8,128)S(1)}, f32[2,6,144,128]{3,2,1,0:T(8,128)S(1)}, f32[2,2,64,128]{3,2,1,0:T(8,128)S(1)}, f32[2,2,64,128]{3,2,1,0:T(8,128)S(1)}) custom-call(f32[2,8,144,128]{3,2,1,0:T(8,128)S(1)} %get-tuple-element.29.zero_in_ref.near_ref, f32[2,8,144,128]{3,2,1,0:T(8,128)S(1)} %get-tuple-element.30.one_in_ref, ...), custom_call_target="tpu_custom_call" | custom-call | flops 67108864 | bytes 4194304 | tf_op jit(solution)/shard_map/pallas_call | solution.py:570
  22.2 0.4 %collective-permute-start.6 = (f32[2,2,64,128]{3,2,1,0:T(8,128)S(1)}, f32[2,2,64,128]{3,2,1,0:T(8,128)S(1)}, u32[]{:S(2)}, u32[]{:S(2)}) collective-permute-start(f32[2,2,64,128]{3,2,1,0:T(8,128)S(1)} %get-tuple-element.43), channel_id=1, source_target_pairs={{0,1},{1,0},{2,3},{3,2},{4,5},{5,4},{6,7},{7,6},{8,9},{9,8},{10,11... | collective-permute-start | bytes 393224 | tf_op jit(solution)/shard_map/ppermute | solution.py:580
  22.6 0.0 collective-permute-done.4.halo_ref
  22.6 0.8 %shard_map.118 = (f32[2,4,144,128]{3,2,1,0:T(8,128)S(1)}, f32[2,6,144,128]{3,2,1,0:T(8,128)S(1)}, f32[2,2,64,128]{3,2,1,0:T(8,128)S(1)}, f32[2,2,64,128]{3,2,1,0:T(8,128)S(1)}) custom-call(f32[2,4,144,128]{3,2,1,0:T(8,128)S(1)} %get-tuple-element.35.zero_in_ref.zero_a_ref, f32[2,6,144,128]{3,2,1,0:T(8,128)S(1)} %get-tuple-element.36.one_in_ref.one_a_ref, ...), custom_call_target="tpu_custom_call" | custom-call | flops 67108864 | bytes 4194304 | tf_op jit(solution)/shard_map/pallas_call | solution.py:570
  23.4 0.3 collective-permute-start.5
  23.7 0.0 collective-permute-done.6.got_b_ref
  23.7 1.1 %collective-permute-done.5.got_a_ref = f32[2,2,64,128]{3,2,1,0:T(8,128)S(1)} collective-permute-done((f32[2,2,64,128]{3,2,1,0:T(8,128)S(1)}, f32[2,2,64,128]{3,2,1,0:T(8,128)S(1)}, u32[]{:S(2)}, u32[]{:S(2)}) %collective-permute-start.5) | collective-permute-done | bytes 131104 | tf_op jit(solution)/shard_map/ppermute | solution.py:582
  24.8 2.0 %collective-permute-start.7 = (f32[1,4,64,128]{3,2,1,0:T(8,128)S(1)}, f32[1,4,64,128]{3,2,1,0:T(8,128)S(1)}, u32[]{:S(2)}, u32[]{:S(2)}) collective-permute-start(f32[1,4,64,128]{3,2,1,0:T(8,128)S(1)} %get-tuple-element.45), channel_id=1, source_target_pairs={{0,2},{1,3},{2,0},{3,1},{4,6},{5,7},{6,4},{7,5},{8,10},{9,11},{10,... | collective-permute-start | bytes 393224 | tf_op jit(solution)/shard_map/ppermute | solution.py:599
  26.8 1.0 %shard_map.119 = f32[1,2,4,256,128]{4,3,2,1,0:T(8,128)} custom-call(f32[2,8,144,128]{3,2,1,0:T(8,128)S(1)} %get-tuple-element.29.zero_in_ref.near_ref, f32[2,4,144,128]{3,2,1,0:T(8,128)S(1)} %get-tuple-element.35.zero_in_ref.zero_a_ref, f32[2,6,144,128]{3,2,1,0:T(8,128)S(1)} %get-tuple-element.36.one_in_ref.one_a_ref, ...), custom_call_target="tpu_custom_call" | custom-call | flops 1048576 | bytes 4194304 | tf_op jit(solution)/shard_map/pallas_call | solution.py:584
  27.9 3.0 %collective-permute-done.7 = f32[1,4,64,128]{3,2,1,0:T(8,128)S(1)} collective-permute-done((f32[1,4,64,128]{3,2,1,0:T(8,128)S(1)}, f32[1,4,64,128]{3,2,1,0:T(8,128)S(1)}, u32[]{:S(2)}, u32[]{:S(2)}) %collective-permute-start.7) | collective-permute-done | bytes 131104 | tf_op jit(solution)/shard_map/ppermute | solution.py:599
  30.9 0.7 %add_bitcast_fusion = f32[4,64,128]{2,1,0:T(8,128)} fusion(f32[1,4,64,128]{3,2,1,0:T(8,128)S(1)} %get-tuple-element.44, f32[1,4,64,128]{3,2,1,0:T(8,128)S(1)} %collective-permute-done.7), kind=kLoop, calls=%fused_computation | loop fusion | flops 32768 | bytes 393216 | tf_op jit(solution)/shard_map/squeeze | solution.py:604
  (3 shorter events, 0.0 us)
Async XLA Ops:
  1.7 9.8 %collective-permute-start.1 = (f32[5,128,128]{2,1,0:T(8,128)S(1)}, f32[5,128,128]{2,1,0:T(8,128)S(1)}, u32[]{:S(2)}, u32[]{:S(2)}) collective-permute-start(f32[5,128,128]{2,1,0:T(8,128)S(1)} %shard_map.114), channel_id=1, source_target_pairs={{0,4},{1,3},{2,6},{3,1},{4,0},{5,9},{6,2},{7,11},{8,12},{9,5},{10,... | collective-permute-start | bytes 983048 | tf_op jit(solution)/shard_map/ppermute | solution.py:520
  6.1 13.9 %collective-permute-start = (f32[2,4,128,128]{3,2,1,0:T(8,128)S(1)}, f32[2,4,128,128]{3,2,1,0:T(8,128)S(1)}, u32[]{:S(2)}, u32[]{:S(2)}) collective-permute-start(f32[2,4,128,128]{3,2,1,0:T(8,128)S(1)} %get-tuple-element.24.adj_ref), channel_id=1, source_target_pairs={{0,2},{1,5},{2,0},{3,7},{4,8},{5,1},{6,10},{7,3},{8,4},{9,13},{10,... | collective-permute-start | bytes 1572872 | tf_op jit(solution)/shard_map/ppermute | solution.py:521
  11.5 8.5 %collective-permute-start.2 = (f32[5,128,128]{2,1,0:T(8,128)S(1)}, f32[5,128,128]{2,1,0:T(8,128)S(1)}, u32[]{:S(2)}, u32[]{:S(2)}) collective-permute-start(f32[5,128,128]{2,1,0:T(8,128)S(1)} %collective-permute-done.1.far_cells_ref), channel_id=1, source_target_pairs={{0,1},{1,0},{2,3},{3,2},{4,5},{5,4},{6,7},{7,6},{8,9},{9,8},{10,11... | collective-permute-start | bytes 983048 | tf_op jit(solution)/shard_map/ppermute | solution.py:553
  11.5 9.8 %collective-permute-start.3 = (f32[2,2,128,128]{3,2,1,0:T(8,128)S(1)}, f32[2,2,128,128]{3,2,1,0:T(8,128)S(1)}, u32[]{:S(2)}, u32[]{:S(2)}) collective-permute-start(f32[2,2,128,128]{3,2,1,0:T(8,128)S(1)} %get-tuple-element.31), channel_id=1, source_target_pairs={{0,4},{1,3},{2,6},{3,1},{4,0},{5,9},{6,2},{7,11},{8,12},{9,5},{10,... | collective-permute-start | bytes 786440 | tf_op jit(solution)/shard_map/ppermute | solution.py:522
  13.9 8.7 %collective-permute-start.4 = (f32[2,2,128,128]{3,2,1,0:T(8,128)S(1)}, f32[2,2,128,128]{3,2,1,0:T(8,128)S(1)}, u32[]{:S(2)}, u32[]{:S(2)}) collective-permute-start(f32[2,2,128,128]{3,2,1,0:T(8,128)S(1)} %get-tuple-element.37), channel_id=1, source_target_pairs={{0,4},{1,3},{2,6},{3,1},{4,0},{5,9},{6,2},{7,11},{8,12},{9,5},{10,... | collective-permute-start | bytes 786440 | tf_op jit(solution)/shard_map/ppermute | solution.py:523
  20.0 1.3 %copy-start = (f32[1,2,4,256,128]{4,3,2,1,0:T(8,128)S(1)}, f32[1,2,4,256,128]{4,3,2,1,0:T(8,128)}, u32[]{:S(2)}) copy-start(f32[1,2,4,256,128]{4,3,2,1,0:T(8,128)} %forward_ref.3) | copy-start | bytes 3145732
  22.2 1.5 %collective-permute-start.6 = (f32[2,2,64,128]{3,2,1,0:T(8,128)S(1)}, f32[2,2,64,128]{3,2,1,0:T(8,128)S(1)}, u32[]{:S(2)}, u32[]{:S(2)}) collective-permute-start(f32[2,2,64,128]{3,2,1,0:T(8,128)S(1)} %get-tuple-element.43), channel_id=1, source_target_pairs={{0,1},{1,0},{2,3},{3,2},{4,5},{5,4},{6,7},{7,6},{8,9},{9,8},{10,11... | collective-permute-start | bytes 393224 | tf_op jit(solution)/shard_map/ppermute | solution.py:580
  23.4 1.4 %collective-permute-start.5 = (f32[2,2,64,128]{3,2,1,0:T(8,128)S(1)}, f32[2,2,64,128]{3,2,1,0:T(8,128)S(1)}, u32[]{:S(2)}, u32[]{:S(2)}) collective-permute-start(f32[2,2,64,128]{3,2,1,0:T(8,128)S(1)} %get-tuple-element.41), channel_id=1, source_target_pairs={{0,1},{1,0},{2,3},{3,2},{4,5},{5,4},{6,7},{7,6},{8,9},{9,8},{10,11... | collective-permute-start | bytes 393224 | tf_op jit(solution)/shard_map/ppermute | solution.py:582
  24.8 6.0 %collective-permute-start.7 = (f32[1,4,64,128]{3,2,1,0:T(8,128)S(1)}, f32[1,4,64,128]{3,2,1,0:T(8,128)S(1)}, u32[]{:S(2)}, u32[]{:S(2)}) collective-permute-start(f32[1,4,64,128]{3,2,1,0:T(8,128)S(1)} %get-tuple-element.45), channel_id=1, source_target_pairs={{0,2},{1,3},{2,0},{3,1},{4,6},{5,7},{6,4},{7,5},{8,10},{9,11},{10,... | collective-permute-start | bytes 393224 | tf_op jit(solution)/shard_map/ppermute | solution.py:599

commit v6 on v5

--- a/solution.py
+++ b/solution.py
@@ -429,14 +429,18 @@
         copy.wait()
 
 
-def join_kernel(keep_a_ref, got_a_ref, keep_b_ref, got_b_ref, send_ref, keep_ref):
-    depth = keep_a_ref.shape[1]
-    begun = jnp.where(near_on_right(), depth, 0)
-    for i in range(keep_a_ref.shape[0]):
+def join_kernel(keep_in_ref, got_ref, send_ref, keep_ref):
+    for i in range(keep_in_ref.shape[0]):
         ref = send_ref if i % 2 else keep_ref
-        for d in range(depth):
-            ref[i // 2, begun + d] = keep_a_ref[i, d] + got_a_ref[i, d]
-            ref[i // 2, depth - begun + d] = keep_b_ref[i, d] + got_b_ref[i, d]
+        ref[i // 2] = keep_in_ref[i] + got_ref[i]
+
+
+def finish_kernel(begun_ref, begun_got_ref, ended_ref, ended_got_ref, out_ref):
+    depth = begun_ref.shape[1]
+    base = jnp.where(near_on_right(), depth, 0)
+    for d in range(depth):
+        out_ref[base + d] = begun_ref[0, d] + begun_got_ref[0, d]
+        out_ref[depth - base + d] = ended_ref[0, d] + ended_got_ref[0, d]
 
 
 def call(kernel, outs, scratch, specs, out_specs, flops, room=8):
@@ -590,18 +594,26 @@
         1 << 20,
     )(zero, zero_a, one_a, zero_b, one_b)
 
-    joined = (shards // 4, layers, shard_rows, size_z)
-    send, keep = call(
-        join_kernel, [joined, joined], [], [VMEM] * 4, [VMEM] * 2, 1 << 20
-    )(keep_a, got_a, keep_b, got_b)
-    bit = 2
-    while True:
-        keep = keep + lax.ppermute(send, "src", [(i, i ^ bit) for i in range(shards)])
-        bit *= 2
-        if bit == shards:
-            break
-        send, keep = keep[1::2], keep[0::2]
-    return (field, keep[0])
+    def join(keep, got):
+        joined = (shards // 4, depth, shard_rows, size_z)
+        return call(join_kernel, [joined, joined], [], [VMEM] * 2, [VMEM] * 2, 1 << 20)(keep, got)
+
+    def add_up(send, keep):
+        bit = 2
+        while True:
+            got = lax.ppermute(send, "src", [(i, i ^ bit) for i in range(shards)])
+            bit *= 2
+            if bit == shards:
+                return keep, got
+            keep = keep + got
+            send, keep = keep[1::2], keep[0::2]
+
+    ended = add_up(*join(keep_b, got_b))
+    begun = add_up(*join(keep_a, got_a))
+    (gradient,) = call(
+        finish_kernel, [(layers, shard_rows, size_z)], [], [VMEM] * 4, [VMEM], 1 << 20
+    )(*begun, *ended)
+    return (field, gradient)
 
 
 def solution(mesh):

time: 31.7 us -> 31.1 us (0.981)
  waiting for transfers between devices: 8 us -> 6.21 us
  starting transfers between devices: 9.7 us -> 10.8 us
  other arithmetic: 0.67 us -> 0 us
  Pallas kernels: 11.8 us -> 12.4 us
    ppermute x1, waiting for transfers between devices: 1.14 us -> 0.01 us  [body(): got_a = lax.ppermute(send_b, 'src', flip)]
    ppermute x1 -> x2, starting transfers between devices: 1.99 us -> 3.1 us  [add_up(): got = lax.ppermute(send, 'src', [(i, i ^ bit) for i in range(shards)])]
    squeeze x1 -> x0, other arithmetic: 0.67 us -> none  [body(): return (field, keep[0])]
    pallas_call x1 -> x3, Pallas kernels: 0.04 us -> 0.7 us  [the longest x1 0.67 us: body(): call(finish_kernel, [(layers, shard_rows, size_z)], [], [VMEM] * 4, [VMEM...]
    ppermute x1 -> x2, waiting for transfers between devices: 2.99 us -> 2.34 us  [add_up(): got = lax.ppermute(send, 'src', [(i, i ^ bit) for i in range(shards)])]
  transfers between devices with their start and end apart: 8 -> 9, of which waited for: 3 -> 3; matrix products, arithmetic and copies ran while one was open for 0% -> 0% of each run, Pallas kernels for 34% -> 35%
where the time goes in v6:
time: 31.1 us; the launch traced here: 30.9 us
  Pallas kernels  12.4 us (40%)
  starting transfers between devices  10.8 us (35%)
  waiting for transfers between devices  6.21 us (20%)
  between operations  1.38 us (4%)
    pallas_call x1, Pallas kernels, body(): call(source_kernel, [(2, 2, reach, half, size_z), (2, layers, half, size_...  5.41 us
    ppermute x1, waiting for transfers between devices, body(): far_cells = lax.ppermute(cells_out, both, to_far)  3.86 us
    ppermute x1, starting transfers between devices, body(): far_cells = lax.ppermute(cells_out, both, to_far)  3.12 us
    ppermute x2, starting transfers between devices, add_up(): got = lax.ppermute(send, 'src', [(i, i ^ bit) for i in range(shards)])  3.1 us
    ppermute x1, starting transfers between devices, body(): first_halo = lax.ppermute(adj_first, both, to_far)  2.38 us
    ppermute x2, waiting for transfers between devices, add_up(): got = lax.ppermute(send, 'src', [(i, i ^ bit) for i in range(shards)])  2.34 us
    pallas_call x2, Pallas kernels, far(): call(kernel, [state_zero, state_one, part_shape, part_shape], [], [VMEM]...  1.67 us
    ppermute x1, starting transfers between devices, body(): near_halo = lax.ppermute(adj, both, to_near)  1.56 us
  transfers between devices with their start and end apart: 9, of which 3 were waited for; matrix products, arithmetic and copies ran while one was open for 0% of the time, Pallas kernels for 35%

profile of v6, /device:TPU:0, one launch (start us, length us, event | category | flops | bytes accessed | tf_op | source)
XLA Modules:
  0.0 30.9 jit_solution(11797448175078213254)
XLA Ops:
  0.6 1.1 %shard_map.114 = f32[5,128,128]{2,1,0:T(8,128)S(1)} custom-call(f32[4,256,128]{2,1,0:T(8,128)} %cond_hbm.3), custom_call_target="tpu_custom_call" | custom-call | flops 1048576 | bytes 4194304 | tf_op jit(solution)/shard_map/pallas_call | solution.py:513
  1.7 3.1 %collective-permute-start.1 = (f32[5,128,128]{2,1,0:T(8,128)S(1)}, f32[5,128,128]{2,1,0:T(8,128)S(1)}, u32[]{:S(2)}, u32[]{:S(2)}) collective-permute-start(f32[5,128,128]{2,1,0:T(8,128)S(1)} %shard_map.114), channel_id=1, source_target_pairs={{0,4},{1,3},{2,6},{3,1},{4,0},{5,9},{6,2},{7,11},{8,12},{9,5},{10,... | collective-permute-start | bytes 983048 | tf_op jit(solution)/shard_map/ppermute | solution.py:524
  4.8 1.3 %shard_map.113 = (f32[2,4,128,128]{3,2,1,0:T(8,128)S(1)}, f32[2,2,128,128]{3,2,1,0:T(8,128)S(1)}, f32[2,2,128,128]{3,2,1,0:T(8,128)S(1)}) custom-call(f32[1,2,4,256,128]{4,3,2,1,0:T(8,128)} %guess_hbm.1), custom_call_target="tpu_custom_call" | custom-call | flops 1048576 | bytes 4194304 | tf_op jit(solution)/shard_map/pallas_call | solution.py:505
  6.1 1.6 %collective-permute-start = (f32[2,4,128,128]{3,2,1,0:T(8,128)S(1)}, f32[2,4,128,128]{3,2,1,0:T(8,128)S(1)}, u32[]{:S(2)}, u32[]{:S(2)}) collective-permute-start(f32[2,4,128,128]{3,2,1,0:T(8,128)S(1)} %get-tuple-element.26.adj_ref), channel_id=1, source_target_pairs={{0,2},{1,5},{2,0},{3,7},{4,8},{5,1},{6,10},{7,3},{8,4},{9,13},{10,... | collective-permute-start | bytes 1572872 | tf_op jit(solution)/shard_map/ppermute | solution.py:525
  7.6 3.9 %collective-permute-done.1.far_cells_ref = f32[5,128,128]{2,1,0:T(8,128)S(1)} collective-permute-done((f32[5,128,128]{2,1,0:T(8,128)S(1)}, f32[5,128,128]{2,1,0:T(8,128)S(1)}, u32[]{:S(2)}, u32[]{:S(2)}) %collective-permute-start.1) | collective-permute-done | bytes 327712 | tf_op jit(solution)/shard_map/ppermute | solution.py:524
  11.5 0.0 collective-permute-start.2
  11.5 2.4 %collective-permute-start.3 = (f32[2,2,128,128]{3,2,1,0:T(8,128)S(1)}, f32[2,2,128,128]{3,2,1,0:T(8,128)S(1)}, u32[]{:S(2)}, u32[]{:S(2)}) collective-permute-start(f32[2,2,128,128]{3,2,1,0:T(8,128)S(1)} %get-tuple-element.33), channel_id=1, source_target_pairs={{0,4},{1,3},{2,6},{3,1},{4,0},{5,9},{6,2},{7,11},{8,12},{9,5},{10,... | collective-permute-start | bytes 786440 | tf_op jit(solution)/shard_map/ppermute | solution.py:526
  13.9 0.0 collective-permute-start.4
  14.6 5.4 %shard_map.115 = (f32[2,2,10,128,128]{4,3,2,1,0:T(8,128)S(1)}, f32[2,4,128,128]{3,2,1,0:T(8,128)S(1)}, f32[2,4,128,128]{3,2,1,0:T(8,128)S(1)}, f32[4,256,128]{2,1,0:T(8,128)S(1)}, f32[8,128]{1,0:T(8,128)S(1)}) custom-call(s32[256]{0:T(256)} %x_hbm.1, s32[256]{0:T(256)} %y_hbm.1, s32[256]{0:T(256)} %z_hbm.1, f32[4]{0:T(128)} %kappas_hbm.1, ...), custom_call_target="tpu_custom_call" | custom-call | flops 1073741824 | bytes 4194304 | tf_op jit(solution)/shard_map/pallas_call | solution.py:529
  20.0 0.0 collective-permute-done.2.near_cells_ref
  20.0 0.0 copy-start
  20.0 1.3 %shard_map.116 = (f32[2,8,144,128]{3,2,1,0:T(8,128)S(1)}, f32[2,8,144,128]{3,2,1,0:T(8,128)S(1)}, f32[2,12,128,128]{3,2,1,0:T(8,128)S(1)}, f32[2,12,128,128]{3,2,1,0:T(8,128)S(1)}) custom-call(f32[2,4,128,128]{3,2,1,0:T(8,128)S(1)} %get-tuple-element.26.adj_ref, f32[2,4,128,128]{3,2,1,0:T(8,128)S(1)} %collective-permute-done.halo_ref, ...), custom_call_target="tpu_custom_call" | custom-call | flops 67108864 | bytes 4194304 | tf_op jit(solution)/shard_map/pallas_call | solution.py:561
  21.3 0.0 collective-permute-done.3.halo_ref
  21.3 0.9 %shard_map.117 = (f32[2,4,144,128]{3,2,1,0:T(8,128)S(1)}, f32[2,6,144,128]{3,2,1,0:T(8,128)S(1)}, f32[2,2,64,128]{3,2,1,0:T(8,128)S(1)}, f32[2,2,64,128]{3,2,1,0:T(8,128)S(1)}) custom-call(f32[2,8,144,128]{3,2,1,0:T(8,128)S(1)} %get-tuple-element.31.zero_in_ref.near_ref, f32[2,8,144,128]{3,2,1,0:T(8,128)S(1)} %get-tuple-element.32.one_in_ref, ...), custom_call_target="tpu_custom_call" | custom-call | flops 67108864 | bytes 4194304 | tf_op jit(solution)/shard_map/pallas_call | solution.py:574
  22.2 0.4 %collective-permute-start.7 = (f32[2,2,64,128]{3,2,1,0:T(8,128)S(1)}, f32[2,2,64,128]{3,2,1,0:T(8,128)S(1)}, u32[]{:S(2)}, u32[]{:S(2)}) collective-permute-start(f32[2,2,64,128]{3,2,1,0:T(8,128)S(1)} %get-tuple-element.47), channel_id=1, source_target_pairs={{0,1},{1,0},{2,3},{3,2},{4,5},{5,4},{6,7},{7,6},{8,9},{9,8},{10,11... | collective-permute-start | bytes 393224 | tf_op jit(solution)/shard_map/ppermute | solution.py:584
  22.6 0.0 collective-permute-done.4.halo_ref
  22.6 0.8 %shard_map.118 = (f32[2,4,144,128]{3,2,1,0:T(8,128)S(1)}, f32[2,6,144,128]{3,2,1,0:T(8,128)S(1)}, f32[2,2,64,128]{3,2,1,0:T(8,128)S(1)}, f32[2,2,64,128]{3,2,1,0:T(8,128)S(1)}) custom-call(f32[2,4,144,128]{3,2,1,0:T(8,128)S(1)} %get-tuple-element.37.zero_in_ref.zero_a_ref, f32[2,6,144,128]{3,2,1,0:T(8,128)S(1)} %get-tuple-element.38.one_in_ref.one_a_ref, ...), custom_call_target="tpu_custom_call" | custom-call | flops 67108864 | bytes 4194304 | tf_op jit(solution)/shard_map/pallas_call | solution.py:574
  23.4 0.3 collective-permute-start.5
  23.7 2.1 %collective-permute-start.8 = (f32[1,2,64,128]{3,2,1,0:T(8,128)S(1)}, f32[1,2,64,128]{3,2,1,0:T(8,128)S(1)}, u32[]{:S(2)}, u32[]{:S(2)}) collective-permute-start(f32[1,2,64,128]{3,2,1,0:T(8,128)S(1)} %get-tuple-element.49), channel_id=1, source_target_pairs={{0,2},{1,3},{2,0},{3,1},{4,6},{5,7},{6,4},{7,5},{8,10},{9,11},{10,... | collective-permute-start | bytes 196616 | tf_op jit(solution)/shard_map/ppermute | solution.py:604
  25.9 1.0 %collective-permute-start.6 = (f32[1,2,64,128]{3,2,1,0:T(8,128)S(1)}, f32[1,2,64,128]{3,2,1,0:T(8,128)S(1)}, u32[]{:S(2)}, u32[]{:S(2)}) collective-permute-start(f32[1,2,64,128]{3,2,1,0:T(8,128)S(1)} %get-tuple-element.45), channel_id=1, source_target_pairs={{0,2},{1,3},{2,0},{3,1},{4,6},{5,7},{6,4},{7,5},{8,10},{9,11},{10,... | collective-permute-start | bytes 196616 | tf_op jit(solution)/shard_map/ppermute | solution.py:604
  26.8 1.0 %shard_map.119 = f32[1,2,4,256,128]{4,3,2,1,0:T(8,128)} custom-call(f32[2,8,144,128]{3,2,1,0:T(8,128)S(1)} %get-tuple-element.31.zero_in_ref.near_ref, f32[2,4,144,128]{3,2,1,0:T(8,128)S(1)} %get-tuple-element.37.zero_in_ref.zero_a_ref, f32[2,6,144,128]{3,2,1,0:T(8,128)S(1)} %get-tuple-element.38.one_in_ref.one_a_ref, ...), custom_call_target="tpu_custom_call" | custom-call | flops 1048576 | bytes 4194304 | tf_op jit(solution)/shard_map/pallas_call | solution.py:588
  27.8 0.3 %collective-permute-done.8.ended_got_ref = f32[1,2,64,128]{3,2,1,0:T(8,128)S(1)} collective-permute-done((f32[1,2,64,128]{3,2,1,0:T(8,128)S(1)}, f32[1,2,64,128]{3,2,1,0:T(8,128)S(1)}, u32[]{:S(2)}, u32[]{:S(2)}) %collective-permute-start.8) | collective-permute-done | bytes 65568 | tf_op jit(solution)/shard_map/ppermute | solution.py:604
  28.2 2.0 %collective-permute-done.6.begun_got_ref = f32[1,2,64,128]{3,2,1,0:T(8,128)S(1)} collective-permute-done((f32[1,2,64,128]{3,2,1,0:T(8,128)S(1)}, f32[1,2,64,128]{3,2,1,0:T(8,128)S(1)}, u32[]{:S(2)}, u32[]{:S(2)}) %collective-permute-start.6) | collective-permute-done | bytes 65568 | tf_op jit(solution)/shard_map/ppermute | solution.py:604
  30.2 0.7 %shard_map.122 = f32[4,64,128]{2,1,0:T(8,128)} custom-call(f32[1,2,64,128]{3,2,1,0:T(8,128)S(1)} %get-tuple-element.44.begun_ref, f32[1,2,64,128]{3,2,1,0:T(8,128)S(1)} %collective-permute-done.6.begun_got_ref, f32[1,2,64,128]{3,2,1,0:T(8,128)S(1)} %get-tuple-element.48.ended_ref, f32[1,2,64,128]{3,2,1,0:T(8,128)S(1)} %collective-permute-done.8.ended_got_ref), custom_call_target="tpu_custom_call" | custom-call | flops 1048576 | bytes 4194304 | tf_op jit(solution)/shard_map/pallas_call | solution.py:613
  (6 shorter events, 0.0 us)
Async XLA Ops:
  1.7 9.8 %collective-permute-start.1 = (f32[5,128,128]{2,1,0:T(8,128)S(1)}, f32[5,128,128]{2,1,0:T(8,128)S(1)}, u32[]{:S(2)}, u32[]{:S(2)}) collective-permute-start(f32[5,128,128]{2,1,0:T(8,128)S(1)} %shard_map.114), channel_id=1, source_target_pairs={{0,4},{1,3},{2,6},{3,1},{4,0},{5,9},{6,2},{7,11},{8,12},{9,5},{10,... | collective-permute-start | bytes 983048 | tf_op jit(solution)/shard_map/ppermute | solution.py:524
  6.1 13.9 %collective-permute-start = (f32[2,4,128,128]{3,2,1,0:T(8,128)S(1)}, f32[2,4,128,128]{3,2,1,0:T(8,128)S(1)}, u32[]{:S(2)}, u32[]{:S(2)}) collective-permute-start(f32[2,4,128,128]{3,2,1,0:T(8,128)S(1)} %get-tuple-element.26.adj_ref), channel_id=1, source_target_pairs={{0,2},{1,5},{2,0},{3,7},{4,8},{5,1},{6,10},{7,3},{8,4},{9,13},{10,... | collective-permute-start | bytes 1572872 | tf_op jit(solution)/shard_map/ppermute | solution.py:525
  11.5 8.5 %collective-permute-start.2 = (f32[5,128,128]{2,1,0:T(8,128)S(1)}, f32[5,128,128]{2,1,0:T(8,128)S(1)}, u32[]{:S(2)}, u32[]{:S(2)}) collective-permute-start(f32[5,128,128]{2,1,0:T(8,128)S(1)} %collective-permute-done.1.far_cells_ref), channel_id=1, source_target_pairs={{0,1},{1,0},{2,3},{3,2},{4,5},{5,4},{6,7},{7,6},{8,9},{9,8},{10,11... | collective-permute-start | bytes 983048 | tf_op jit(solution)/shard_map/ppermute | solution.py:557
  11.5 9.8 %collective-permute-start.3 = (f32[2,2,128,128]{3,2,1,0:T(8,128)S(1)}, f32[2,2,128,128]{3,2,1,0:T(8,128)S(1)}, u32[]{:S(2)}, u32[]{:S(2)}) collective-permute-start(f32[2,2,128,128]{3,2,1,0:T(8,128)S(1)} %get-tuple-element.33), channel_id=1, source_target_pairs={{0,4},{1,3},{2,6},{3,1},{4,0},{5,9},{6,2},{7,11},{8,12},{9,5},{10,... | collective-permute-start | bytes 786440 | tf_op jit(solution)/shard_map/ppermute | solution.py:526
  13.9 8.7 %collective-permute-start.4 = (f32[2,2,128,128]{3,2,1,0:T(8,128)S(1)}, f32[2,2,128,128]{3,2,1,0:T(8,128)S(1)}, u32[]{:S(2)}, u32[]{:S(2)}) collective-permute-start(f32[2,2,128,128]{3,2,1,0:T(8,128)S(1)} %get-tuple-element.39), channel_id=1, source_target_pairs={{0,4},{1,3},{2,6},{3,1},{4,0},{5,9},{6,2},{7,11},{8,12},{9,5},{10,... | collective-permute-start | bytes 786440 | tf_op jit(solution)/shard_map/ppermute | solution.py:527
  20.0 1.3 %copy-start = (f32[1,2,4,256,128]{4,3,2,1,0:T(8,128)S(1)}, f32[1,2,4,256,128]{4,3,2,1,0:T(8,128)}, u32[]{:S(2)}) copy-start(f32[1,2,4,256,128]{4,3,2,1,0:T(8,128)} %forward_ref.3) | copy-start | bytes 3145732
  22.2 1.5 %collective-permute-start.7 = (f32[2,2,64,128]{3,2,1,0:T(8,128)S(1)}, f32[2,2,64,128]{3,2,1,0:T(8,128)S(1)}, u32[]{:S(2)}, u32[]{:S(2)}) collective-permute-start(f32[2,2,64,128]{3,2,1,0:T(8,128)S(1)} %get-tuple-element.47), channel_id=1, source_target_pairs={{0,1},{1,0},{2,3},{3,2},{4,5},{5,4},{6,7},{7,6},{8,9},{9,8},{10,11... | collective-permute-start | bytes 393224 | tf_op jit(solution)/shard_map/ppermute | solution.py:584
  23.4 2.4 %collective-permute-start.5 = (f32[2,2,64,128]{3,2,1,0:T(8,128)S(1)}, f32[2,2,64,128]{3,2,1,0:T(8,128)S(1)}, u32[]{:S(2)}, u32[]{:S(2)}) collective-permute-start(f32[2,2,64,128]{3,2,1,0:T(8,128)S(1)} %get-tuple-element.43), channel_id=1, source_target_pairs={{0,1},{1,0},{2,3},{3,2},{4,5},{5,4},{6,7},{7,6},{8,9},{9,8},{10,11... | collective-permute-start | bytes 393224 | tf_op jit(solution)/shard_map/ppermute | solution.py:586
  23.7 4.5 %collective-permute-start.8 = (f32[1,2,64,128]{3,2,1,0:T(8,128)S(1)}, f32[1,2,64,128]{3,2,1,0:T(8,128)S(1)}, u32[]{:S(2)}, u32[]{:S(2)}) collective-permute-start(f32[1,2,64,128]{3,2,1,0:T(8,128)S(1)} %get-tuple-element.49), channel_id=1, source_target_pairs={{0,2},{1,3},{2,0},{3,1},{4,6},{5,7},{6,4},{7,5},{8,10},{9,11},{10,... | collective-permute-start | bytes 196616 | tf_op jit(solution)/shard_map/ppermute | solution.py:604
  25.9 4.3 %collective-permute-start.6 = (f32[1,2,64,128]{3,2,1,0:T(8,128)S(1)}, f32[1,2,64,128]{3,2,1,0:T(8,128)S(1)}, u32[]{:S(2)}, u32[]{:S(2)}) collective-permute-start(f32[1,2,64,128]{3,2,1,0:T(8,128)S(1)} %get-tuple-element.45), channel_id=1, source_target_pairs={{0,2},{1,3},{2,0},{3,1},{4,6},{5,7},{6,4},{7,5},{8,10},{9,11},{10,... | collective-permute-start | bytes 196616 | tf_op jit(solution)/shard_map/ppermute | solution.py:604

commit v7 on v6

--- a/solution.py
+++ b/solution.py
@@ -463,18 +463,19 @@
     return [pltpu.VMEM(s, jnp.float32) for s in shapes]
 
 
-def swaps(tiles, shards, odd_of):
+def swaps(jobs, tiles, shards, odd_of, spare):
     pairs = []
-    for t in range(tiles):
-        for s in range(shards):
-            other = (t + 1 ^ 1) - 1 if odd_of(s) else t ^ 1
-            to = (other, s) if 0 <= other < tiles else (t, spare(s, shards, odd_of))
-            pairs.append((t * shards + s, to[0] * shards + to[1]))
+    for j in range(jobs):
+        for t in range(tiles):
+            for s in range(shards):
+                other = (t + 1 ^ 1) - 1 if odd_of(s) else t ^ 1
+                to = (j, other, s)
+                if not 0 <= other < tiles:
+                    k, u = spare(j, s)
+                    to = (k, t, u)
+                to = (to[0] * tiles + to[1]) * shards + to[2]
+                pairs.append(((j * tiles + t) * shards + s, to))
     return pairs
-
-
-def spare(s, shards, odd_of):
-    return next((o for o in (s ^ 1, s ^ 2) if o < shards and odd_of(o) == odd_of(s)), s)
 
 
 def body(
@@ -518,13 +519,15 @@
         [VMEM],
         1 << 20,
     )(in_hbm(conductivity))
-    both = ("tile", "src")
-    to_near = swaps(tiles, shards, is_even)
-    to_far = swaps(tiles, shards, is_odd)
-    far_cells = lax.ppermute(cells_out, both, to_far)
-    near_halo = lax.ppermute(adj, both, to_near)
-    first_halo = lax.ppermute(adj_first, both, to_far)
-    second_halo = lax.ppermute(adj_second, both, to_far)
+    every = ("job", "tile", "src")
+    jobs = lax.axis_size("job")
+    unused = (lambda j, s: (j, s ^ 2)) if jobs % 2 else (lambda j, s: (j ^ 1, s))
+    to_near = swaps(jobs, tiles, shards, is_even, lambda j, s: (j, s ^ 2))
+    to_far = swaps(jobs, tiles, shards, is_odd, unused)
+    far_cells = lax.ppermute(cells_out, every, to_far)
+    near_halo = lax.ppermute(adj, every, to_near)
+    first_halo = lax.ppermute(adj_first, every, to_far)
+    second_halo = lax.ppermute(adj_second, every, to_far)
 
     source, six_own, cross_own, scale, kappa = call(
         source_kernel,

time: 31.1 us -> 31 us (level)
  no operation moved by 1% of the time
where the time goes in v7:
time: 31 us; the launch traced here: 30.7 us
  Pallas kernels  12.4 us (40%)
  starting transfers between devices  10.7 us (35%)
  waiting for transfers between devices  6.19 us (20%)
  between operations  1.38 us (4%)
    pallas_call x1, Pallas kernels, body(): call(source_kernel, [(2, 2, reach, half, size_z), (2, layers, half, size_...  5.41 us
    ppermute x1, waiting for transfers between devices, body(): far_cells = lax.ppermute(cells_out, every, to_far)  3.83 us
    ppermute x1, starting transfers between devices, body(): far_cells = lax.ppermute(cells_out, every, to_far)  3.12 us
    ppermute x2, starting transfers between devices, add_up(): got = lax.ppermute(send, 'src', [(i, i ^ bit) for i in range(shards)])  2.99 us
    ppermute x1, starting transfers between devices, body(): first_halo = lax.ppermute(adj_first, every, to_far)  2.41 us
    ppermute x2, waiting for transfers between devices, add_up(): got = lax.ppermute(send, 'src', [(i, i ^ bit) for i in range(shards)])  2.34 us
    pallas_call x2, Pallas kernels, far(): call(kernel, [state_zero, state_one, part_shape, part_shape], [], [VMEM]...  1.67 us
    ppermute x1, starting transfers between devices, body(): near_halo = lax.ppermute(adj, every, to_near)  1.56 us
  transfers between devices with their start and end apart: 9, of which 3 were waited for; matrix products, arithmetic and copies ran while one was open for 0% of the time, Pallas kernels for 35%

profile of v7, /device:TPU:0, one launch (start us, length us, event | category | flops | bytes accessed | tf_op | source)
XLA Modules:
  0.0 30.7 jit_solution(5211822670885433)
XLA Ops:
  0.6 1.1 %shard_map.114 = f32[5,128,128]{2,1,0:T(8,128)S(1)} custom-call(f32[4,256,128]{2,1,0:T(8,128)} %cond_hbm.3), custom_call_target="tpu_custom_call" | custom-call | flops 1048576 | bytes 4194304 | tf_op jit(solution)/shard_map/pallas_call | solution.py:514
  1.7 3.1 %collective-permute-start.1 = (f32[5,128,128]{2,1,0:T(8,128)S(1)}, f32[5,128,128]{2,1,0:T(8,128)S(1)}, u32[]{:S(2)}, u32[]{:S(2)}) collective-permute-start(f32[5,128,128]{2,1,0:T(8,128)S(1)} %shard_map.114), channel_id=1, source_target_pairs={{0,4},{1,17},{2,6},{3,19},{4,0},{5,9},{6,2},{7,11},{8,12},{9,5},{1... | collective-permute-start | bytes 983048 | tf_op jit(solution)/shard_map/ppermute | solution.py:527
  4.8 1.3 %shard_map.113 = (f32[2,4,128,128]{3,2,1,0:T(8,128)S(1)}, f32[2,2,128,128]{3,2,1,0:T(8,128)S(1)}, f32[2,2,128,128]{3,2,1,0:T(8,128)S(1)}) custom-call(f32[1,2,4,256,128]{4,3,2,1,0:T(8,128)} %guess_hbm.1), custom_call_target="tpu_custom_call" | custom-call | flops 1048576 | bytes 4194304 | tf_op jit(solution)/shard_map/pallas_call | solution.py:506
  6.1 1.6 %collective-permute-start = (f32[2,4,128,128]{3,2,1,0:T(8,128)S(1)}, f32[2,4,128,128]{3,2,1,0:T(8,128)S(1)}, u32[]{:S(2)}, u32[]{:S(2)}) collective-permute-start(f32[2,4,128,128]{3,2,1,0:T(8,128)S(1)} %get-tuple-element.26.adj_ref), channel_id=1, source_target_pairs={{0,2},{1,5},{2,0},{3,7},{4,8},{5,1},{6,10},{7,3},{8,4},{9,13},{10,... | collective-permute-start | bytes 1572872 | tf_op jit(solution)/shard_map/ppermute | solution.py:528
  7.6 3.8 %collective-permute-done.1.far_cells_ref = f32[5,128,128]{2,1,0:T(8,128)S(1)} collective-permute-done((f32[5,128,128]{2,1,0:T(8,128)S(1)}, f32[5,128,128]{2,1,0:T(8,128)S(1)}, u32[]{:S(2)}, u32[]{:S(2)}) %collective-permute-start.1) | collective-permute-done | bytes 327712 | tf_op jit(solution)/shard_map/ppermute | solution.py:527
  11.5 2.4 %collective-permute-start.3 = (f32[2,2,128,128]{3,2,1,0:T(8,128)S(1)}, f32[2,2,128,128]{3,2,1,0:T(8,128)S(1)}, u32[]{:S(2)}, u32[]{:S(2)}) collective-permute-start(f32[2,2,128,128]{3,2,1,0:T(8,128)S(1)} %get-tuple-element.33), channel_id=1, source_target_pairs={{0,4},{1,17},{2,6},{3,19},{4,0},{5,9},{6,2},{7,11},{8,12},{9,5},{1... | collective-permute-start | bytes 786440 | tf_op jit(solution)/shard_map/ppermute | solution.py:529
  13.9 0.0 collective-permute-start.4
  14.6 5.4 %shard_map.115 = (f32[2,2,10,128,128]{4,3,2,1,0:T(8,128)S(1)}, f32[2,4,128,128]{3,2,1,0:T(8,128)S(1)}, f32[2,4,128,128]{3,2,1,0:T(8,128)S(1)}, f32[4,256,128]{2,1,0:T(8,128)S(1)}, f32[8,128]{1,0:T(8,128)S(1)}) custom-call(s32[256]{0:T(256)} %x_hbm.1, s32[256]{0:T(256)} %y_hbm.1, s32[256]{0:T(256)} %z_hbm.1, f32[4]{0:T(128)} %kappas_hbm.1, ...), custom_call_target="tpu_custom_call" | custom-call | flops 1073741824 | bytes 4194304 | tf_op jit(solution)/shard_map/pallas_call | solution.py:532
  20.0 0.0 collective-permute-done.2.near_cells_ref
  20.0 0.0 copy-start
  20.0 1.3 %shard_map.116 = (f32[2,8,144,128]{3,2,1,0:T(8,128)S(1)}, f32[2,8,144,128]{3,2,1,0:T(8,128)S(1)}, f32[2,12,128,128]{3,2,1,0:T(8,128)S(1)}, f32[2,12,128,128]{3,2,1,0:T(8,128)S(1)}) custom-call(f32[2,4,128,128]{3,2,1,0:T(8,128)S(1)} %get-tuple-element.26.adj_ref, f32[2,4,128,128]{3,2,1,0:T(8,128)S(1)} %collective-permute-done.halo_ref, ...), custom_call_target="tpu_custom_call" | custom-call | flops 67108864 | bytes 4194304 | tf_op jit(solution)/shard_map/pallas_call | solution.py:564
  21.3 0.0 collective-permute-done.3.halo_ref
  21.3 0.9 %shard_map.117 = (f32[2,4,144,128]{3,2,1,0:T(8,128)S(1)}, f32[2,6,144,128]{3,2,1,0:T(8,128)S(1)}, f32[2,2,64,128]{3,2,1,0:T(8,128)S(1)}, f32[2,2,64,128]{3,2,1,0:T(8,128)S(1)}) custom-call(f32[2,8,144,128]{3,2,1,0:T(8,128)S(1)} %get-tuple-element.31.zero_in_ref.near_ref, f32[2,8,144,128]{3,2,1,0:T(8,128)S(1)} %get-tuple-element.32.one_in_ref, ...), custom_call_target="tpu_custom_call" | custom-call | flops 67108864 | bytes 4194304 | tf_op jit(solution)/shard_map/pallas_call | solution.py:577
  22.2 0.4 %collective-permute-start.7 = (f32[2,2,64,128]{3,2,1,0:T(8,128)S(1)}, f32[2,2,64,128]{3,2,1,0:T(8,128)S(1)}, u32[]{:S(2)}, u32[]{:S(2)}) collective-permute-start(f32[2,2,64,128]{3,2,1,0:T(8,128)S(1)} %get-tuple-element.47), channel_id=1, source_target_pairs={{0,1},{1,0},{2,3},{3,2},{4,5},{5,4},{6,7},{7,6},{8,9},{9,8},{10,11... | collective-permute-start | bytes 393224 | tf_op jit(solution)/shard_map/ppermute | solution.py:587
  22.6 0.0 collective-permute-done.4.halo_ref
  22.6 0.8 %shard_map.118 = (f32[2,4,144,128]{3,2,1,0:T(8,128)S(1)}, f32[2,6,144,128]{3,2,1,0:T(8,128)S(1)}, f32[2,2,64,128]{3,2,1,0:T(8,128)S(1)}, f32[2,2,64,128]{3,2,1,0:T(8,128)S(1)}) custom-call(f32[2,4,144,128]{3,2,1,0:T(8,128)S(1)} %get-tuple-element.37.zero_in_ref.zero_a_ref, f32[2,6,144,128]{3,2,1,0:T(8,128)S(1)} %get-tuple-element.38.one_in_ref.one_a_ref, ...), custom_call_target="tpu_custom_call" | custom-call | flops 67108864 | bytes 4194304 | tf_op jit(solution)/shard_map/pallas_call | solution.py:577
  23.4 0.2 collective-permute-start.5
  23.7 0.0 collective-permute-done.7.got_ref
  23.7 2.0 %collective-permute-start.8 = (f32[1,2,64,128]{3,2,1,0:T(8,128)S(1)}, f32[1,2,64,128]{3,2,1,0:T(8,128)S(1)}, u32[]{:S(2)}, u32[]{:S(2)}) collective-permute-start(f32[1,2,64,128]{3,2,1,0:T(8,128)S(1)} %get-tuple-element.49), channel_id=1, source_target_pairs={{0,2},{1,3},{2,0},{3,1},{4,6},{5,7},{6,4},{7,5},{8,10},{9,11},{10,... | collective-permute-start | bytes 196616 | tf_op jit(solution)/shard_map/ppermute | solution.py:607
  25.7 1.0 %collective-permute-start.6 = (f32[1,2,64,128]{3,2,1,0:T(8,128)S(1)}, f32[1,2,64,128]{3,2,1,0:T(8,128)S(1)}, u32[]{:S(2)}, u32[]{:S(2)}) collective-permute-start(f32[1,2,64,128]{3,2,1,0:T(8,128)S(1)} %get-tuple-element.45), channel_id=1, source_target_pairs={{0,2},{1,3},{2,0},{3,1},{4,6},{5,7},{6,4},{7,5},{8,10},{9,11},{10,... | collective-permute-start | bytes 196616 | tf_op jit(solution)/shard_map/ppermute | solution.py:607
  26.7 1.0 %shard_map.119 = f32[1,2,4,256,128]{4,3,2,1,0:T(8,128)} custom-call(f32[2,8,144,128]{3,2,1,0:T(8,128)S(1)} %get-tuple-element.31.zero_in_ref.near_ref, f32[2,4,144,128]{3,2,1,0:T(8,128)S(1)} %get-tuple-element.37.zero_in_ref.zero_a_ref, f32[2,6,144,128]{3,2,1,0:T(8,128)S(1)} %get-tuple-element.38.one_in_ref.one_a_ref, ...), custom_call_target="tpu_custom_call" | custom-call | flops 1048576 | bytes 4194304 | tf_op jit(solution)/shard_map/pallas_call | solution.py:591
  27.7 0.3 %collective-permute-done.8.ended_got_ref = f32[1,2,64,128]{3,2,1,0:T(8,128)S(1)} collective-permute-done((f32[1,2,64,128]{3,2,1,0:T(8,128)S(1)}, f32[1,2,64,128]{3,2,1,0:T(8,128)S(1)}, u32[]{:S(2)}, u32[]{:S(2)}) %collective-permute-start.8) | collective-permute-done | bytes 65568 | tf_op jit(solution)/shard_map/ppermute | solution.py:607
  28.1 2.0 %collective-permute-done.6.begun_got_ref = f32[1,2,64,128]{3,2,1,0:T(8,128)S(1)} collective-permute-done((f32[1,2,64,128]{3,2,1,0:T(8,128)S(1)}, f32[1,2,64,128]{3,2,1,0:T(8,128)S(1)}, u32[]{:S(2)}, u32[]{:S(2)}) %collective-permute-start.6) | collective-permute-done | bytes 65568 | tf_op jit(solution)/shard_map/ppermute | solution.py:607
  30.1 0.7 %shard_map.122 = f32[4,64,128]{2,1,0:T(8,128)} custom-call(f32[1,2,64,128]{3,2,1,0:T(8,128)S(1)} %get-tuple-element.44.begun_ref, f32[1,2,64,128]{3,2,1,0:T(8,128)S(1)} %collective-permute-done.6.begun_got_ref, f32[1,2,64,128]{3,2,1,0:T(8,128)S(1)} %get-tuple-element.48.ended_ref, f32[1,2,64,128]{3,2,1,0:T(8,128)S(1)} %collective-permute-done.8.ended_got_ref), custom_call_target="tpu_custom_call" | custom-call | flops 1048576 | bytes 4194304 | tf_op jit(solution)/shard_map/pallas_call | solution.py:616
  (6 shorter events, 0.0 us)
Async XLA Ops:
  1.7 9.8 %collective-permute-start.1 = (f32[5,128,128]{2,1,0:T(8,128)S(1)}, f32[5,128,128]{2,1,0:T(8,128)S(1)}, u32[]{:S(2)}, u32[]{:S(2)}) collective-permute-start(f32[5,128,128]{2,1,0:T(8,128)S(1)} %shard_map.114), channel_id=1, source_target_pairs={{0,4},{1,17},{2,6},{3,19},{4,0},{5,9},{6,2},{7,11},{8,12},{9,5},{1... | collective-permute-start | bytes 983048 | tf_op jit(solution)/shard_map/ppermute | solution.py:527
  6.1 13.9 %collective-permute-start = (f32[2,4,128,128]{3,2,1,0:T(8,128)S(1)}, f32[2,4,128,128]{3,2,1,0:T(8,128)S(1)}, u32[]{:S(2)}, u32[]{:S(2)}) collective-permute-start(f32[2,4,128,128]{3,2,1,0:T(8,128)S(1)} %get-tuple-element.26.adj_ref), channel_id=1, source_target_pairs={{0,2},{1,5},{2,0},{3,7},{4,8},{5,1},{6,10},{7,3},{8,4},{9,13},{10,... | collective-permute-start | bytes 1572872 | tf_op jit(solution)/shard_map/ppermute | solution.py:528
  11.5 8.5 %collective-permute-start.2 = (f32[5,128,128]{2,1,0:T(8,128)S(1)}, f32[5,128,128]{2,1,0:T(8,128)S(1)}, u32[]{:S(2)}, u32[]{:S(2)}) collective-permute-start(f32[5,128,128]{2,1,0:T(8,128)S(1)} %collective-permute-done.1.far_cells_ref), channel_id=1, source_target_pairs={{0,1},{1,0},{2,3},{3,2},{4,5},{5,4},{6,7},{7,6},{8,9},{9,8},{10,11... | collective-permute-start | bytes 983048 | tf_op jit(solution)/shard_map/ppermute | solution.py:560
  11.5 9.8 %collective-permute-start.3 = (f32[2,2,128,128]{3,2,1,0:T(8,128)S(1)}, f32[2,2,128,128]{3,2,1,0:T(8,128)S(1)}, u32[]{:S(2)}, u32[]{:S(2)}) collective-permute-start(f32[2,2,128,128]{3,2,1,0:T(8,128)S(1)} %get-tuple-element.33), channel_id=1, source_target_pairs={{0,4},{1,17},{2,6},{3,19},{4,0},{5,9},{6,2},{7,11},{8,12},{9,5},{1... | collective-permute-start | bytes 786440 | tf_op jit(solution)/shard_map/ppermute | solution.py:529
  13.9 8.7 %collective-permute-start.4 = (f32[2,2,128,128]{3,2,1,0:T(8,128)S(1)}, f32[2,2,128,128]{3,2,1,0:T(8,128)S(1)}, u32[]{:S(2)}, u32[]{:S(2)}) collective-permute-start(f32[2,2,128,128]{3,2,1,0:T(8,128)S(1)} %get-tuple-element.39), channel_id=1, source_target_pairs={{0,4},{1,17},{2,6},{3,19},{4,0},{5,9},{6,2},{7,11},{8,12},{9,5},{1... | collective-permute-start | bytes 786440 | tf_op jit(solution)/shard_map/ppermute | solution.py:530
  20.0 1.3 %copy-start = (f32[1,2,4,256,128]{4,3,2,1,0:T(8,128)S(1)}, f32[1,2,4,256,128]{4,3,2,1,0:T(8,128)}, u32[]{:S(2)}) copy-start(f32[1,2,4,256,128]{4,3,2,1,0:T(8,128)} %forward_ref.3) | copy-start | bytes 3145732
  22.2 1.5 %collective-permute-start.7 = (f32[2,2,64,128]{3,2,1,0:T(8,128)S(1)}, f32[2,2,64,128]{3,2,1,0:T(8,128)S(1)}, u32[]{:S(2)}, u32[]{:S(2)}) collective-permute-start(f32[2,2,64,128]{3,2,1,0:T(8,128)S(1)} %get-tuple-element.47), channel_id=1, source_target_pairs={{0,1},{1,0},{2,3},{3,2},{4,5},{5,4},{6,7},{7,6},{8,9},{9,8},{10,11... | collective-permute-start | bytes 393224 | tf_op jit(solution)/shard_map/ppermute | solution.py:587
  23.4 2.3 %collective-permute-start.5 = (f32[2,2,64,128]{3,2,1,0:T(8,128)S(1)}, f32[2,2,64,128]{3,2,1,0:T(8,128)S(1)}, u32[]{:S(2)}, u32[]{:S(2)}) collective-permute-start(f32[2,2,64,128]{3,2,1,0:T(8,128)S(1)} %get-tuple-element.43), channel_id=1, source_target_pairs={{0,1},{1,0},{2,3},{3,2},{4,5},{5,4},{6,7},{7,6},{8,9},{9,8},{10,11... | collective-permute-start | bytes 393224 | tf_op jit(solution)/shard_map/ppermute | solution.py:589
  23.7 4.4 %collective-permute-start.8 = (f32[1,2,64,128]{3,2,1,0:T(8,128)S(1)}, f32[1,2,64,128]{3,2,1,0:T(8,128)S(1)}, u32[]{:S(2)}, u32[]{:S(2)}) collective-permute-start(f32[1,2,64,128]{3,2,1,0:T(8,128)S(1)} %get-tuple-element.49), channel_id=1, source_target_pairs={{0,2},{1,3},{2,0},{3,1},{4,6},{5,7},{6,4},{7,5},{8,10},{9,11},{10,... | collective-permute-start | bytes 196616 | tf_op jit(solution)/shard_map/ppermute | solution.py:607
  25.7 4.3 %collective-permute-start.6 = (f32[1,2,64,128]{3,2,1,0:T(8,128)S(1)}, f32[1,2,64,128]{3,2,1,0:T(8,128)S(1)}, u32[]{:S(2)}, u32[]{:S(2)}) collective-permute-start(f32[1,2,64,128]{3,2,1,0:T(8,128)S(1)} %get-tuple-element.45), channel_id=1, source_target_pairs={{0,2},{1,3},{2,0},{3,1},{4,6},{5,7},{6,4},{7,5},{8,10},{9,11},{10,... | collective-permute-start | bytes 196616 | tf_op jit(solution)/shard_map/ppermute | solution.py:607

commit v8 on v7

--- a/solution.py
+++ b/solution.py
@@ -16,7 +16,7 @@
 )
 PAD = 8
 ROWS = 32
-UNROLL = 32
+UNROLL = 64
 SMEM = pl.BlockSpec(memory_space=pltpu.SMEM)
 VMEM = pl.BlockSpec(memory_space=pltpu.VMEM)
 HBM = pl.BlockSpec(memory_space=pltpu.HBM)
@@ -224,9 +224,9 @@
         old = self.where[1 - c]
         (here, at_here), (left, at_left), (right, at_right) = old[slot], old[slot - 1], old[slot + 1]
         rows = self.rows
-        by_matrix = part == 1
-        if by_matrix:
-            beside = self.along_z(here[part, at_here, pl.ds(PAD, self.half), :])
+        upto = 0 if part == 0 else self.half // 4
+        if upto:
+            beside = self.along_z(here[part, at_here, pl.ds(PAD, upto), :])
         out = []
         for r in range(0, self.half, rows):
             above = here[part, at_here, pl.ds(PAD + r + 1, rows), :]
@@ -236,7 +236,7 @@
             total = left[part, at_left, pl.ds(PAD + r, rows), :]
             total += right[part, at_right, pl.ds(PAD + r, rows), :]
             total += jnp.where(self.odd, above, below)
-            if by_matrix:
+            if r < upto:
                 total += beside[r : r + rows]
             else:
                 centre = here[part, at_here, pl.ds(PAD + r, rows), :]

time: 31 us -> 30.3 us (0.977)
  Pallas kernels: 12.4 us -> 11.7 us
    pallas_call x1, Pallas kernels: 5.41 us -> 4.98 us  [body(): call(source_kernel, [(2, 2, reach, half, size_z), (2, layers, half, size_...]
  transfers between devices with their start and end apart: 9 -> 9, of which waited for: 3 -> 4; matrix products, arithmetic and copies ran while one was open for 0% -> 0% of each run, Pallas kernels for 35% -> 33%
where the time goes in v8:
time: 30.3 us; the launch traced here: 30 us
  Pallas kernels  11.7 us (39%)
  starting transfers between devices  10.7 us (35%)
  waiting for transfers between devices  6.29 us (21%)
  between operations  1.38 us (5%)
    pallas_call x1, Pallas kernels, body(): call(source_kernel, [(2, 2, reach, half, size_z), (2, layers, half, size_...  4.98 us
    ppermute x1, waiting for transfers between devices, body(): far_cells = lax.ppermute(cells_out, every, to_far)  3.83 us
    ppermute x1, starting transfers between devices, body(): far_cells = lax.ppermute(cells_out, every, to_far)  3.12 us
    ppermute x2, starting transfers between devices, add_up(): got = lax.ppermute(send, 'src', [(i, i ^ bit) for i in range(shards)])  2.94 us
    ppermute x1, starting transfers between devices, body(): first_halo = lax.ppermute(adj_first, every, to_far)  2.41 us
    ppermute x2, waiting for transfers between devices, add_up(): got = lax.ppermute(send, 'src', [(i, i ^ bit) for i in range(shards)])  2.39 us
    ppermute x1, starting transfers between devices, body(): near_halo = lax.ppermute(adj, every, to_near)  1.56 us
    pallas_call x2, Pallas kernels, far(): call(kernel, [state_zero, state_one, part_shape, part_shape], [], [VMEM]...  1.47 us
  transfers between devices with their start and end apart: 9, of which 4 were waited for; matrix products, arithmetic and copies ran while one was open for 0% of the time, Pallas kernels for 33%

profile of v8, /device:TPU:0, one launch (start us, length us, event | category | flops | bytes accessed | tf_op | source)
XLA Modules:
  0.0 30.0 jit_solution(3887941712763258601)
XLA Ops:
  0.6 1.1 %shard_map.114 = f32[5,128,128]{2,1,0:T(8,128)S(1)} custom-call(f32[4,256,128]{2,1,0:T(8,128)} %cond_hbm.3), custom_call_target="tpu_custom_call" | custom-call | flops 1048576 | bytes 4194304 | tf_op jit(solution)/shard_map/pallas_call | solution.py:514
  1.7 3.1 %collective-permute-start.1 = (f32[5,128,128]{2,1,0:T(8,128)S(1)}, f32[5,128,128]{2,1,0:T(8,128)S(1)}, u32[]{:S(2)}, u32[]{:S(2)}) collective-permute-start(f32[5,128,128]{2,1,0:T(8,128)S(1)} %shard_map.114), channel_id=1, source_target_pairs={{0,4},{1,17},{2,6},{3,19},{4,0},{5,9},{6,2},{7,11},{8,12},{9,5},{1... | collective-permute-start | bytes 983048 | tf_op jit(solution)/shard_map/ppermute | solution.py:527
  4.8 1.3 %shard_map.113 = (f32[2,4,128,128]{3,2,1,0:T(8,128)S(1)}, f32[2,2,128,128]{3,2,1,0:T(8,128)S(1)}, f32[2,2,128,128]{3,2,1,0:T(8,128)S(1)}) custom-call(f32[1,2,4,256,128]{4,3,2,1,0:T(8,128)} %guess_hbm.1), custom_call_target="tpu_custom_call" | custom-call | flops 1048576 | bytes 4194304 | tf_op jit(solution)/shard_map/pallas_call | solution.py:506
  6.1 1.6 %collective-permute-start = (f32[2,4,128,128]{3,2,1,0:T(8,128)S(1)}, f32[2,4,128,128]{3,2,1,0:T(8,128)S(1)}, u32[]{:S(2)}, u32[]{:S(2)}) collective-permute-start(f32[2,4,128,128]{3,2,1,0:T(8,128)S(1)} %get-tuple-element.26.adj_ref), channel_id=1, source_target_pairs={{0,2},{1,5},{2,0},{3,7},{4,8},{5,1},{6,10},{7,3},{8,4},{9,13},{10,... | collective-permute-start | bytes 1572872 | tf_op jit(solution)/shard_map/ppermute | solution.py:528
  7.6 3.8 %collective-permute-done.1.far_cells_ref = f32[5,128,128]{2,1,0:T(8,128)S(1)} collective-permute-done((f32[5,128,128]{2,1,0:T(8,128)S(1)}, f32[5,128,128]{2,1,0:T(8,128)S(1)}, u32[]{:S(2)}, u32[]{:S(2)}) %collective-permute-start.1) | collective-permute-done | bytes 327712 | tf_op jit(solution)/shard_map/ppermute | solution.py:527
  11.5 0.0 collective-permute-start.2
  11.5 2.4 %collective-permute-start.3 = (f32[2,2,128,128]{3,2,1,0:T(8,128)S(1)}, f32[2,2,128,128]{3,2,1,0:T(8,128)S(1)}, u32[]{:S(2)}, u32[]{:S(2)}) collective-permute-start(f32[2,2,128,128]{3,2,1,0:T(8,128)S(1)} %get-tuple-element.33), channel_id=1, source_target_pairs={{0,4},{1,17},{2,6},{3,19},{4,0},{5,9},{6,2},{7,11},{8,12},{9,5},{1... | collective-permute-start | bytes 786440 | tf_op jit(solution)/shard_map/ppermute | solution.py:529
  13.9 0.0 collective-permute-start.4
  14.6 5.0 %shard_map.115 = (f32[2,2,10,128,128]{4,3,2,1,0:T(8,128)S(1)}, f32[2,4,128,128]{3,2,1,0:T(8,128)S(1)}, f32[2,4,128,128]{3,2,1,0:T(8,128)S(1)}, f32[4,256,128]{2,1,0:T(8,128)S(1)}, f32[8,128]{1,0:T(8,128)S(1)}) custom-call(s32[256]{0:T(256)} %x_hbm.1, s32[256]{0:T(256)} %y_hbm.1, s32[256]{0:T(256)} %z_hbm.1, f32[4]{0:T(128)} %kappas_hbm.1, ...), custom_call_target="tpu_custom_call" | custom-call | flops 1073741824 | bytes 4194304 | tf_op jit(solution)/shard_map/pallas_call | solution.py:532
  19.6 0.0 collective-permute-done.halo_ref
  19.6 0.0 copy-start
  19.6 1.2 %shard_map.116 = (f32[2,8,144,128]{3,2,1,0:T(8,128)S(1)}, f32[2,8,144,128]{3,2,1,0:T(8,128)S(1)}, f32[2,12,128,128]{3,2,1,0:T(8,128)S(1)}, f32[2,12,128,128]{3,2,1,0:T(8,128)S(1)}) custom-call(f32[2,4,128,128]{3,2,1,0:T(8,128)S(1)} %get-tuple-element.26.adj_ref, f32[2,4,128,128]{3,2,1,0:T(8,128)S(1)} %collective-permute-done.halo_ref, ...), custom_call_target="tpu_custom_call" | custom-call | flops 67108864 | bytes 4194304 | tf_op jit(solution)/shard_map/pallas_call | solution.py:564
  20.8 0.0 copy-done
  20.8 0.7 %shard_map.117 = (f32[2,4,144,128]{3,2,1,0:T(8,128)S(1)}, f32[2,6,144,128]{3,2,1,0:T(8,128)S(1)}, f32[2,2,64,128]{3,2,1,0:T(8,128)S(1)}, f32[2,2,64,128]{3,2,1,0:T(8,128)S(1)}) custom-call(f32[2,8,144,128]{3,2,1,0:T(8,128)S(1)} %get-tuple-element.31.zero_in_ref.near_ref, f32[2,8,144,128]{3,2,1,0:T(8,128)S(1)} %get-tuple-element.32.one_in_ref, ...), custom_call_target="tpu_custom_call" | custom-call | flops 67108864 | bytes 4194304 | tf_op jit(solution)/shard_map/pallas_call | solution.py:577
  21.6 0.4 %collective-permute-start.7 = (f32[2,2,64,128]{3,2,1,0:T(8,128)S(1)}, f32[2,2,64,128]{3,2,1,0:T(8,128)S(1)}, u32[]{:S(2)}, u32[]{:S(2)}) collective-permute-start(f32[2,2,64,128]{3,2,1,0:T(8,128)S(1)} %get-tuple-element.47), channel_id=1, source_target_pairs={{0,1},{1,0},{2,3},{3,2},{4,5},{5,4},{6,7},{7,6},{8,9},{9,8},{10,11... | collective-permute-start | bytes 393224 | tf_op jit(solution)/shard_map/ppermute | solution.py:587
  21.9 0.7 %shard_map.118 = (f32[2,4,144,128]{3,2,1,0:T(8,128)S(1)}, f32[2,6,144,128]{3,2,1,0:T(8,128)S(1)}, f32[2,2,64,128]{3,2,1,0:T(8,128)S(1)}, f32[2,2,64,128]{3,2,1,0:T(8,128)S(1)}) custom-call(f32[2,4,144,128]{3,2,1,0:T(8,128)S(1)} %get-tuple-element.37.zero_in_ref.zero_a_ref, f32[2,6,144,128]{3,2,1,0:T(8,128)S(1)} %get-tuple-element.38.one_in_ref.one_a_ref, ...), custom_call_target="tpu_custom_call" | custom-call | flops 67108864 | bytes 4194304 | tf_op jit(solution)/shard_map/pallas_call | solution.py:577
  22.7 0.2 collective-permute-start.5
  22.9 0.1 collective-permute-done.7.got_ref
  23.0 2.0 %collective-permute-start.8 = (f32[1,2,64,128]{3,2,1,0:T(8,128)S(1)}, f32[1,2,64,128]{3,2,1,0:T(8,128)S(1)}, u32[]{:S(2)}, u32[]{:S(2)}) collective-permute-start(f32[1,2,64,128]{3,2,1,0:T(8,128)S(1)} %get-tuple-element.49), channel_id=1, source_target_pairs={{0,2},{1,3},{2,0},{3,1},{4,6},{5,7},{6,4},{7,5},{8,10},{9,11},{10,... | collective-permute-start | bytes 196616 | tf_op jit(solution)/shard_map/ppermute | solution.py:607
  25.0 0.9 %collective-permute-start.6 = (f32[1,2,64,128]{3,2,1,0:T(8,128)S(1)}, f32[1,2,64,128]{3,2,1,0:T(8,128)S(1)}, u32[]{:S(2)}, u32[]{:S(2)}) collective-permute-start(f32[1,2,64,128]{3,2,1,0:T(8,128)S(1)} %get-tuple-element.45), channel_id=1, source_target_pairs={{0,2},{1,3},{2,0},{3,1},{4,6},{5,7},{6,4},{7,5},{8,10},{9,11},{10,... | collective-permute-start | bytes 196616 | tf_op jit(solution)/shard_map/ppermute | solution.py:607
  26.0 1.0 %shard_map.119 = f32[1,2,4,256,128]{4,3,2,1,0:T(8,128)} custom-call(f32[2,8,144,128]{3,2,1,0:T(8,128)S(1)} %get-tuple-element.31.zero_in_ref.near_ref, f32[2,4,144,128]{3,2,1,0:T(8,128)S(1)} %get-tuple-element.37.zero_in_ref.zero_a_ref, f32[2,6,144,128]{3,2,1,0:T(8,128)S(1)} %get-tuple-element.38.one_in_ref.one_a_ref, ...), custom_call_target="tpu_custom_call" | custom-call | flops 1048576 | bytes 4194304 | tf_op jit(solution)/shard_map/pallas_call | solution.py:591
  27.0 0.4 %collective-permute-done.8.ended_got_ref = f32[1,2,64,128]{3,2,1,0:T(8,128)S(1)} collective-permute-done((f32[1,2,64,128]{3,2,1,0:T(8,128)S(1)}, f32[1,2,64,128]{3,2,1,0:T(8,128)S(1)}, u32[]{:S(2)}, u32[]{:S(2)}) %collective-permute-start.8) | collective-permute-done | bytes 65568 | tf_op jit(solution)/shard_map/ppermute | solution.py:607
  27.4 1.9 %collective-permute-done.6.begun_got_ref = f32[1,2,64,128]{3,2,1,0:T(8,128)S(1)} collective-permute-done((f32[1,2,64,128]{3,2,1,0:T(8,128)S(1)}, f32[1,2,64,128]{3,2,1,0:T(8,128)S(1)}, u32[]{:S(2)}, u32[]{:S(2)}) %collective-permute-start.6) | collective-permute-done | bytes 65568 | tf_op jit(solution)/shard_map/ppermute | solution.py:607
  29.4 0.7 %shard_map.122 = f32[4,64,128]{2,1,0:T(8,128)} custom-call(f32[1,2,64,128]{3,2,1,0:T(8,128)S(1)} %get-tuple-element.44.begun_ref, f32[1,2,64,128]{3,2,1,0:T(8,128)S(1)} %collective-permute-done.6.begun_got_ref, f32[1,2,64,128]{3,2,1,0:T(8,128)S(1)} %get-tuple-element.48.ended_ref, f32[1,2,64,128]{3,2,1,0:T(8,128)S(1)} %collective-permute-done.8.ended_got_ref), custom_call_target="tpu_custom_call" | custom-call | flops 1048576 | bytes 4194304 | tf_op jit(solution)/shard_map/pallas_call | solution.py:616
  (6 shorter events, 0.0 us)
Async XLA Ops:
  1.7 9.8 %collective-permute-start.1 = (f32[5,128,128]{2,1,0:T(8,128)S(1)}, f32[5,128,128]{2,1,0:T(8,128)S(1)}, u32[]{:S(2)}, u32[]{:S(2)}) collective-permute-start(f32[5,128,128]{2,1,0:T(8,128)S(1)} %shard_map.114), channel_id=1, source_target_pairs={{0,4},{1,17},{2,6},{3,19},{4,0},{5,9},{6,2},{7,11},{8,12},{9,5},{1... | collective-permute-start | bytes 983048 | tf_op jit(solution)/shard_map/ppermute | solution.py:527
  6.1 13.5 %collective-permute-start = (f32[2,4,128,128]{3,2,1,0:T(8,128)S(1)}, f32[2,4,128,128]{3,2,1,0:T(8,128)S(1)}, u32[]{:S(2)}, u32[]{:S(2)}) collective-permute-start(f32[2,4,128,128]{3,2,1,0:T(8,128)S(1)} %get-tuple-element.26.adj_ref), channel_id=1, source_target_pairs={{0,2},{1,5},{2,0},{3,7},{4,8},{5,1},{6,10},{7,3},{8,4},{9,13},{10,... | collective-permute-start | bytes 1572872 | tf_op jit(solution)/shard_map/ppermute | solution.py:528
  11.5 8.1 %collective-permute-start.2 = (f32[5,128,128]{2,1,0:T(8,128)S(1)}, f32[5,128,128]{2,1,0:T(8,128)S(1)}, u32[]{:S(2)}, u32[]{:S(2)}) collective-permute-start(f32[5,128,128]{2,1,0:T(8,128)S(1)} %collective-permute-done.1.far_cells_ref), channel_id=1, source_target_pairs={{0,1},{1,0},{2,3},{3,2},{4,5},{5,4},{6,7},{7,6},{8,9},{9,8},{10,11... | collective-permute-start | bytes 983048 | tf_op jit(solution)/shard_map/ppermute | solution.py:560
  11.5 9.3 %collective-permute-start.3 = (f32[2,2,128,128]{3,2,1,0:T(8,128)S(1)}, f32[2,2,128,128]{3,2,1,0:T(8,128)S(1)}, u32[]{:S(2)}, u32[]{:S(2)}) collective-permute-start(f32[2,2,128,128]{3,2,1,0:T(8,128)S(1)} %get-tuple-element.33), channel_id=1, source_target_pairs={{0,4},{1,17},{2,6},{3,19},{4,0},{5,9},{6,2},{7,11},{8,12},{9,5},{1... | collective-permute-start | bytes 786440 | tf_op jit(solution)/shard_map/ppermute | solution.py:529
  13.9 8.1 %collective-permute-start.4 = (f32[2,2,128,128]{3,2,1,0:T(8,128)S(1)}, f32[2,2,128,128]{3,2,1,0:T(8,128)S(1)}, u32[]{:S(2)}, u32[]{:S(2)}) collective-permute-start(f32[2,2,128,128]{3,2,1,0:T(8,128)S(1)} %get-tuple-element.39), channel_id=1, source_target_pairs={{0,4},{1,17},{2,6},{3,19},{4,0},{5,9},{6,2},{7,11},{8,12},{9,5},{1... | collective-permute-start | bytes 786440 | tf_op jit(solution)/shard_map/ppermute | solution.py:530
  19.6 1.2 %copy-start = (f32[1,2,4,256,128]{4,3,2,1,0:T(8,128)S(1)}, f32[1,2,4,256,128]{4,3,2,1,0:T(8,128)}, u32[]{:S(2)}) copy-start(f32[1,2,4,256,128]{4,3,2,1,0:T(8,128)} %forward_ref.3) | copy-start | bytes 3145732
  21.6 1.4 %collective-permute-start.7 = (f32[2,2,64,128]{3,2,1,0:T(8,128)S(1)}, f32[2,2,64,128]{3,2,1,0:T(8,128)S(1)}, u32[]{:S(2)}, u32[]{:S(2)}) collective-permute-start(f32[2,2,64,128]{3,2,1,0:T(8,128)S(1)} %get-tuple-element.47), channel_id=1, source_target_pairs={{0,1},{1,0},{2,3},{3,2},{4,5},{5,4},{6,7},{7,6},{8,9},{9,8},{10,11... | collective-permute-start | bytes 393224 | tf_op jit(solution)/shard_map/ppermute | solution.py:587
  22.7 2.4 %collective-permute-start.5 = (f32[2,2,64,128]{3,2,1,0:T(8,128)S(1)}, f32[2,2,64,128]{3,2,1,0:T(8,128)S(1)}, u32[]{:S(2)}, u32[]{:S(2)}) collective-permute-start(f32[2,2,64,128]{3,2,1,0:T(8,128)S(1)} %get-tuple-element.43), channel_id=1, source_target_pairs={{0,1},{1,0},{2,3},{3,2},{4,5},{5,4},{6,7},{7,6},{8,9},{9,8},{10,11... | collective-permute-start | bytes 393224 | tf_op jit(solution)/shard_map/ppermute | solution.py:589
  23.0 4.4 %collective-permute-start.8 = (f32[1,2,64,128]{3,2,1,0:T(8,128)S(1)}, f32[1,2,64,128]{3,2,1,0:T(8,128)S(1)}, u32[]{:S(2)}, u32[]{:S(2)}) collective-permute-start(f32[1,2,64,128]{3,2,1,0:T(8,128)S(1)} %get-tuple-element.49), channel_id=1, source_target_pairs={{0,2},{1,3},{2,0},{3,1},{4,6},{5,7},{6,4},{7,5},{8,10},{9,11},{10,... | collective-permute-start | bytes 196616 | tf_op jit(solution)/shard_map/ppermute | solution.py:607
  25.0 4.3 %collective-permute-start.6 = (f32[1,2,64,128]{3,2,1,0:T(8,128)S(1)}, f32[1,2,64,128]{3,2,1,0:T(8,128)S(1)}, u32[]{:S(2)}, u32[]{:S(2)}) collective-permute-start(f32[1,2,64,128]{3,2,1,0:T(8,128)S(1)} %get-tuple-element.45), channel_id=1, source_target_pairs={{0,2},{1,3},{2,0},{3,1},{4,6},{5,7},{6,4},{7,5},{8,10},{9,11},{10,... | collective-permute-start | bytes 196616 | tf_op jit(solution)/shard_map/ppermute | solution.py:607
